TPU v7x, 32 devices: a whole 2x2x4 slice. The times are simulated.
32 devices in a mesh: fsdp: 8 (over y, x, core), tp: 4 (over z).
Axes of the slice: x: 2, y: 2, z: 4, core: 2. Of those that a mesh axis runs over, the one named last changes fastest.
Arguments:
- activations: bfloat16 [4096, 5120], P('fsdp'), may hold values from -80 to 80
- cotangent: bfloat16 [4096, 5120], P('fsdp'), may hold values from -80 to 80
- lengths: int32 [16], P('fsdp'), may hold values from 64 to 256, as said below
- grow_operator: bfloat16 [5120, 4096], P('fsdp', 'tp'), may hold values from -0.078125 to 0.078125
- proxy_weight: bfloat16 [4096, 4096], P('fsdp', 'tp'), may hold values from -0.09375 to 0.09375
Outputs:
- update: bfloat16 [5120, 4096], P('fsdp', 'tp')
Inputs may be any that keep to these rules, and one draw needn't show every extreme that they name: `lengths`: each entry is the length of one sequence; at least one is 256 and at least one is 64.
All inputs are finite; a program needn't handle non-finite values.
Results may differ from a plain program's by a relative error of at most 0.0057.
Values may be sent and summed in bfloat16 or wider, within the bound.
No kernel may reach another device: no remote copies, remote signals or barrier semaphores. Data moves between devices by JAX's collectives and lax.ppermute only.
A program may use at most 128 MiB of HBM per device.

v0:
```python
import functools

import jax
import jax.numpy as jnp
from jax import lax
from jax.experimental import pallas as pl
from jax.experimental.pallas import tpu as pltpu
from jax.sharding import PartitionSpec as P


LEN = 256
BF = jnp.bfloat16
F32 = jnp.float32


def dot(left, right, dims):
    return lax.dot_general(left, right, ((dims[:1], dims[1:]), ((), ())), preferred_element_type=F32)


def flip(value, axis, size, bit):
    return lax.ppermute(value, axis, [(i, i ^ bit) for i in range(size)])


def after(value, *others):
    return lax.optimization_barrier((value,) + others)[0]


def masks_of(bits):
    masks = [0]
    for bit in bits:
        masks = masks + [m | bit for m in masks]
    return sorted(masks, key=lambda m: (bin(m).count("1"), m))


def gather_near(shard, size, bits):
    return {0: shard, **{bit: flip(shard, "fsdp", size, bit) for bit in bits}}


def gather_far(got, size, bits, gate):
    got = {m: after(block, gate) for m, block in got.items()}
    half = got[0].shape[0] // 2
    low = high = None
    for mask in masks_of(bits)[1 + len(bits) :]:
        inside = [bit for bit in bits if mask & bit]
        first, last = inside[0], inside[-1]
        low, high = got[mask ^ last][:half], got[mask ^ first][half:]
        low, high = flip(low, "fsdp", size, last), flip(high, "fsdp", size, first)
        got[mask] = jnp.concatenate([low, high], axis=0)
    for mask in masks_of(bits):
        got[mask ^ 1] = flip(got[mask], "fsdp", size, 1)
    return got, (low, high)


def order_kernel(places, lengths, act_ref, cot_ref, out_ref):
    tokens = act_ref.shape[0]
    out_ref[:tokens, :] = act_ref[...]
    position = lax.broadcasted_iota(jnp.int32, (LEN, act_ref.shape[1]), 0)
    for i in range(tokens // LEN):
        rows = cot_ref[i * LEN : (i + 1) * LEN, :]
        kept = jnp.where(position < lengths[i], rows, jnp.zeros_like(rows))
        out_ref[tokens + i * LEN : tokens + (i + 1) * LEN, :] = kept


def ordered(places, lengths, activations, cotangent, cols):
    tokens, total = activations.shape
    if cols % 128:
        keep = (jnp.arange(LEN, dtype=jnp.int32)[None, :] < lengths[:, None]).reshape(-1)
        kept = jnp.where(keep[:, None], cotangent, jnp.zeros_like(cotangent))
        both = jnp.concatenate([activations, kept], axis=0)
        return jnp.concatenate(
            [lax.dynamic_slice_in_dim(both, p * cols, cols, axis=1) for p in places], axis=1
        )
    block = pl.BlockSpec((tokens, cols), lambda m, where, _: (0, where[m]))
    return pl.pallas_call(
        order_kernel,
        out_shape=jax.ShapeDtypeStruct((2 * tokens, total), activations.dtype),
        grid_spec=pltpu.PrefetchScalarGridSpec(
            num_scalar_prefetch=2,
            grid=(total // cols,),
            in_specs=[block, block],
            out_specs=pl.BlockSpec((2 * tokens, cols), lambda m, where, _: (0, m)),
        ),
        compiler_params=pltpu.CompilerParams(vmem_limit_bytes=24 << 20),
        cost_estimate=pl.CostEstimate(flops=0, bytes_accessed=8 * tokens * total, transcendentals=0),
    )(jnp.stack(places), lengths, activations, cotangent)


def scale_kernel(count, total_ref, *refs):
    refs, out_ref = refs[:-1], refs[-1]
    cols = refs[0].shape[1]
    scale = lax.rsqrt(total_ref[0:1, :] / count + 1e-06)
    scale = jnp.concatenate([scale] * (cols // 128), axis=1)
    for i, ref in enumerate(refs):
        out_ref[:, i * cols : (i + 1) * cols] = (ref[...] * scale).astype(out_ref.dtype)


def scaled(total, pieces, count):
    rows, cols = pieces[0].shape
    if cols % 128:
        scale = lax.rsqrt(total[0, 0] / count + 1e-06)
        return jnp.concatenate([(piece * scale).astype(BF) for piece in pieces], axis=1)
    return pl.pallas_call(
        functools.partial(scale_kernel, count),
        out_shape=jax.ShapeDtypeStruct((rows, cols * len(pieces)), BF),
        compiler_params=pltpu.CompilerParams(vmem_limit_bytes=16 << 20),
    )(total, *pieces)


def per_device(n_fsdp, n_tp, activations, cotangent, lengths, grow_operator, proxy_weight):
    me = lax.axis_index("fsdp")
    at = lax.axis_index("tp")
    bits = []
    while 2 << len(bits) < n_fsdp:
        bits.append(2 << len(bits))
    keeps = masks_of(bits)
    order = keeps + [m ^ 1 for m in keeps]
    tokens = activations.shape[0]
    rows, width = grow_operator.shape
    depth = proxy_weight.shape[0]
    split = len(keeps) * rows
    total_d, total_p = rows * n_fsdp, width * n_tp
    chunks = width // depth
    close = n_fsdp - 2
    last = n_tp - 1

    both = ordered([me ^ m for m in order], lengths, activations, cotangent, rows)

    w = gather_near(grow_operator, n_fsdp, bits)
    w, ends = gather_far(w, n_fsdp, bits, both)
    r = gather_near(after(proxy_weight, *ends), n_fsdp, bits)

    acc = dot(both, jnp.concatenate([w[m] for m in order], axis=0), (1, 0))
    forward = acc[:tokens].astype(BF)
    back = acc[tokens:].astype(BF)

    r, _ = gather_far(r, n_fsdp, bits, forward)

    r_near = jnp.concatenate([r[m] for m in range(close)], axis=0)
    r_far = jnp.concatenate([r[close], r[close + 1]], axis=0)
    product_near = dot(forward, r_near, (1, 1)).astype(BF)
    product_far = [dot(forward, r[close + i], (1, 1)).astype(BF) for i in range(2)]

    def place(c, owner):
        return me ^ (jnp.clip(owner, 0, last) * chunks + c)

    from_low, from_high = [back], [back]
    for hop in range(last):
        pairs = [(i, i + 1) for i in range(hop, last)]
        from_low.append(lax.ppermute(from_low[-1], "tp", pairs))
        pairs = [(last - i, last - 1 - i) for i in range(hop, last)]
        from_high.append(lax.ppermute(from_high[-1], "tp", pairs))
    back_all = jnp.zeros((tokens, total_p), BF)
    for hop in range(n_tp):
        owner = lax.rem(at - hop + n_tp, n_tp)
        for c in range(chunks):
            span = slice(c * depth, (c + 1) * depth)
            part = from_low[hop][:, span]
            if hop:
                part = part + from_high[n_tp - hop][:, span]
            back_all = lax.dynamic_update_slice_in_dim(back_all, part, place(c, owner) * depth, axis=1)
    delta = dot(back_all[:, : close * depth], r_near, (1, 0))
    delta = (delta + dot(back_all[:, close * depth :], r_far, (1, 0))).astype(BF)

    def partial(products, c, owner):
        block = place(c, owner)
        start = jnp.minimum(block, close - 1) * depth
        near = lax.dynamic_slice_in_dim(products[0], start, depth, axis=1)
        far = jnp.where(block == close, *products[1:])
        return jnp.where(block < close, near, far).astype(F32)

    products = (product_near, *product_far)
    sums, own = [], []
    for c in range(chunks):
        if c:
            products = lax.optimization_barrier(products + sums[-1][0])[:3]
        up = down = None
        hops = []
        for hop in range(1, n_tp):
            send_up, send_down = (partial(products, c, at + k) for k in (n_tp - hop, hop - n_tp))
            if up is not None:
                send_up, send_down = send_up + up, send_down + down
            send_up, send_down = send_up.astype(BF), send_down.astype(BF)
            send_up, send_down = lax.optimization_barrier((send_up, send_down))
            up = lax.ppermute(send_up, "tp", [(i, i + 1) for i in range(hop)])
            down = lax.ppermute(send_down, "tp", [(last - i, last - 1 - i) for i in range(hop)])
            hops.append((up, down))
        sums.append(hops)
        own.append(partial(products, c, at).astype(BF))

    squares = jnp.zeros((), F32)
    pieces = []
    for c in range(chunks):
        up, down = sums[c][-1]
        if c + 1 < chunks:
            up, down = after(up, *sums[c + 1][-2]), after(down, *sums[c + 1][-2])
        proxy_out = (own[c].astype(F32) + up.astype(F32) + down.astype(F32)).astype(BF)
        values = jnp.concatenate([delta[:, c * depth : (c + 1) * depth], proxy_out], axis=0)

        send = dot(both[:, split:], values, (0, 0)).astype(BF)
        arrived = flip(send, "fsdp", n_fsdp, 1)
        keep = after(dot(both[:, :split], values, (0, 0)), values)
        pair = (keep + arrived.astype(F32)).astype(BF)
        blocks = {m: pair[i * rows : (i + 1) * rows] for i, m in enumerate(keeps)}
        for number, sequence in enumerate((bits, bits[::-1])):
            lo = number * (depth // 2)
            held = {m: blocks[m][:, lo : lo + depth // 2].astype(F32) for m in keeps}
            for bit in sequence:
                leaving = [m for m in held if m & bit]
                packed = jnp.stack([held[m].astype(BF) for m in leaving])
                packed = flip(packed, "fsdp", n_fsdp, bit)
                for i, m in enumerate(leaving):
                    held[m ^ bit] = held[m ^ bit] + packed[i].astype(F32)
                    del held[m]
            pieces.append(held[0])
            squares = squares + jnp.sum(held[0] * held[0])

    total = jnp.broadcast_to(squares, (8, 128))
    total = total + flip(total, "fsdp", n_fsdp, 1)
    total = total + sum(flip(total, "fsdp", n_fsdp, m) for m in keeps[1:])
    total = total + sum(
        lax.ppermute(total, "tp", [(i, (i + k) % n_tp) for i in range(n_tp)]) for k in range(1, n_tp)
    )
    return scaled(total, pieces, total_d * total_p)


def solution(mesh):
    n_fsdp, n_tp = mesh.shape["fsdp"], mesh.shape["tp"]
    placed = (P("fsdp", None), P("fsdp", None), P("fsdp"), P("fsdp", "tp"), P("fsdp", "tp"))

    def body(*args):
        return per_device(n_fsdp, n_tp, *args)

    return jax.shard_map(
        body, mesh=mesh, in_specs=placed, out_specs=P("fsdp", "tp"), check_vma=False
    )
```

profile of v0, /device:TPU:0, one launch (start us, length us, event | category | flops | bytes accessed | tf_op | source)
XLA Modules:
  0.0 327.7 jit_solution(8665159692000029493)
XLA Ops:
  0.0 3.0 collective-permute-start
  3.0 1.5 collective-permute-start.1
  4.6 2.5 copy-done.1
  7.1 2.5 copy-done.2
  10.2 4.0 %shard_map.55 = bf16[1024,5120]{1,0:T(8,128)(2,1)S(1)} custom-call(s32[8]{0:T(128)S(1)} %stack.83.places, s32[2]{0:T(128)S(1)} %copy-done.3, bf16[512,5120]{1,0:T(8,128)(2,1)S(1)} %copy-done.1, bf16[512,5120]{1,0:T(8,128)(2,1)S(1)} %copy-done.2), custom_call_target="tpu_custom_call" | custom-call | bytes 20971520 | tf_op jit(solution)/shard_map/pallas_call | solution.py:74
  14.2 17.7 %collective-permute-done = bf16[640,1024]{1,0:T(8,128)(2,1)S(1)} collective-permute-done((bf16[640,1024]{1,0:T(8,128)(2,1)}, bf16[640,1024]{1,0:T(8,128)(2,1)S(1)}, u32[]{:S(2)}, u32[]{:S(2)}) %collective-permute-start) | collective-permute-done | bytes 1310752 | tf_op jit(solution)/shard_map/ppermute | solution.py:21
  32.0 1.8 collective-permute-start.2
  33.9 1.6 collective-permute-start.3
  36.0 12.0 %collective-permute-done.2 = bf16[320,1024]{1,0:T(8,128)(2,1)S(1)} collective-permute-done((bf16[320,1024]{1,0:T(8,128)(2,1)S(1)}, bf16[320,1024]{1,0:T(8,128)(2,1)S(1)}, u32[]{:S(2)}, u32[]{:S(2)}) %collective-permute-start.2) | collective-permute-done | bytes 655392 | tf_op jit(solution)/shard_map/ppermute | solution.py:21
  49.8 1.6 collective-permute-start.15
  52.6 11.2 %convolution_convert_fusion.1 = bf16[1024,1024]{1,0:T(8,128)(2,1)S(1)} fusion(bf16[1024,5120]{1,0:T(8,128)(2,1)S(1)} %shard_map.55, bf16[5120,1024]{1,0:T(8,128)(2,1)S(1)} %constant_dynamic-update-slice_fusion), kind=kOutput, calls=%fused_computation.22 | convolution fusion | flops 10738466816 | bytes 23068672 | tf_op jit(solution)/shard_map/dot_general | solution.py:17
  65.0 10.7 %collective-permute-done.15 = bf16[512,1024]{1,0:T(8,128)(2,1)} collective-permute-done((bf16[512,1024]{1,0:T(8,128)(2,1)}, bf16[512,1024]{1,0:T(8,128)(2,1)}, u32[]{:S(2)}, u32[]{:S(2)}) %collective-permute-start.15) | collective-permute-done | bytes 1048608 | tf_op jit(solution)/shard_map/ppermute | solution.py:21
  75.7 1.9 slice.201
  78.7 1.9 slice.202
  83.0 8.3 %collective-permute-done.19 = bf16[256,1024]{1,0:T(8,128)(2,1)} collective-permute-done((bf16[256,1024]{1,0:T(8,128)(2,1)}, bf16[256,1024]{1,0:T(8,128)(2,1)}, u32[]{:S(2)}, u32[]{:S(2)}) %collective-permute-start.19) | collective-permute-done | bytes 524320 | tf_op jit(solution)/shard_map/ppermute | solution.py:21
  92.4 2.8 collective-permute-done.20
  101.7 3.7 %convolution_convert_fusion = bf16[512,3072]{1,0:T(8,128)(2,1)S(1)} fusion(bf16[3072,1024]{1,0:T(8,128)(2,1)S(1)} %constant_dynamic-update-slice_fusion.9, bf16[1024,1024]{1,0:T(8,128)(2,1)S(1)} %convolution_convert_fusion.1), kind=kOutput, calls=%fused_computation.12 | convolution fusion | flops 3222798336 | bytes 10485760 | tf_op jit(solution)/shard_map/dot_general | solution.py:17
  106.2 1.9 select_select_fusion.2
  108.1 1.5 collective-permute-start.23
  109.6 4.3 %collective-permute-start.22 = (bf16[512,512]{1,0:T(8,128)(2,1)}, bf16[512,512]{1,0:T(8,128)(2,1)}, u32[]{:S(2)}, u32[]{:S(2)}) collective-permute-start(bf16[512,512]{1,0:T(8,128)(2,1)} %get-tuple-element.38), channel_id=1, source_target_pairs={{0,1},{4,5},{8,9},{12,13},{16,17},{20,21},{24,25},{28,29}} | collective-permute-start | bytes 1572872 | tf_op jit(solution)/shard_map/ppermute | solution.py:184
  115.1 5.6 %collective-permute-start.8 = (bf16[512,1024]{1,0:T(8,128)(2,1)}, bf16[512,1024]{1,0:T(8,128)(2,1)}, u32[]{:S(2)}, u32[]{:S(2)}) collective-permute-start(bf16[512,1024]{1,0:T(8,128)(2,1)} %fusion.43), channel_id=1, source_target_pairs={{0,1},{1,2},{2,3},{4,5},{5,6},{6,7},{8,9},{9,10},{10,11},{12,13},{... | collective-permute-start | bytes 3145736 | tf_op jit(solution)/shard_map/ppermute | solution.py:149
  120.7 5.0 %collective-permute-done.22 = bf16[512,512]{1,0:T(8,128)(2,1)} collective-permute-done((bf16[512,512]{1,0:T(8,128)(2,1)}, bf16[512,512]{1,0:T(8,128)(2,1)}, u32[]{:S(2)}, u32[]{:S(2)}) %collective-permute-start.22) | collective-permute-done | bytes 524320 | tf_op jit(solution)/shard_map/ppermute | solution.py:184
  125.7 3.0 add_convert_fusion.11
  128.6 1.5 collective-permute-start.25
  130.1 5.2 %collective-permute-start.24 = (bf16[512,512]{1,0:T(8,128)(2,1)}, bf16[512,512]{1,0:T(8,128)(2,1)}, u32[]{:S(2)}, u32[]{:S(2)}) collective-permute-start(bf16[512,512]{1,0:T(8,128)(2,1)} %get-tuple-element.40), channel_id=1, source_target_pairs={{0,1},{1,2},{4,5},{5,6},{8,9},{9,10},{12,13},{13,14},{16,17},{17,1... | collective-permute-start | bytes 1572872 | tf_op jit(solution)/shard_map/ppermute | solution.py:184
  135.3 6.0 %collective-permute-done.9 = bf16[512,1024]{1,0:T(8,128)(2,1)} collective-permute-done((bf16[512,1024]{1,0:T(8,128)(2,1)}, bf16[512,1024]{1,0:T(8,128)(2,1)}, u32[]{:S(2)}, u32[]{:S(2)}) %collective-permute-start.9) | collective-permute-done | bytes 1048608 | tf_op jit(solution)/shard_map/ppermute | solution.py:151
  142.6 5.5 %collective-permute-done.8 = bf16[512,1024]{1,0:T(8,128)(2,1)} collective-permute-done((bf16[512,1024]{1,0:T(8,128)(2,1)}, bf16[512,1024]{1,0:T(8,128)(2,1)}, u32[]{:S(2)}, u32[]{:S(2)}) %collective-permute-start.8) | collective-permute-done | bytes 1048608 | tf_op jit(solution)/shard_map/ppermute | solution.py:149
  148.1 1.7 collective-permute-start.12
  149.8 2.5 select_select_fusion
  152.3 1.5 collective-permute-start.28
  153.8 8.9 %collective-permute-start.27 = (bf16[512,512]{1,0:T(8,128)(2,1)}, bf16[512,512]{1,0:T(8,128)(2,1)}, u32[]{:S(2)}, u32[]{:S(2)}) collective-permute-start(bf16[512,512]{1,0:T(8,128)(2,1)} %get-tuple-element.46), channel_id=1, source_target_pairs={{0,1},{4,5},{8,9},{12,13},{16,17},{20,21},{24,25},{28,29}} | collective-permute-start | bytes 1572872 | tf_op jit(solution)/shard_map/ppermute | solution.py:184
  162.7 2.9 add_convert_fusion.9
  166.9 5.4 %collective-permute-done.27 = bf16[512,512]{1,0:T(8,128)(2,1)} collective-permute-done((bf16[512,512]{1,0:T(8,128)(2,1)}, bf16[512,512]{1,0:T(8,128)(2,1)}, u32[]{:S(2)}, u32[]{:S(2)}) %collective-permute-start.27) | collective-permute-done | bytes 524320 | tf_op jit(solution)/shard_map/ppermute | solution.py:184
  172.3 3.0 add_convert_fusion.7
  175.3 5.2 %collective-permute-start.29 = (bf16[512,512]{1,0:T(8,128)(2,1)}, bf16[512,512]{1,0:T(8,128)(2,1)}, u32[]{:S(2)}, u32[]{:S(2)}) collective-permute-start(bf16[512,512]{1,0:T(8,128)(2,1)} %get-tuple-element.48), channel_id=1, source_target_pairs={{0,1},{1,2},{4,5},{5,6},{8,9},{9,10},{12,13},{13,14},{16,17},{17,1... | collective-permute-start | bytes 1572872 | tf_op jit(solution)/shard_map/ppermute | solution.py:184
  180.5 1.5 collective-permute-start.30
  182.0 2.1 collective-permute-start.26
  184.1 1.5 collective-permute-start.11
  187.0 5.3 %collective-permute-done.29 = bf16[512,512]{1,0:T(8,128)(2,1)} collective-permute-done((bf16[512,512]{1,0:T(8,128)(2,1)}, bf16[512,512]{1,0:T(8,128)(2,1)}, u32[]{:S(2)}, u32[]{:S(2)}) %collective-permute-start.29) | collective-permute-done | bytes 524320 | tf_op jit(solution)/shard_map/ppermute | solution.py:184
  192.3 8.3 %collective-permute-done.26 = bf16[512,512]{1,0:T(8,128)(2,1)} collective-permute-done((bf16[512,512]{1,0:T(8,128)(2,1)}, bf16[512,512]{1,0:T(8,128)(2,1)}, u32[]{:S(2)}, u32[]{:S(2)}) %collective-permute-start.26) | collective-permute-done | bytes 524320 | tf_op jit(solution)/shard_map/ppermute | solution.py:184
  200.6 1.8 add_convert_fusion.4
  203.6 5.8 %collective-permute-start.37 = (bf16[512,512]{1,0:T(8,128)(2,1)S(1)}, bf16[512,512]{1,0:T(8,128)(2,1)}, u32[]{:S(2)}, u32[]{:S(2)}) collective-permute-start(bf16[512,512]{1,0:T(8,128)(2,1)S(1)} %get-tuple-element.54), channel_id=1, source_target_pairs={{0,1},{1,2},{2,3},{4,5},{5,6},{6,7},{8,9},{9,10},{10,11},{12,13},{... | collective-permute-start | bytes 1572872 | tf_op jit(solution)/shard_map/ppermute | solution.py:184
  209.5 1.7 add_convert_fusion.6
  215.0 1.4 fusion.32
  216.4 1.4 fusion.31
  219.0 1.4 fusion.29
  220.4 2.6 fusion.16
  223.1 3.4 %add_convert_fusion.2 = bf16[512,1024]{1,0:T(8,128)(2,1)S(1)} fusion(f32[512,1024]{1,0:T(8,128)S(1)} %fusion.16, bf16[3072,1024]{1,0:T(8,128)(2,1)S(1)} %bitcast.103, bf16[512,4096]{1,0:T(8,128)(2,1)S(1)} %fusion.29), kind=kOutput, calls=%fused_computation.21 | convolution fusion | flops 3222274048 | bytes 12582912 | tf_op jit(solution)/shard_map/dot_general | solution.py:17
  227.4 4.3 %fusion.8 = bf16[2560,512]{1,0:T(8,128)(2,1)} fusion(bf16[1024,5120]{1,0:T(8,128)(2,1)S(1)} %bitcast.99, bf16[512,512]{1,0:T(8,128)(2,1)S(1)} %add_convert_fusion.6, bf16[512,512]{1,0:T(8,128)(2,1)S(1)} %get-tuple-element.90), kind=kOutput, calls=%fused_computation.10 | convolution fusion | flops 2687762432 | bytes 8912896 | tf_op jit(solution)/shard_map/dot_general | solution.py:17
  231.7 1.7 add_convert_fusion.3
  233.5 5.7 %fusion.11 = bf16[2560,512]{1,0:T(8,128)(2,1)S(1)} fusion(bf16[1024,5120]{1,0:T(8,128)(2,1)} %copy-done, bf16[512,512]{1,0:T(8,128)(2,1)S(1)} %add_convert_fusion.3, bf16[512,512]{1,0:T(8,128)(2,1)} %get-tuple-element.89), kind=kOutput, calls=%fused_computation.11 | convolution fusion | flops 2687762432 | bytes 8912896 | tf_op jit(solution)/shard_map/dot_general | solution.py:17
  239.7 2.9 fusion.6
  242.7 3.0 fusion.4
  245.7 2.9 add_convert_fusion.1
  254.3 12.0 %collective-permute-done.35 = bf16[2,640,256]{2,1,0:T(8,128)(2,1)S(1)} collective-permute-done((bf16[2,640,256]{2,1,0:T(8,128)(2,1)S(1)}, bf16[2,640,256]{2,1,0:T(8,128)(2,1)S(1)}, u32[]{:S(2)}, u32[]{:S(2)}) %collective-permute-start.35) | collective-permute-done | bytes 655392 | tf_op jit(solution)/shard_map/ppermute | solution.py:21
  267.4 12.0 %collective-permute-done.42 = bf16[2,640,256]{2,1,0:T(8,128)(2,1)S(1)} collective-permute-done((bf16[2,640,256]{2,1,0:T(8,128)(2,1)S(1)}, bf16[2,640,256]{2,1,0:T(8,128)(2,1)S(1)}, u32[]{:S(2)}, u32[]{:S(2)}) %collective-permute-start.42) | collective-permute-done | bytes 655392 | tf_op jit(solution)/shard_map/ppermute | solution.py:21
  280.6 10.3 %collective-permute-done.36 = bf16[1,640,256]{2,1,0:T(8,128)(2,1)S(1)} collective-permute-done((bf16[1,640,256]{2,1,0:T(8,128)(2,1)S(1)}, bf16[1,640,256]{2,1,0:T(8,128)(2,1)S(1)}, u32[]{:S(2)}, u32[]{:S(2)}) %collective-permute-start.36) | collective-permute-done | bytes 327712 | tf_op jit(solution)/shard_map/ppermute | solution.py:21
  292.7 3.7 %collective-permute-done.43 = bf16[1,640,256]{2,1,0:T(8,128)(2,1)S(1)} collective-permute-done((bf16[1,640,256]{2,1,0:T(8,128)(2,1)S(1)}, bf16[1,640,256]{2,1,0:T(8,128)(2,1)S(1)}, u32[]{:S(2)}, u32[]{:S(2)}) %collective-permute-start.43) | collective-permute-done | bytes 327712 | tf_op jit(solution)/shard_map/ppermute | solution.py:21
  296.4 1.6 multiply_reduce_fusion
  300.9 5.6 %collective-permute-done.41 = bf16[1,640,256]{2,1,0:T(8,128)(2,1)} collective-permute-done((bf16[1,640,256]{2,1,0:T(8,128)(2,1)}, bf16[1,640,256]{2,1,0:T(8,128)(2,1)}, u32[]{:S(2)}, u32[]{:S(2)}) %collective-permute-start.41) | collective-permute-done | bytes 327712 | tf_op jit(solution)/shard_map/ppermute | solution.py:21
  306.5 1.8 multiply_reduce_fusion.1
  310.9 1.9 collective-permute-start.47
  316.9 4.1 %collective-permute-start.50 = (f32[8,128]{1,0:T(8,128)S(1)}, f32[8,128]{1,0:T(8,128)S(1)}, u32[]{:S(2)}, u32[]{:S(2)}) collective-permute-start(f32[8,128]{1,0:T(8,128)S(1)} %add_add_fusion.1), channel_id=1, source_target_pairs={{0,3},{1,0},{2,1},{3,2},{4,7},{5,4},{6,5},{7,6},{8,11},{9,8},{10,9... | collective-permute-start | bytes 12296 | tf_op jit(solution)/shard_map/ppermute | solution.py:221
  322.4 4.1 %collective-permute-done.48 = f32[8,128]{1,0:T(8,128)S(1)} collective-permute-done((f32[8,128]{1,0:T(8,128)S(1)}, f32[8,128]{1,0:T(8,128)S(1)}, u32[]{:S(2)}, u32[]{:S(2)}) %collective-permute-start.48) | collective-permute-done | bytes 4128 | tf_op jit(solution)/shard_map/ppermute | solution.py:221
  (156 shorter events, 49.7 us)
Async XLA Ops:
  0.0 32.0 %collective-permute-start = (bf16[640,1024]{1,0:T(8,128)(2,1)}, bf16[640,1024]{1,0:T(8,128)(2,1)S(1)}, u32[]{:S(2)}, u32[]{:S(2)}) collective-permute-start(bf16[640,1024]{1,0:T(8,128)(2,1)} %param.8), channel_id=1, source_target_pairs={{0,8},{4,12},{8,0},{12,4},{16,24},{20,28},{24,16},{28,20},{1,9},{5... | collective-permute-start | bytes 3932168 | tf_op jit(solution)/shard_map/ppermute | solution.py:21
  3.0 30.9 %collective-permute-start.1 = (bf16[640,1024]{1,0:T(8,128)(2,1)}, bf16[640,1024]{1,0:T(8,128)(2,1)S(1)}, u32[]{:S(2)}, u32[]{:S(2)}) collective-permute-start(bf16[640,1024]{1,0:T(8,128)(2,1)} %param.8), channel_id=1, source_target_pairs={{0,16},{4,20},{8,24},{12,28},{16,0},{20,4},{24,8},{28,12},{1,17},{... | collective-permute-start | bytes 3932168 | tf_op jit(solution)/shard_map/ppermute | solution.py:21
  10.2 25.2 %copy-start.7 = (bf16[640,1024]{1,0:T(8,128)(2,1)S(1)}, bf16[640,1024]{1,0:T(8,128)(2,1)}, u32[]{:S(2)}) copy-start(bf16[640,1024]{1,0:T(8,128)(2,1)} %param.8) | copy-start | bytes 3932164
  14.2 38.4 %copy-start = (bf16[1024,5120]{1,0:T(8,128)(2,1)}, bf16[1024,5120]{1,0:T(8,128)(2,1)S(1)}, u32[]{:S(2)}) copy-start(bf16[1024,5120]{1,0:T(8,128)(2,1)S(1)} %shard_map.55) | copy-start | bytes 31457284
  32.0 16.0 %collective-permute-start.2 = (bf16[320,1024]{1,0:T(8,128)(2,1)S(1)}, bf16[320,1024]{1,0:T(8,128)(2,1)S(1)}, u32[]{:S(2)}, u32[]{:S(2)}) collective-permute-start(bf16[320,1024]{1,0:T(8,128)(2,1)S(1)} %slice.181), channel_id=1, source_target_pairs={{0,16},{4,20},{8,24},{12,28},{16,0},{20,4},{24,8},{28,12},{1,17},{... | collective-permute-start | bytes 1966088 | tf_op jit(solution)/shard_map/ppermute | solution.py:21
  33.9 15.4 %collective-permute-start.3 = (bf16[320,1024]{1,0:T(8,128)(2,1)S(1)}, bf16[320,1024]{1,0:T(8,128)(2,1)S(1)}, u32[]{:S(2)}, u32[]{:S(2)}) collective-permute-start(bf16[320,1024]{1,0:T(8,128)(2,1)S(1)} %slice.182), channel_id=1, source_target_pairs={{0,8},{4,12},{8,0},{12,4},{16,24},{20,28},{24,16},{28,20},{1,9},{5... | collective-permute-start | bytes 1966088 | tf_op jit(solution)/shard_map/ppermute | solution.py:21
  35.4 16.0 %collective-permute-start.4 = (bf16[640,1024]{1,0:T(8,128)(2,1)S(1)}, bf16[640,1024]{1,0:T(8,128)(2,1)S(1)}, u32[]{:S(2)}, u32[]{:S(2)}) collective-permute-start(bf16[640,1024]{1,0:T(8,128)(2,1)S(1)} %copy-done.7), channel_id=1, source_target_pairs={{0,4},{4,0},{8,12},{12,8},{16,20},{20,16},{24,28},{28,24},{1,5},{5... | collective-permute-start | bytes 3932168 | tf_op jit(solution)/shard_map/ppermute | solution.py:21
  35.4 16.7 %collective-permute-start.5 = (bf16[640,1024]{1,0:T(8,128)(2,1)S(1)}, bf16[640,1024]{1,0:T(8,128)(2,1)S(1)}, u32[]{:S(2)}, u32[]{:S(2)}) collective-permute-start(bf16[640,1024]{1,0:T(8,128)(2,1)S(1)} %collective-permute-done), channel_id=1, source_target_pairs={{0,4},{4,0},{8,12},{12,8},{16,20},{20,16},{24,28},{28,24},{1,5},{5... | collective-permute-start | bytes 3932168 | tf_op jit(solution)/shard_map/ppermute | solution.py:21
  36.0 16.3 %collective-permute-start.6 = (bf16[640,1024]{1,0:T(8,128)(2,1)S(1)}, bf16[640,1024]{1,0:T(8,128)(2,1)S(1)}, u32[]{:S(2)}, u32[]{:S(2)}) collective-permute-start(bf16[640,1024]{1,0:T(8,128)(2,1)S(1)} %collective-permute-done.1), channel_id=1, source_target_pairs={{0,4},{4,0},{8,12},{12,8},{16,20},{20,16},{24,28},{28,24},{1,5},{5... | collective-permute-start | bytes 3932168 | tf_op jit(solution)/shard_map/ppermute | solution.py:21
  49.4 3.1 collective-permute-start.7
  49.8 25.9 %collective-permute-start.15 = (bf16[512,1024]{1,0:T(8,128)(2,1)}, bf16[512,1024]{1,0:T(8,128)(2,1)}, u32[]{:S(2)}, u32[]{:S(2)}) collective-permute-start(bf16[512,1024]{1,0:T(8,128)(2,1)} %param.9), channel_id=1, source_target_pairs={{0,8},{4,12},{8,0},{12,4},{16,24},{20,28},{24,16},{28,20},{1,9},{5... | collective-permute-start | bytes 3145736 | tf_op jit(solution)/shard_map/ppermute | solution.py:21
  51.4 27.2 %collective-permute-start.17 = (bf16[512,1024]{1,0:T(8,128)(2,1)}, bf16[512,1024]{1,0:T(8,128)(2,1)}, u32[]{:S(2)}, u32[]{:S(2)}) collective-permute-start(bf16[512,1024]{1,0:T(8,128)(2,1)} %param.9), channel_id=1, source_target_pairs={{0,16},{4,20},{8,24},{12,28},{16,0},{20,4},{24,8},{28,12},{1,17},{... | collective-permute-start | bytes 3145736 | tf_op jit(solution)/shard_map/ppermute | solution.py:21
  64.9 31.5 %collective-permute-start.14 = (bf16[512,1024]{1,0:T(8,128)(2,1)}, bf16[512,1024]{1,0:T(8,128)(2,1)S(1)}, u32[]{:S(2)}, u32[]{:S(2)}) collective-permute-start(bf16[512,1024]{1,0:T(8,128)(2,1)} %param.9), channel_id=1, source_target_pairs={{0,4},{4,0},{8,12},{12,8},{16,20},{20,16},{24,28},{28,24},{1,5},{5... | collective-permute-start | bytes 3145736 | tf_op jit(solution)/shard_map/ppermute | solution.py:21
  77.6 13.8 %collective-permute-start.19 = (bf16[256,1024]{1,0:T(8,128)(2,1)}, bf16[256,1024]{1,0:T(8,128)(2,1)}, u32[]{:S(2)}, u32[]{:S(2)}) collective-permute-start(bf16[256,1024]{1,0:T(8,128)(2,1)} %slice.201), channel_id=1, source_target_pairs={{0,16},{4,20},{8,24},{12,28},{16,0},{20,4},{24,8},{28,12},{1,17},{... | collective-permute-start | bytes 1572872 | tf_op jit(solution)/shard_map/ppermute | solution.py:21
  78.7 19.1 %collective-permute-start.16 = (bf16[512,1024]{1,0:T(8,128)(2,1)}, bf16[512,1024]{1,0:T(8,128)(2,1)}, u32[]{:S(2)}, u32[]{:S(2)}) collective-permute-start(bf16[512,1024]{1,0:T(8,128)(2,1)} %collective-permute-done.15), channel_id=1, source_target_pairs={{0,4},{4,0},{8,12},{12,8},{16,20},{20,16},{24,28},{28,24},{1,5},{5... | collective-permute-start | bytes 3145736 | tf_op jit(solution)/shard_map/ppermute | solution.py:21
  80.6 14.7 %collective-permute-start.20 = (bf16[256,1024]{1,0:T(8,128)(2,1)}, bf16[256,1024]{1,0:T(8,128)(2,1)}, u32[]{:S(2)}, u32[]{:S(2)}) collective-permute-start(bf16[256,1024]{1,0:T(8,128)(2,1)} %slice.202), channel_id=1, source_target_pairs={{0,8},{4,12},{8,0},{12,4},{16,24},{20,28},{24,16},{28,20},{1,9},{5... | collective-permute-start | bytes 1572872 | tf_op jit(solution)/shard_map/ppermute | solution.py:21
  81.5 18.9 %collective-permute-start.18 = (bf16[512,1024]{1,0:T(8,128)(2,1)}, bf16[512,1024]{1,0:T(8,128)(2,1)}, u32[]{:S(2)}, u32[]{:S(2)}) collective-permute-start(bf16[512,1024]{1,0:T(8,128)(2,1)} %collective-permute-done.17), channel_id=1, source_target_pairs={{0,4},{4,0},{8,12},{12,8},{16,20},{20,16},{24,28},{28,24},{1,5},{5... | collective-permute-start | bytes 3145736 | tf_op jit(solution)/shard_map/ppermute | solution.py:21
  96.3 9.1 %collective-permute-start.21 = (bf16[512,1024]{1,0:T(8,128)(2,1)S(1)}, bf16[512,1024]{1,0:T(8,128)(2,1)S(1)}, u32[]{:S(2)}, u32[]{:S(2)}) collective-permute-start(bf16[512,1024]{1,0:T(8,128)(2,1)S(1)} %constant_dynamic-update-slice_fusion.15), channel_id=1, source_target_pairs={{0,4},{4,0},{8,12},{12,8},{16,20},{20,16},{24,28},{28,24},{1,5},{5... | collective-permute-start | bytes 3145736 | tf_op jit(solution)/shard_map/ppermute | solution.py:21
  108.1 12.6 %collective-permute-start.23 = (bf16[512,512]{1,0:T(8,128)(2,1)}, bf16[512,512]{1,0:T(8,128)(2,1)}, u32[]{:S(2)}, u32[]{:S(2)}) collective-permute-start(bf16[512,512]{1,0:T(8,128)(2,1)} %get-tuple-element.39), channel_id=1, source_target_pairs={{3,2},{7,6},{11,10},{15,14},{19,18},{23,22},{27,26},{31,30}} | collective-permute-start | bytes 1572872 | tf_op jit(solution)/shard_map/ppermute | solution.py:185
  109.6 16.1 %collective-permute-start.22 = (bf16[512,512]{1,0:T(8,128)(2,1)}, bf16[512,512]{1,0:T(8,128)(2,1)}, u32[]{:S(2)}, u32[]{:S(2)}) collective-permute-start(bf16[512,512]{1,0:T(8,128)(2,1)} %get-tuple-element.38), channel_id=1, source_target_pairs={{0,1},{4,5},{8,9},{12,13},{16,17},{20,21},{24,25},{28,29}} | collective-permute-start | bytes 1572872 | tf_op jit(solution)/shard_map/ppermute | solution.py:184
  113.8 27.5 %collective-permute-start.9 = (bf16[512,1024]{1,0:T(8,128)(2,1)}, bf16[512,1024]{1,0:T(8,128)(2,1)}, u32[]{:S(2)}, u32[]{:S(2)}) collective-permute-start(bf16[512,1024]{1,0:T(8,128)(2,1)} %fusion.43), channel_id=1, source_target_pairs={{3,2},{2,1},{1,0},{7,6},{6,5},{5,4},{11,10},{10,9},{9,8},{15,14},{... | collective-permute-start | bytes 3145736 | tf_op jit(solution)/shard_map/ppermute | solution.py:151
  115.1 33.0 %collective-permute-start.8 = (bf16[512,1024]{1,0:T(8,128)(2,1)}, bf16[512,1024]{1,0:T(8,128)(2,1)}, u32[]{:S(2)}, u32[]{:S(2)}) collective-permute-start(bf16[512,1024]{1,0:T(8,128)(2,1)} %fusion.43), channel_id=1, source_target_pairs={{0,1},{1,2},{2,3},{4,5},{5,6},{6,7},{8,9},{9,10},{10,11},{12,13},{... | collective-permute-start | bytes 3145736 | tf_op jit(solution)/shard_map/ppermute | solution.py:149
  128.6 25.2 %collective-permute-start.25 = (bf16[512,512]{1,0:T(8,128)(2,1)}, bf16[512,512]{1,0:T(8,128)(2,1)}, u32[]{:S(2)}, u32[]{:S(2)}) collective-permute-start(bf16[512,512]{1,0:T(8,128)(2,1)} %get-tuple-element.41), channel_id=1, source_target_pairs={{3,2},{2,1},{7,6},{6,5},{11,10},{10,9},{15,14},{14,13},{19,18},{18... | collective-permute-start | bytes 1572872 | tf_op jit(solution)/shard_map/ppermute | solution.py:185
  130.1 32.6 %collective-permute-start.24 = (bf16[512,512]{1,0:T(8,128)(2,1)}, bf16[512,512]{1,0:T(8,128)(2,1)}, u32[]{:S(2)}, u32[]{:S(2)}) collective-permute-start(bf16[512,512]{1,0:T(8,128)(2,1)} %get-tuple-element.40), channel_id=1, source_target_pairs={{0,1},{1,2},{4,5},{5,6},{8,9},{9,10},{12,13},{13,14},{16,17},{17,1... | collective-permute-start | bytes 1572872 | tf_op jit(solution)/shard_map/ppermute | solution.py:184
  141.3 40.7 %collective-permute-start.10 = (bf16[512,1024]{1,0:T(8,128)(2,1)}, bf16[512,1024]{1,0:T(8,128)(2,1)}, u32[]{:S(2)}, u32[]{:S(2)}) collective-permute-start(bf16[512,1024]{1,0:T(8,128)(2,1)} %collective-permute-done.9), channel_id=1, source_target_pairs={{2,1},{1,0},{6,5},{5,4},{10,9},{9,8},{14,13},{13,12},{18,17},{17,1... | collective-permute-start | bytes 3145736 | tf_op jit(solution)/shard_map/ppermute | solution.py:151
  148.1 35.9 %collective-permute-start.12 = (bf16[512,1024]{1,0:T(8,128)(2,1)}, bf16[512,1024]{1,0:T(8,128)(2,1)}, u32[]{:S(2)}, u32[]{:S(2)}) collective-permute-start(bf16[512,1024]{1,0:T(8,128)(2,1)} %collective-permute-done.8), channel_id=1, source_target_pairs={{1,2},{2,3},{5,6},{6,7},{9,10},{10,11},{13,14},{14,15},{17,18},{18... | collective-permute-start | bytes 3145736 | tf_op jit(solution)/shard_map/ppermute | solution.py:149
  152.3 14.6 %collective-permute-start.28 = (bf16[512,512]{1,0:T(8,128)(2,1)}, bf16[512,512]{1,0:T(8,128)(2,1)}, u32[]{:S(2)}, u32[]{:S(2)}) collective-permute-start(bf16[512,512]{1,0:T(8,128)(2,1)} %get-tuple-element.47), channel_id=1, source_target_pairs={{3,2},{7,6},{11,10},{15,14},{19,18},{23,22},{27,26},{31,30}} | collective-permute-start | bytes 1572872 | tf_op jit(solution)/shard_map/ppermute | solution.py:185
  153.8 18.5 %collective-permute-start.27 = (bf16[512,512]{1,0:T(8,128)(2,1)}, bf16[512,512]{1,0:T(8,128)(2,1)}, u32[]{:S(2)}, u32[]{:S(2)}) collective-permute-start(bf16[512,512]{1,0:T(8,128)(2,1)} %get-tuple-element.46), channel_id=1, source_target_pairs={{0,1},{4,5},{8,9},{12,13},{16,17},{20,21},{24,25},{28,29}} | collective-permute-start | bytes 1572872 | tf_op jit(solution)/shard_map/ppermute | solution.py:184
  165.6 20.6 %collective-permute-start.31 = (bf16[512,512]{1,0:T(8,128)(2,1)}, bf16[512,512]{1,0:T(8,128)(2,1)}, u32[]{:S(2)}, u32[]{:S(2)}) collective-permute-start(bf16[512,512]{1,0:T(8,128)(2,1)} %get-tuple-element.51), channel_id=1, source_target_pairs={{3,2},{2,1},{1,0},{7,6},{6,5},{5,4},{11,10},{10,9},{9,8},{15,14},{... | collective-permute-start | bytes 1572872 | tf_op jit(solution)/shard_map/ppermute | solution.py:185
  175.3 17.0 %collective-permute-start.29 = (bf16[512,512]{1,0:T(8,128)(2,1)}, bf16[512,512]{1,0:T(8,128)(2,1)}, u32[]{:S(2)}, u32[]{:S(2)}) collective-permute-start(bf16[512,512]{1,0:T(8,128)(2,1)} %get-tuple-element.48), channel_id=1, source_target_pairs={{0,1},{1,2},{4,5},{5,6},{8,9},{9,10},{12,13},{13,14},{16,17},{17,1... | collective-permute-start | bytes 1572872 | tf_op jit(solution)/shard_map/ppermute | solution.py:184
  180.5 11.8 %collective-permute-start.30 = (bf16[512,512]{1,0:T(8,128)(2,1)}, bf16[512,512]{1,0:T(8,128)(2,1)}, u32[]{:S(2)}, u32[]{:S(2)}) collective-permute-start(bf16[512,512]{1,0:T(8,128)(2,1)} %get-tuple-element.49), channel_id=1, source_target_pairs={{3,2},{2,1},{7,6},{6,5},{11,10},{10,9},{15,14},{14,13},{19,18},{18... | collective-permute-start | bytes 1572872 | tf_op jit(solution)/shard_map/ppermute | solution.py:185
  182.0 18.6 %collective-permute-start.26 = (bf16[512,512]{1,0:T(8,128)(2,1)}, bf16[512,512]{1,0:T(8,128)(2,1)}, u32[]{:S(2)}, u32[]{:S(2)}) collective-permute-start(bf16[512,512]{1,0:T(8,128)(2,1)} %get-tuple-element.42), channel_id=1, source_target_pairs={{0,1},{1,2},{2,3},{4,5},{5,6},{6,7},{8,9},{9,10},{10,11},{12,13},{... | collective-permute-start | bytes 1572872 | tf_op jit(solution)/shard_map/ppermute | solution.py:184
  184.1 16.5 %copy-start.5 = (bf16[512,3072]{1,0:T(8,128)(2,1)S(1)}, bf16[512,3072]{1,0:T(8,128)(2,1)}, u32[]{:S(2)}) copy-start(bf16[512,3072]{1,0:T(8,128)(2,1)} %copy-done.4) | copy-start | bytes 9437188
  184.1 28.4 %collective-permute-start.11 = (bf16[512,1024]{1,0:T(8,128)(2,1)}, bf16[512,1024]{1,0:T(8,128)(2,1)S(1)}, u32[]{:S(2)}, u32[]{:S(2)}) collective-permute-start(bf16[512,1024]{1,0:T(8,128)(2,1)} %collective-permute-done.10), channel_id=1, source_target_pairs={{1,0},{5,4},{9,8},{13,12},{17,16},{21,20},{25,24},{29,28}} | collective-permute-start | bytes 3145736 | tf_op jit(solution)/shard_map/ppermute | solution.py:151
  186.3 31.5 %collective-permute-start.13 = (bf16[512,1024]{1,0:T(8,128)(2,1)}, bf16[512,1024]{1,0:T(8,128)(2,1)S(1)}, u32[]{:S(2)}, u32[]{:S(2)}) collective-permute-start(bf16[512,1024]{1,0:T(8,128)(2,1)} %collective-permute-done.12), channel_id=1, source_target_pairs={{2,3},{6,7},{10,11},{14,15},{18,19},{22,23},{26,27},{30,31}} | collective-permute-start | bytes 3145736 | tf_op jit(solution)/shard_map/ppermute | solution.py:149
  202.3 29.4 %collective-permute-start.38 = (bf16[512,512]{1,0:T(8,128)(2,1)S(1)}, bf16[512,512]{1,0:T(8,128)(2,1)S(1)}, u32[]{:S(2)}, u32[]{:S(2)}) collective-permute-start(bf16[512,512]{1,0:T(8,128)(2,1)S(1)} %get-tuple-element.55), channel_id=1, source_target_pairs={{3,2},{2,1},{1,0},{7,6},{6,5},{5,4},{11,10},{10,9},{9,8},{15,14},{... | collective-permute-start | bytes 1572872 | tf_op jit(solution)/shard_map/ppermute | solution.py:185
  203.6 28.1 %collective-permute-start.37 = (bf16[512,512]{1,0:T(8,128)(2,1)S(1)}, bf16[512,512]{1,0:T(8,128)(2,1)}, u32[]{:S(2)}, u32[]{:S(2)}) collective-permute-start(bf16[512,512]{1,0:T(8,128)(2,1)S(1)} %get-tuple-element.54), channel_id=1, source_target_pairs={{0,1},{1,2},{2,3},{4,5},{5,6},{6,7},{8,9},{9,10},{10,11},{12,13},{... | collective-permute-start | bytes 1572872 | tf_op jit(solution)/shard_map/ppermute | solution.py:184
  209.5 13.6 %slice-start.6 = ((s8[6291456]{0:T(1024)(128)(4,1)}), s8[4194304]{0:T(1024)(128)(4,1)S(1)}, s32[]{:S(2)}) async-start(s8[6291456]{0:T(1024)(128)(4,1)} %bitcast.102), calls=%async_computation.6 | async-start | bytes 8388608
  213.7 6.7 %copy-start.13 = (bf16[512,1024]{1,0:T(8,128)(2,1)S(1)}, bf16[512,1024]{1,0:T(8,128)(2,1)}, u32[]{:S(2)}) copy-start(bf16[512,1024]{1,0:T(8,128)(2,1)} %copy-done.12) | copy-start | bytes 3145732
  220.4 7.0 %slice-start = ((s8[10485760]{0:T(1024)(128)(4,1)}), s8[4194304]{0:T(1024)(128)(4,1)S(1)}, s32[]{:S(2)}) async-start(s8[10485760]{0:T(1024)(128)(4,1)} %bitcast.98), calls=%async_computation | async-start | bytes 8388608
  223.1 4.3 %slice-start.1 = ((s8[10485760]{0:T(1024)(128)(4,1)}), s8[4194304]{0:T(1024)(128)(4,1)S(1)}, s32[]{:S(2)}) async-start(s8[10485760]{0:T(1024)(128)(4,1)} %bitcast.98), calls=%async_computation.1 | async-start | bytes 8388608
  223.1 4.3 %slice-start.2 = ((s8[10485760]{0:T(1024)(128)(4,1)}), s8[2097152]{0:T(1024)(128)(4,1)S(1)}, s32[]{:S(2)}) async-start(s8[10485760]{0:T(1024)(128)(4,1)} %bitcast.98), calls=%async_computation.2 | async-start | bytes 4194304
  231.7 13.9 %collective-permute-start.32 = (bf16[2560,512]{1,0:T(8,128)(2,1)}, bf16[2560,512]{1,0:T(8,128)(2,1)}, u32[]{:S(2)}, u32[]{:S(2)}) collective-permute-start(bf16[2560,512]{1,0:T(8,128)(2,1)} %fusion.8), channel_id=1, source_target_pairs={{0,4},{4,0},{8,12},{12,8},{16,20},{20,16},{24,28},{28,24},{1,5},{5... | collective-permute-start | bytes 7864328 | tf_op jit(solution)/shard_map/ppermute | solution.py:21
  231.7 8.0 %slice-start.3 = ((s8[10485760]{0:T(1024)(128)(4,1)}), s8[4194304]{0:T(1024)(128)(4,1)S(1)}, s32[]{:S(2)}) async-start(s8[10485760]{0:T(1024)(128)(4,1)} %bitcast.100), calls=%async_computation.3 | async-start | bytes 8388608
  233.5 6.3 %slice-start.4 = ((s8[10485760]{0:T(1024)(128)(4,1)}), s8[4194304]{0:T(1024)(128)(4,1)S(1)}, s32[]{:S(2)}) async-start(s8[10485760]{0:T(1024)(128)(4,1)} %bitcast.100), calls=%async_computation.4 | async-start | bytes 8388608
  233.5 6.3 %slice-start.5 = ((s8[10485760]{0:T(1024)(128)(4,1)}), s8[2097152]{0:T(1024)(128)(4,1)S(1)}, s32[]{:S(2)}) async-start(s8[10485760]{0:T(1024)(128)(4,1)} %bitcast.100), calls=%async_computation.5 | async-start | bytes 4194304
  233.5 6.3 %copy-start.10 = (bf16[512,512]{1,0:T(8,128)(2,1)S(1)}, bf16[512,512]{1,0:T(8,128)(2,1)}, u32[]{:S(2)}) copy-start(bf16[512,512]{1,0:T(8,128)(2,1)} %copy-done.9) | copy-start | bytes 1572868
  239.2 10.6 %collective-permute-start.39 = (bf16[2560,512]{1,0:T(8,128)(2,1)S(1)}, bf16[2560,512]{1,0:T(8,128)(2,1)S(1)}, u32[]{:S(2)}, u32[]{:S(2)}) collective-permute-start(bf16[2560,512]{1,0:T(8,128)(2,1)S(1)} %fusion.11), channel_id=1, source_target_pairs={{0,4},{4,0},{8,12},{12,8},{16,20},{20,16},{24,28},{28,24},{1,5},{5... | collective-permute-start | bytes 7864328 | tf_op jit(solution)/shard_map/ppermute | solution.py:21
  248.7 17.7 %collective-permute-start.35 = (bf16[2,640,256]{2,1,0:T(8,128)(2,1)S(1)}, bf16[2,640,256]{2,1,0:T(8,128)(2,1)S(1)}, u32[]{:S(2)}, u32[]{:S(2)}) collective-permute-start(bf16[2,640,256]{2,1,0:T(8,128)(2,1)S(1)} %pad_maximum_fusion.4), channel_id=1, source_target_pairs={{0,16},{4,20},{8,24},{12,28},{16,0},{20,4},{24,8},{28,12},{1,17},{... | collective-permute-start | bytes 1966088 | tf_op jit(solution)/shard_map/ppermute | solution.py:21
  250.7 45.7 %copy-start.6 = (bf16[2560,512]{1,0:T(8,128)(2,1)}, bf16[2560,512]{1,0:T(8,128)(2,1)S(1)}, u32[]{:S(2)}) copy-start(bf16[2560,512]{1,0:T(8,128)(2,1)S(1)} %add_convert_fusion) | copy-start | bytes 7864324
  250.9 28.6 %collective-permute-start.42 = (bf16[2,640,256]{2,1,0:T(8,128)(2,1)S(1)}, bf16[2,640,256]{2,1,0:T(8,128)(2,1)S(1)}, u32[]{:S(2)}, u32[]{:S(2)}) collective-permute-start(bf16[2,640,256]{2,1,0:T(8,128)(2,1)S(1)} %pad_maximum_fusion.6), channel_id=1, source_target_pairs={{0,16},{4,20},{8,24},{12,28},{16,0},{20,4},{24,8},{28,12},{1,17},{... | collective-permute-start | bytes 1966088 | tf_op jit(solution)/shard_map/ppermute | solution.py:21
  252.1 28.5 %collective-permute-start.33 = (bf16[2,640,256]{2,1,0:T(8,128)(2,1)S(1)}, bf16[2,640,256]{2,1,0:T(8,128)(2,1)S(1)}, u32[]{:S(2)}, u32[]{:S(2)}) collective-permute-start(bf16[2,640,256]{2,1,0:T(8,128)(2,1)S(1)} %pad_maximum_fusion.3), channel_id=1, source_target_pairs={{0,8},{4,12},{8,0},{12,4},{16,24},{20,28},{24,16},{28,20},{1,9},{5... | collective-permute-start | bytes 1966088 | tf_op jit(solution)/shard_map/ppermute | solution.py:21
  253.2 39.5 %collective-permute-start.40 = (bf16[2,640,256]{2,1,0:T(8,128)(2,1)S(1)}, bf16[2,640,256]{2,1,0:T(8,128)(2,1)S(1)}, u32[]{:S(2)}, u32[]{:S(2)}) collective-permute-start(bf16[2,640,256]{2,1,0:T(8,128)(2,1)S(1)} %pad_maximum_fusion.5), channel_id=1, source_target_pairs={{0,8},{4,12},{8,0},{12,4},{16,24},{20,28},{24,16},{28,20},{1,9},{5... | collective-permute-start | bytes 1966088 | tf_op jit(solution)/shard_map/ppermute | solution.py:21
  266.5 24.4 %collective-permute-start.36 = (bf16[1,640,256]{2,1,0:T(8,128)(2,1)S(1)}, bf16[1,640,256]{2,1,0:T(8,128)(2,1)S(1)}, u32[]{:S(2)}, u32[]{:S(2)}) collective-permute-start(bf16[1,640,256]{2,1,0:T(8,128)(2,1)S(1)} %fusion.36), channel_id=1, source_target_pairs={{0,8},{4,12},{8,0},{12,4},{16,24},{20,28},{24,16},{28,20},{1,9},{5... | collective-permute-start | bytes 983048 | tf_op jit(solution)/shard_map/ppermute | solution.py:21
  279.6 16.8 %collective-permute-start.43 = (bf16[1,640,256]{2,1,0:T(8,128)(2,1)S(1)}, bf16[1,640,256]{2,1,0:T(8,128)(2,1)S(1)}, u32[]{:S(2)}, u32[]{:S(2)}) collective-permute-start(bf16[1,640,256]{2,1,0:T(8,128)(2,1)S(1)} %fusion.38), channel_id=1, source_target_pairs={{0,8},{4,12},{8,0},{12,4},{16,24},{20,28},{24,16},{28,20},{1,9},{5... | collective-permute-start | bytes 983048 | tf_op jit(solution)/shard_map/ppermute | solution.py:21
  291.7 7.2 %collective-permute-start.34 = (bf16[1,640,256]{2,1,0:T(8,128)(2,1)S(1)}, bf16[1,640,256]{2,1,0:T(8,128)(2,1)S(1)}, u32[]{:S(2)}, u32[]{:S(2)}) collective-permute-start(bf16[1,640,256]{2,1,0:T(8,128)(2,1)S(1)} %get-tuple-element.82), channel_id=1, source_target_pairs={{0,16},{4,20},{8,24},{12,28},{16,0},{20,4},{24,8},{28,12},{1,17},{... | collective-permute-start | bytes 983048 | tf_op jit(solution)/shard_map/ppermute | solution.py:21
  298.0 8.6 %collective-permute-start.41 = (bf16[1,640,256]{2,1,0:T(8,128)(2,1)}, bf16[1,640,256]{2,1,0:T(8,128)(2,1)}, u32[]{:S(2)}, u32[]{:S(2)}) collective-permute-start(bf16[1,640,256]{2,1,0:T(8,128)(2,1)} %get-tuple-element.77), channel_id=1, source_target_pairs={{0,16},{4,20},{8,24},{12,28},{16,0},{20,4},{24,8},{28,12},{1,17},{... | collective-permute-start | bytes 983048 | tf_op jit(solution)/shard_map/ppermute | solution.py:21
  309.7 1.2 collective-permute-start.44
  310.9 4.5 %collective-permute-start.47 = (f32[8,128]{1,0:T(8,128)S(1)}, f32[8,128]{1,0:T(8,128)S(1)}, u32[]{:S(2)}, u32[]{:S(2)}) collective-permute-start(f32[8,128]{1,0:T(8,128)S(1)} %broadcast_add_fusion), channel_id=1, source_target_pairs={{0,24},{4,28},{8,16},{12,20},{16,8},{20,12},{24,0},{28,4},{1,25},{... | collective-permute-start | bytes 12296 | tf_op jit(solution)/shard_map/ppermute | solution.py:21
  312.8 3.6 %collective-permute-start.45 = (f32[8,128]{1,0:T(8,128)S(1)}, f32[8,128]{1,0:T(8,128)S(1)}, u32[]{:S(2)}, u32[]{:S(2)}) collective-permute-start(f32[8,128]{1,0:T(8,128)S(1)} %broadcast_add_fusion), channel_id=1, source_target_pairs={{0,8},{4,12},{8,0},{12,4},{16,24},{20,28},{24,16},{28,20},{1,9},{5... | collective-permute-start | bytes 12296 | tf_op jit(solution)/shard_map/ppermute | solution.py:21
  313.3 3.6 %collective-permute-start.46 = (f32[8,128]{1,0:T(8,128)S(1)}, f32[8,128]{1,0:T(8,128)S(1)}, u32[]{:S(2)}, u32[]{:S(2)}) collective-permute-start(f32[8,128]{1,0:T(8,128)S(1)} %broadcast_add_fusion), channel_id=1, source_target_pairs={{0,16},{4,20},{8,24},{12,28},{16,0},{20,4},{24,8},{28,12},{1,17},{... | collective-permute-start | bytes 12296 | tf_op jit(solution)/shard_map/ppermute | solution.py:21
  316.9 5.5 %collective-permute-start.50 = (f32[8,128]{1,0:T(8,128)S(1)}, f32[8,128]{1,0:T(8,128)S(1)}, u32[]{:S(2)}, u32[]{:S(2)}) collective-permute-start(f32[8,128]{1,0:T(8,128)S(1)} %add_add_fusion.1), channel_id=1, source_target_pairs={{0,3},{1,0},{2,1},{3,2},{4,7},{5,4},{6,5},{7,6},{8,11},{9,8},{10,9... | collective-permute-start | bytes 12296 | tf_op jit(solution)/shard_map/ppermute | solution.py:221
  321.0 5.4 %collective-permute-start.48 = (f32[8,128]{1,0:T(8,128)S(1)}, f32[8,128]{1,0:T(8,128)S(1)}, u32[]{:S(2)}, u32[]{:S(2)}) collective-permute-start(f32[8,128]{1,0:T(8,128)S(1)} %add_add_fusion.1), channel_id=1, source_target_pairs={{0,1},{1,2},{2,3},{3,0},{4,5},{5,6},{6,7},{7,4},{8,9},{9,10},{10,1... | collective-permute-start | bytes 12296 | tf_op jit(solution)/shard_map/ppermute | solution.py:221
  321.1 5.4 %collective-permute-start.49 = (f32[8,128]{1,0:T(8,128)S(1)}, f32[8,128]{1,0:T(8,128)S(1)}, u32[]{:S(2)}, u32[]{:S(2)}) collective-permute-start(f32[8,128]{1,0:T(8,128)S(1)} %add_add_fusion.1), channel_id=1, source_target_pairs={{0,2},{1,3},{2,0},{3,1},{4,6},{5,7},{6,4},{7,5},{8,10},{9,11},{10,... | collective-permute-start | bytes 12296 | tf_op jit(solution)/shard_map/ppermute | solution.py:221
  (9 other events, 26.6 us)
where the time goes:
time: 329 us; the launch traced here: 328 us
  waiting for transfers between devices  142 us (43%)
  starting transfers between devices  82.1 us (25%)
  matrix products  39.4 us (12%)
  other arithmetic  33.9 us (10%)
  local copies, waits for them, and re-layouts  21.8 us (7%)
  Pallas kernels  5.27 us (2%)
    ppermute x30, waiting for transfers between devices, flip(): return lax.ppermute(value, axis, [(i, i ^ bit) for i in range(size)])  100 us
    dot_general x10, matrix products, dot(): lax.dot_general(left, right, ((dims[:1], dims[1:]), ((), ())), preferred_...  39.4 us
    ppermute x6, starting transfers between devices, per_device(): up = lax.ppermute(send_up, 'tp', [(i, i + 1) for i in range(hop)])  31.5 us
    ppermute x30, starting transfers between devices, flip(): return lax.ppermute(value, axis, [(i, i ^ bit) for i in range(size)])  25.3 us
    ppermute x6, waiting for transfers between devices, per_device(): up = lax.ppermute(send_up, 'tp', [(i, i + 1) for i in range(hop)])  24 us
    unnamed x58, local copies, waits for them, and re-layouts  12.7 us
    convert_element_type x4, other arithmetic, per_device(): send_up, send_down = (send_up.astype(BF), send_down.astype(BF))  10.6 us
    ppermute x6, starting transfers between devices, per_device(): lax.ppermute(send_down, 'tp', [(last - i, last - 1 - i) for i in range(ho...  8.41 us
  transfers between devices with their start and end apart: 51, of which 25 were waited for; matrix products, arithmetic and copies ran while one was open for 26% of the time, Pallas kernels for 1%

commit v1 on v0

--- a/solution.py
+++ b/solution.py
@@ -201,16 +201,21 @@
         keep = after(dot(both[:, :split], values, (0, 0)), values)
         pair = (keep + arrived.astype(F32)).astype(BF)
         blocks = {m: pair[i * rows : (i + 1) * rows] for i, m in enumerate(keeps)}
-        for number, sequence in enumerate((bits, bits[::-1])):
-            lo = number * (depth // 2)
-            held = {m: blocks[m][:, lo : lo + depth // 2].astype(F32) for m in keeps}
-            for bit in sequence:
-                leaving = [m for m in held if m & bit]
-                packed = jnp.stack([held[m].astype(BF) for m in leaving])
-                packed = flip(packed, "fsdp", n_fsdp, bit)
-                for i, m in enumerate(leaving):
+        half = depth // 2
+        halves = [
+            {m: blocks[m][:, n * half : (n + 1) * half].astype(F32) for m in keeps} for n in range(2)
+        ]
+        for turn in range(len(bits)):
+            arrived = []
+            for held, bit in zip(halves, (bits[turn], bits[-1 - turn])):
+                packed = jnp.stack([held[m].astype(BF) for m in held if m & bit])
+                arrived.append(flip(packed, "fsdp", n_fsdp, bit))
+            arrived = lax.optimization_barrier(tuple(arrived))
+            for held, bit, packed in zip(halves, (bits[turn], bits[-1 - turn]), arrived):
+                for i, m in enumerate([m for m in held if m & bit]):
                     held[m ^ bit] = held[m ^ bit] + packed[i].astype(F32)
                     del held[m]
+        for held in halves:
             pieces.append(held[0])
             squares = squares + jnp.sum(held[0] * held[0])
 

time: 329 us -> 319 us (0.970)
  waiting for transfers between devices: 142 us -> 132 us
    ppermute x30, waiting for transfers between devices: 100 us -> 90.5 us  [flip(): return lax.ppermute(value, axis, [(i, i ^ bit) for i in range(size)])]
    unnamed x58 -> x62, local copies, waits for them, and re-layouts: 12.7 us -> 13.4 us
  transfers between devices with their start and end apart: 51 -> 51, of which waited for: 25 -> 26; matrix products, arithmetic and copies ran while one was open for 26% -> 26% of each run, Pallas kernels for 1% -> 1%
where the time goes in v1:
time: 319 us; the launch traced here: 318 us
  waiting for transfers between devices  132 us (41%)
  starting transfers between devices  82.4 us (26%)
  matrix products  39.6 us (12%)
  other arithmetic  32.4 us (10%)
  local copies, waits for them, and re-layouts  22.5 us (7%)
  Pallas kernels  5.27 us (2%)
  between operations  3.25 us (1%)
    ppermute x30, waiting for transfers between devices, flip(): return lax.ppermute(value, axis, [(i, i ^ bit) for i in range(size)])  90.5 us
    dot_general x10, matrix products, dot(): lax.dot_general(left, right, ((dims[:1], dims[1:]), ((), ())), preferred_...  39.6 us
    ppermute x6, starting transfers between devices, per_device(): up = lax.ppermute(send_up, 'tp', [(i, i + 1) for i in range(hop)])  31.5 us
    ppermute x30, starting transfers between devices, flip(): return lax.ppermute(value, axis, [(i, i ^ bit) for i in range(size)])  25.7 us
    ppermute x6, waiting for transfers between devices, per_device(): up = lax.ppermute(send_up, 'tp', [(i, i + 1) for i in range(hop)])  24 us
    unnamed x62, local copies, waits for them, and re-layouts  13.4 us
    convert_element_type x4, other arithmetic, per_device(): send_up, send_down = (send_up.astype(BF), send_down.astype(BF))  10.6 us
    ppermute x6, starting transfers between devices, per_device(): lax.ppermute(send_down, 'tp', [(last - i, last - 1 - i) for i in range(ho...  8.42 us
  transfers between devices with their start and end apart: 51, of which 26 were waited for; matrix products, arithmetic and copies ran while one was open for 26% of the time, Pallas kernels for 1%

profile of v1, /device:TPU:0, one launch (start us, length us, event | category | flops | bytes accessed | tf_op | source)
XLA Modules:
  0.0 317.5 jit_solution(14652193696682759953)
XLA Ops:
  0.0 3.0 collective-permute-start
  3.0 1.5 collective-permute-start.1
  4.6 2.5 copy-done.1
  7.1 2.5 copy-done.2
  10.2 4.0 %shard_map.55 = bf16[1024,5120]{1,0:T(8,128)(2,1)S(1)} custom-call(s32[8]{0:T(128)S(1)} %stack.83.places, s32[2]{0:T(128)S(1)} %copy-done.3, bf16[512,5120]{1,0:T(8,128)(2,1)S(1)} %copy-done.1, bf16[512,5120]{1,0:T(8,128)(2,1)S(1)} %copy-done.2), custom_call_target="tpu_custom_call" | custom-call | bytes 20971520 | tf_op jit(solution)/shard_map/pallas_call | solution.py:74
  14.2 17.7 %collective-permute-done = bf16[640,1024]{1,0:T(8,128)(2,1)S(1)} collective-permute-done((bf16[640,1024]{1,0:T(8,128)(2,1)}, bf16[640,1024]{1,0:T(8,128)(2,1)S(1)}, u32[]{:S(2)}, u32[]{:S(2)}) %collective-permute-start) | collective-permute-done | bytes 1310752 | tf_op jit(solution)/shard_map/ppermute | solution.py:21
  32.0 1.8 collective-permute-start.2
  33.9 1.6 collective-permute-start.3
  36.0 12.0 %collective-permute-done.2 = bf16[320,1024]{1,0:T(8,128)(2,1)S(1)} collective-permute-done((bf16[320,1024]{1,0:T(8,128)(2,1)S(1)}, bf16[320,1024]{1,0:T(8,128)(2,1)S(1)}, u32[]{:S(2)}, u32[]{:S(2)}) %collective-permute-start.2) | collective-permute-done | bytes 655392 | tf_op jit(solution)/shard_map/ppermute | solution.py:21
  49.8 1.6 collective-permute-start.15
  52.6 11.2 %convolution_convert_fusion.1 = bf16[1024,1024]{1,0:T(8,128)(2,1)S(1)} fusion(bf16[1024,5120]{1,0:T(8,128)(2,1)S(1)} %shard_map.55, bf16[5120,1024]{1,0:T(8,128)(2,1)S(1)} %constant_dynamic-update-slice_fusion), kind=kOutput, calls=%fused_computation.22 | convolution fusion | flops 10738466816 | bytes 23068672 | tf_op jit(solution)/shard_map/dot_general | solution.py:17
  65.1 10.7 %collective-permute-done.15 = bf16[512,1024]{1,0:T(8,128)(2,1)} collective-permute-done((bf16[512,1024]{1,0:T(8,128)(2,1)}, bf16[512,1024]{1,0:T(8,128)(2,1)}, u32[]{:S(2)}, u32[]{:S(2)}) %collective-permute-start.15) | collective-permute-done | bytes 1048608 | tf_op jit(solution)/shard_map/ppermute | solution.py:21
  75.7 1.9 slice.201
  78.7 1.9 slice.202
  83.0 8.4 %collective-permute-done.19 = bf16[256,1024]{1,0:T(8,128)(2,1)} collective-permute-done((bf16[256,1024]{1,0:T(8,128)(2,1)}, bf16[256,1024]{1,0:T(8,128)(2,1)}, u32[]{:S(2)}, u32[]{:S(2)}) %collective-permute-start.19) | collective-permute-done | bytes 524320 | tf_op jit(solution)/shard_map/ppermute | solution.py:21
  92.5 2.8 collective-permute-done.20
  101.7 3.7 %convolution_convert_fusion = bf16[512,3072]{1,0:T(8,128)(2,1)S(1)} fusion(bf16[3072,1024]{1,0:T(8,128)(2,1)S(1)} %constant_dynamic-update-slice_fusion.9, bf16[1024,1024]{1,0:T(8,128)(2,1)S(1)} %convolution_convert_fusion.1), kind=kOutput, calls=%fused_computation.12 | convolution fusion | flops 3222798336 | bytes 10485760 | tf_op jit(solution)/shard_map/dot_general | solution.py:17
  106.2 1.9 select_select_fusion.2
  108.1 1.5 collective-permute-start.23
  109.6 4.3 %collective-permute-start.22 = (bf16[512,512]{1,0:T(8,128)(2,1)}, bf16[512,512]{1,0:T(8,128)(2,1)}, u32[]{:S(2)}, u32[]{:S(2)}) collective-permute-start(bf16[512,512]{1,0:T(8,128)(2,1)} %get-tuple-element.46), channel_id=1, source_target_pairs={{0,1},{4,5},{8,9},{12,13},{16,17},{20,21},{24,25},{28,29}} | collective-permute-start | bytes 1572872 | tf_op jit(solution)/shard_map/ppermute | solution.py:184
  115.2 5.6 %collective-permute-start.8 = (bf16[512,1024]{1,0:T(8,128)(2,1)}, bf16[512,1024]{1,0:T(8,128)(2,1)}, u32[]{:S(2)}, u32[]{:S(2)}) collective-permute-start(bf16[512,1024]{1,0:T(8,128)(2,1)} %fusion.43), channel_id=1, source_target_pairs={{0,1},{1,2},{2,3},{4,5},{5,6},{6,7},{8,9},{9,10},{10,11},{12,13},{... | collective-permute-start | bytes 3145736 | tf_op jit(solution)/shard_map/ppermute | solution.py:149
  120.7 5.0 %collective-permute-done.22 = bf16[512,512]{1,0:T(8,128)(2,1)} collective-permute-done((bf16[512,512]{1,0:T(8,128)(2,1)}, bf16[512,512]{1,0:T(8,128)(2,1)}, u32[]{:S(2)}, u32[]{:S(2)}) %collective-permute-start.22) | collective-permute-done | bytes 524320 | tf_op jit(solution)/shard_map/ppermute | solution.py:184
  125.7 3.0 add_convert_fusion.11
  128.6 1.4 collective-permute-start.25
  130.1 5.2 %collective-permute-start.24 = (bf16[512,512]{1,0:T(8,128)(2,1)}, bf16[512,512]{1,0:T(8,128)(2,1)}, u32[]{:S(2)}, u32[]{:S(2)}) collective-permute-start(bf16[512,512]{1,0:T(8,128)(2,1)} %get-tuple-element.48), channel_id=1, source_target_pairs={{0,1},{1,2},{4,5},{5,6},{8,9},{9,10},{12,13},{13,14},{16,17},{17,1... | collective-permute-start | bytes 1572872 | tf_op jit(solution)/shard_map/ppermute | solution.py:184
  135.3 6.0 %collective-permute-done.9 = bf16[512,1024]{1,0:T(8,128)(2,1)} collective-permute-done((bf16[512,1024]{1,0:T(8,128)(2,1)}, bf16[512,1024]{1,0:T(8,128)(2,1)}, u32[]{:S(2)}, u32[]{:S(2)}) %collective-permute-start.9) | collective-permute-done | bytes 1048608 | tf_op jit(solution)/shard_map/ppermute | solution.py:151
  142.6 5.5 %collective-permute-done.8 = bf16[512,1024]{1,0:T(8,128)(2,1)} collective-permute-done((bf16[512,1024]{1,0:T(8,128)(2,1)}, bf16[512,1024]{1,0:T(8,128)(2,1)}, u32[]{:S(2)}, u32[]{:S(2)}) %collective-permute-start.8) | collective-permute-done | bytes 1048608 | tf_op jit(solution)/shard_map/ppermute | solution.py:149
  148.1 1.7 collective-permute-start.12
  149.8 2.5 select_select_fusion
  152.3 1.5 collective-permute-start.28
  153.8 8.9 %collective-permute-start.27 = (bf16[512,512]{1,0:T(8,128)(2,1)}, bf16[512,512]{1,0:T(8,128)(2,1)}, u32[]{:S(2)}, u32[]{:S(2)}) collective-permute-start(bf16[512,512]{1,0:T(8,128)(2,1)} %get-tuple-element.54), channel_id=1, source_target_pairs={{0,1},{4,5},{8,9},{12,13},{16,17},{20,21},{24,25},{28,29}} | collective-permute-start | bytes 1572872 | tf_op jit(solution)/shard_map/ppermute | solution.py:184
  162.7 2.9 add_convert_fusion.9
  166.9 5.4 %collective-permute-done.27 = bf16[512,512]{1,0:T(8,128)(2,1)} collective-permute-done((bf16[512,512]{1,0:T(8,128)(2,1)}, bf16[512,512]{1,0:T(8,128)(2,1)}, u32[]{:S(2)}, u32[]{:S(2)}) %collective-permute-start.27) | collective-permute-done | bytes 524320 | tf_op jit(solution)/shard_map/ppermute | solution.py:184
  172.3 3.0 add_convert_fusion.7
  175.3 5.2 %collective-permute-start.29 = (bf16[512,512]{1,0:T(8,128)(2,1)}, bf16[512,512]{1,0:T(8,128)(2,1)}, u32[]{:S(2)}, u32[]{:S(2)}) collective-permute-start(bf16[512,512]{1,0:T(8,128)(2,1)} %get-tuple-element.56), channel_id=1, source_target_pairs={{0,1},{1,2},{4,5},{5,6},{8,9},{9,10},{12,13},{13,14},{16,17},{17,1... | collective-permute-start | bytes 1572872 | tf_op jit(solution)/shard_map/ppermute | solution.py:184
  180.5 1.5 collective-permute-start.30
  182.0 2.1 collective-permute-start.26
  184.1 1.5 collective-permute-start.11
  187.0 5.3 %collective-permute-done.29 = bf16[512,512]{1,0:T(8,128)(2,1)} collective-permute-done((bf16[512,512]{1,0:T(8,128)(2,1)}, bf16[512,512]{1,0:T(8,128)(2,1)}, u32[]{:S(2)}, u32[]{:S(2)}) %collective-permute-start.29) | collective-permute-done | bytes 524320 | tf_op jit(solution)/shard_map/ppermute | solution.py:184
  192.3 8.3 %collective-permute-done.26 = bf16[512,512]{1,0:T(8,128)(2,1)} collective-permute-done((bf16[512,512]{1,0:T(8,128)(2,1)}, bf16[512,512]{1,0:T(8,128)(2,1)}, u32[]{:S(2)}, u32[]{:S(2)}) %collective-permute-start.26) | collective-permute-done | bytes 524320 | tf_op jit(solution)/shard_map/ppermute | solution.py:184
  200.6 1.8 add_convert_fusion.4
  203.7 5.8 %collective-permute-start.37 = (bf16[512,512]{1,0:T(8,128)(2,1)S(1)}, bf16[512,512]{1,0:T(8,128)(2,1)}, u32[]{:S(2)}, u32[]{:S(2)}) collective-permute-start(bf16[512,512]{1,0:T(8,128)(2,1)S(1)} %get-tuple-element.66), channel_id=1, source_target_pairs={{0,1},{1,2},{2,3},{4,5},{5,6},{6,7},{8,9},{9,10},{10,11},{12,13},{... | collective-permute-start | bytes 1572872 | tf_op jit(solution)/shard_map/ppermute | solution.py:184
  209.5 1.7 add_convert_fusion.6
  220.5 2.6 fusion.16
  223.1 3.4 %add_convert_fusion.2 = bf16[512,1024]{1,0:T(8,128)(2,1)S(1)} fusion(f32[512,1024]{1,0:T(8,128)S(1)} %fusion.16, bf16[3072,1024]{1,0:T(8,128)(2,1)S(1)} %bitcast.87, bf16[512,4096]{1,0:T(8,128)(2,1)S(1)} %fusion.29), kind=kOutput, calls=%fused_computation.21 | convolution fusion | flops 3222274048 | bytes 12582912 | tf_op jit(solution)/shard_map/dot_general | solution.py:17
  227.5 4.3 %fusion.8 = bf16[2560,512]{1,0:T(8,128)(2,1)} fusion(bf16[1024,5120]{1,0:T(8,128)(2,1)S(1)} %bitcast.83, bf16[512,512]{1,0:T(8,128)(2,1)S(1)} %add_convert_fusion.6, bf16[512,512]{1,0:T(8,128)(2,1)S(1)} %get-tuple-element.112), kind=kOutput, calls=%fused_computation.10 | convolution fusion | flops 2687762432 | bytes 8912896 | tf_op jit(solution)/shard_map/dot_general | solution.py:17
  231.8 1.7 add_convert_fusion.3
  233.5 5.7 %fusion.11 = bf16[2560,512]{1,0:T(8,128)(2,1)S(1)} fusion(bf16[1024,5120]{1,0:T(8,128)(2,1)} %copy-done, bf16[512,512]{1,0:T(8,128)(2,1)S(1)} %add_convert_fusion.3, bf16[512,512]{1,0:T(8,128)(2,1)} %get-tuple-element.111), kind=kOutput, calls=%fused_computation.11 | convolution fusion | flops 2687762432 | bytes 8912896 | tf_op jit(solution)/shard_map/dot_general | solution.py:17
  239.8 3.0 fusion.6
  242.8 3.0 fusion.4
  245.9 2.9 add_convert_fusion.1
  249.9 1.6 collective-permute-start.34
  254.5 12.1 %collective-permute-done.33 = bf16[2,640,256]{2,1,0:T(8,128)(2,1)S(1)} collective-permute-done((bf16[2,640,256]{2,1,0:T(8,128)(2,1)S(1)}, bf16[2,640,256]{2,1,0:T(8,128)(2,1)S(1)}, u32[]{:S(2)}, u32[]{:S(2)}) %collective-permute-start.33) | collective-permute-done | bytes 655392 | tf_op jit(solution)/shard_map/ppermute | solution.py:21
  267.8 1.6 collective-permute-start.35
  269.9 10.7 %collective-permute-done.40 = bf16[2,640,256]{2,1,0:T(8,128)(2,1)S(1)} collective-permute-done((bf16[2,640,256]{2,1,0:T(8,128)(2,1)S(1)}, bf16[2,640,256]{2,1,0:T(8,128)(2,1)S(1)}, u32[]{:S(2)}, u32[]{:S(2)}) %collective-permute-start.40) | collective-permute-done | bytes 655392 | tf_op jit(solution)/shard_map/ppermute | solution.py:21
  281.9 1.6 collective-permute-start.42
  284.0 4.7 %collective-permute-done.35 = bf16[1,640,256]{2,1,0:T(8,128)(2,1)S(1)} collective-permute-done((bf16[1,640,256]{2,1,0:T(8,128)(2,1)S(1)}, bf16[1,640,256]{2,1,0:T(8,128)(2,1)S(1)}, u32[]{:S(2)}, u32[]{:S(2)}) %collective-permute-start.35) | collective-permute-done | bytes 327712 | tf_op jit(solution)/shard_map/ppermute | solution.py:21
  290.8 3.6 %collective-permute-done.42 = bf16[1,640,256]{2,1,0:T(8,128)(2,1)S(1)} collective-permute-done((bf16[1,640,256]{2,1,0:T(8,128)(2,1)S(1)}, bf16[1,640,256]{2,1,0:T(8,128)(2,1)S(1)}, u32[]{:S(2)}, u32[]{:S(2)}) %collective-permute-start.42) | collective-permute-done | bytes 327712 | tf_op jit(solution)/shard_map/ppermute | solution.py:21
  295.2 2.3 multiply_reduce_fusion
  300.1 1.5 collective-permute-start.47
  301.6 1.5 collective-permute-start.45
  305.2 1.5 collective-permute-done.46
  306.7 4.1 %collective-permute-start.50 = (f32[8,128]{1,0:T(8,128)S(1)}, f32[8,128]{1,0:T(8,128)S(1)}, u32[]{:S(2)}, u32[]{:S(2)}) collective-permute-start(f32[8,128]{1,0:T(8,128)S(1)} %add_add_fusion.1), channel_id=1, source_target_pairs={{0,3},{1,0},{2,1},{3,2},{4,7},{5,4},{6,5},{7,6},{8,11},{9,8},{10,9... | collective-permute-start | bytes 12296 | tf_op jit(solution)/shard_map/ppermute | solution.py:226
  312.2 4.1 %collective-permute-done.48 = f32[8,128]{1,0:T(8,128)S(1)} collective-permute-done((f32[8,128]{1,0:T(8,128)S(1)}, f32[8,128]{1,0:T(8,128)S(1)}, u32[]{:S(2)}, u32[]{:S(2)}) %collective-permute-start.48) | collective-permute-done | bytes 4128 | tf_op jit(solution)/shard_map/ppermute | solution.py:226
  (158 shorter events, 49.8 us)
Async XLA Ops:
  0.0 32.0 %collective-permute-start = (bf16[640,1024]{1,0:T(8,128)(2,1)}, bf16[640,1024]{1,0:T(8,128)(2,1)S(1)}, u32[]{:S(2)}, u32[]{:S(2)}) collective-permute-start(bf16[640,1024]{1,0:T(8,128)(2,1)} %param.8), channel_id=1, source_target_pairs={{0,8},{4,12},{8,0},{12,4},{16,24},{20,28},{24,16},{28,20},{1,9},{5... | collective-permute-start | bytes 3932168 | tf_op jit(solution)/shard_map/ppermute | solution.py:21
  3.0 30.9 %collective-permute-start.1 = (bf16[640,1024]{1,0:T(8,128)(2,1)}, bf16[640,1024]{1,0:T(8,128)(2,1)S(1)}, u32[]{:S(2)}, u32[]{:S(2)}) collective-permute-start(bf16[640,1024]{1,0:T(8,128)(2,1)} %param.8), channel_id=1, source_target_pairs={{0,16},{4,20},{8,24},{12,28},{16,0},{20,4},{24,8},{28,12},{1,17},{... | collective-permute-start | bytes 3932168 | tf_op jit(solution)/shard_map/ppermute | solution.py:21
  10.2 25.2 %copy-start.7 = (bf16[640,1024]{1,0:T(8,128)(2,1)S(1)}, bf16[640,1024]{1,0:T(8,128)(2,1)}, u32[]{:S(2)}) copy-start(bf16[640,1024]{1,0:T(8,128)(2,1)} %param.8) | copy-start | bytes 3932164
  14.2 38.4 %copy-start = (bf16[1024,5120]{1,0:T(8,128)(2,1)}, bf16[1024,5120]{1,0:T(8,128)(2,1)S(1)}, u32[]{:S(2)}) copy-start(bf16[1024,5120]{1,0:T(8,128)(2,1)S(1)} %shard_map.55) | copy-start | bytes 31457284
  32.0 16.0 %collective-permute-start.2 = (bf16[320,1024]{1,0:T(8,128)(2,1)S(1)}, bf16[320,1024]{1,0:T(8,128)(2,1)S(1)}, u32[]{:S(2)}, u32[]{:S(2)}) collective-permute-start(bf16[320,1024]{1,0:T(8,128)(2,1)S(1)} %slice.181), channel_id=1, source_target_pairs={{0,16},{4,20},{8,24},{12,28},{16,0},{20,4},{24,8},{28,12},{1,17},{... | collective-permute-start | bytes 1966088 | tf_op jit(solution)/shard_map/ppermute | solution.py:21
  33.9 15.4 %collective-permute-start.3 = (bf16[320,1024]{1,0:T(8,128)(2,1)S(1)}, bf16[320,1024]{1,0:T(8,128)(2,1)S(1)}, u32[]{:S(2)}, u32[]{:S(2)}) collective-permute-start(bf16[320,1024]{1,0:T(8,128)(2,1)S(1)} %slice.182), channel_id=1, source_target_pairs={{0,8},{4,12},{8,0},{12,4},{16,24},{20,28},{24,16},{28,20},{1,9},{5... | collective-permute-start | bytes 1966088 | tf_op jit(solution)/shard_map/ppermute | solution.py:21
  35.4 16.0 %collective-permute-start.4 = (bf16[640,1024]{1,0:T(8,128)(2,1)S(1)}, bf16[640,1024]{1,0:T(8,128)(2,1)S(1)}, u32[]{:S(2)}, u32[]{:S(2)}) collective-permute-start(bf16[640,1024]{1,0:T(8,128)(2,1)S(1)} %copy-done.7), channel_id=1, source_target_pairs={{0,4},{4,0},{8,12},{12,8},{16,20},{20,16},{24,28},{28,24},{1,5},{5... | collective-permute-start | bytes 3932168 | tf_op jit(solution)/shard_map/ppermute | solution.py:21
  35.4 16.7 %collective-permute-start.5 = (bf16[640,1024]{1,0:T(8,128)(2,1)S(1)}, bf16[640,1024]{1,0:T(8,128)(2,1)S(1)}, u32[]{:S(2)}, u32[]{:S(2)}) collective-permute-start(bf16[640,1024]{1,0:T(8,128)(2,1)S(1)} %collective-permute-done), channel_id=1, source_target_pairs={{0,4},{4,0},{8,12},{12,8},{16,20},{20,16},{24,28},{28,24},{1,5},{5... | collective-permute-start | bytes 3932168 | tf_op jit(solution)/shard_map/ppermute | solution.py:21
  36.0 16.3 %collective-permute-start.6 = (bf16[640,1024]{1,0:T(8,128)(2,1)S(1)}, bf16[640,1024]{1,0:T(8,128)(2,1)S(1)}, u32[]{:S(2)}, u32[]{:S(2)}) collective-permute-start(bf16[640,1024]{1,0:T(8,128)(2,1)S(1)} %collective-permute-done.1), channel_id=1, source_target_pairs={{0,4},{4,0},{8,12},{12,8},{16,20},{20,16},{24,28},{28,24},{1,5},{5... | collective-permute-start | bytes 3932168 | tf_op jit(solution)/shard_map/ppermute | solution.py:21
  49.4 3.1 collective-permute-start.7
  49.8 25.9 %collective-permute-start.15 = (bf16[512,1024]{1,0:T(8,128)(2,1)}, bf16[512,1024]{1,0:T(8,128)(2,1)}, u32[]{:S(2)}, u32[]{:S(2)}) collective-permute-start(bf16[512,1024]{1,0:T(8,128)(2,1)} %param.9), channel_id=1, source_target_pairs={{0,8},{4,12},{8,0},{12,4},{16,24},{20,28},{24,16},{28,20},{1,9},{5... | collective-permute-start | bytes 3145736 | tf_op jit(solution)/shard_map/ppermute | solution.py:21
  51.5 27.2 %collective-permute-start.17 = (bf16[512,1024]{1,0:T(8,128)(2,1)}, bf16[512,1024]{1,0:T(8,128)(2,1)}, u32[]{:S(2)}, u32[]{:S(2)}) collective-permute-start(bf16[512,1024]{1,0:T(8,128)(2,1)} %param.9), channel_id=1, source_target_pairs={{0,16},{4,20},{8,24},{12,28},{16,0},{20,4},{24,8},{28,12},{1,17},{... | collective-permute-start | bytes 3145736 | tf_op jit(solution)/shard_map/ppermute | solution.py:21
  64.9 31.5 %collective-permute-start.14 = (bf16[512,1024]{1,0:T(8,128)(2,1)}, bf16[512,1024]{1,0:T(8,128)(2,1)S(1)}, u32[]{:S(2)}, u32[]{:S(2)}) collective-permute-start(bf16[512,1024]{1,0:T(8,128)(2,1)} %param.9), channel_id=1, source_target_pairs={{0,4},{4,0},{8,12},{12,8},{16,20},{20,16},{24,28},{28,24},{1,5},{5... | collective-permute-start | bytes 3145736 | tf_op jit(solution)/shard_map/ppermute | solution.py:21
  77.6 13.8 %collective-permute-start.19 = (bf16[256,1024]{1,0:T(8,128)(2,1)}, bf16[256,1024]{1,0:T(8,128)(2,1)}, u32[]{:S(2)}, u32[]{:S(2)}) collective-permute-start(bf16[256,1024]{1,0:T(8,128)(2,1)} %slice.201), channel_id=1, source_target_pairs={{0,16},{4,20},{8,24},{12,28},{16,0},{20,4},{24,8},{28,12},{1,17},{... | collective-permute-start | bytes 1572872 | tf_op jit(solution)/shard_map/ppermute | solution.py:21
  78.7 19.1 %collective-permute-start.16 = (bf16[512,1024]{1,0:T(8,128)(2,1)}, bf16[512,1024]{1,0:T(8,128)(2,1)}, u32[]{:S(2)}, u32[]{:S(2)}) collective-permute-start(bf16[512,1024]{1,0:T(8,128)(2,1)} %collective-permute-done.15), channel_id=1, source_target_pairs={{0,4},{4,0},{8,12},{12,8},{16,20},{20,16},{24,28},{28,24},{1,5},{5... | collective-permute-start | bytes 3145736 | tf_op jit(solution)/shard_map/ppermute | solution.py:21
  80.6 14.7 %collective-permute-start.20 = (bf16[256,1024]{1,0:T(8,128)(2,1)}, bf16[256,1024]{1,0:T(8,128)(2,1)}, u32[]{:S(2)}, u32[]{:S(2)}) collective-permute-start(bf16[256,1024]{1,0:T(8,128)(2,1)} %slice.202), channel_id=1, source_target_pairs={{0,8},{4,12},{8,0},{12,4},{16,24},{20,28},{24,16},{28,20},{1,9},{5... | collective-permute-start | bytes 1572872 | tf_op jit(solution)/shard_map/ppermute | solution.py:21
  81.5 18.9 %collective-permute-start.18 = (bf16[512,1024]{1,0:T(8,128)(2,1)}, bf16[512,1024]{1,0:T(8,128)(2,1)}, u32[]{:S(2)}, u32[]{:S(2)}) collective-permute-start(bf16[512,1024]{1,0:T(8,128)(2,1)} %collective-permute-done.17), channel_id=1, source_target_pairs={{0,4},{4,0},{8,12},{12,8},{16,20},{20,16},{24,28},{28,24},{1,5},{5... | collective-permute-start | bytes 3145736 | tf_op jit(solution)/shard_map/ppermute | solution.py:21
  96.3 9.1 %collective-permute-start.21 = (bf16[512,1024]{1,0:T(8,128)(2,1)S(1)}, bf16[512,1024]{1,0:T(8,128)(2,1)S(1)}, u32[]{:S(2)}, u32[]{:S(2)}) collective-permute-start(bf16[512,1024]{1,0:T(8,128)(2,1)S(1)} %constant_dynamic-update-slice_fusion.15), channel_id=1, source_target_pairs={{0,4},{4,0},{8,12},{12,8},{16,20},{20,16},{24,28},{28,24},{1,5},{5... | collective-permute-start | bytes 3145736 | tf_op jit(solution)/shard_map/ppermute | solution.py:21
  108.1 12.6 %collective-permute-start.23 = (bf16[512,512]{1,0:T(8,128)(2,1)}, bf16[512,512]{1,0:T(8,128)(2,1)}, u32[]{:S(2)}, u32[]{:S(2)}) collective-permute-start(bf16[512,512]{1,0:T(8,128)(2,1)} %get-tuple-element.47), channel_id=1, source_target_pairs={{3,2},{7,6},{11,10},{15,14},{19,18},{23,22},{27,26},{31,30}} | collective-permute-start | bytes 1572872 | tf_op jit(solution)/shard_map/ppermute | solution.py:185
  109.6 16.1 %collective-permute-start.22 = (bf16[512,512]{1,0:T(8,128)(2,1)}, bf16[512,512]{1,0:T(8,128)(2,1)}, u32[]{:S(2)}, u32[]{:S(2)}) collective-permute-start(bf16[512,512]{1,0:T(8,128)(2,1)} %get-tuple-element.46), channel_id=1, source_target_pairs={{0,1},{4,5},{8,9},{12,13},{16,17},{20,21},{24,25},{28,29}} | collective-permute-start | bytes 1572872 | tf_op jit(solution)/shard_map/ppermute | solution.py:184
  113.9 27.5 %collective-permute-start.9 = (bf16[512,1024]{1,0:T(8,128)(2,1)}, bf16[512,1024]{1,0:T(8,128)(2,1)}, u32[]{:S(2)}, u32[]{:S(2)}) collective-permute-start(bf16[512,1024]{1,0:T(8,128)(2,1)} %fusion.43), channel_id=1, source_target_pairs={{3,2},{2,1},{1,0},{7,6},{6,5},{5,4},{11,10},{10,9},{9,8},{15,14},{... | collective-permute-start | bytes 3145736 | tf_op jit(solution)/shard_map/ppermute | solution.py:151
  115.2 33.0 %collective-permute-start.8 = (bf16[512,1024]{1,0:T(8,128)(2,1)}, bf16[512,1024]{1,0:T(8,128)(2,1)}, u32[]{:S(2)}, u32[]{:S(2)}) collective-permute-start(bf16[512,1024]{1,0:T(8,128)(2,1)} %fusion.43), channel_id=1, source_target_pairs={{0,1},{1,2},{2,3},{4,5},{5,6},{6,7},{8,9},{9,10},{10,11},{12,13},{... | collective-permute-start | bytes 3145736 | tf_op jit(solution)/shard_map/ppermute | solution.py:149
  128.6 25.2 %collective-permute-start.25 = (bf16[512,512]{1,0:T(8,128)(2,1)}, bf16[512,512]{1,0:T(8,128)(2,1)}, u32[]{:S(2)}, u32[]{:S(2)}) collective-permute-start(bf16[512,512]{1,0:T(8,128)(2,1)} %get-tuple-element.49), channel_id=1, source_target_pairs={{3,2},{2,1},{7,6},{6,5},{11,10},{10,9},{15,14},{14,13},{19,18},{18... | collective-permute-start | bytes 1572872 | tf_op jit(solution)/shard_map/ppermute | solution.py:185
  130.1 32.6 %collective-permute-start.24 = (bf16[512,512]{1,0:T(8,128)(2,1)}, bf16[512,512]{1,0:T(8,128)(2,1)}, u32[]{:S(2)}, u32[]{:S(2)}) collective-permute-start(bf16[512,512]{1,0:T(8,128)(2,1)} %get-tuple-element.48), channel_id=1, source_target_pairs={{0,1},{1,2},{4,5},{5,6},{8,9},{9,10},{12,13},{13,14},{16,17},{17,1... | collective-permute-start | bytes 1572872 | tf_op jit(solution)/shard_map/ppermute | solution.py:184
  141.3 40.7 %collective-permute-start.10 = (bf16[512,1024]{1,0:T(8,128)(2,1)}, bf16[512,1024]{1,0:T(8,128)(2,1)}, u32[]{:S(2)}, u32[]{:S(2)}) collective-permute-start(bf16[512,1024]{1,0:T(8,128)(2,1)} %collective-permute-done.9), channel_id=1, source_target_pairs={{2,1},{1,0},{6,5},{5,4},{10,9},{9,8},{14,13},{13,12},{18,17},{17,1... | collective-permute-start | bytes 3145736 | tf_op jit(solution)/shard_map/ppermute | solution.py:151
  148.1 36.0 %collective-permute-start.12 = (bf16[512,1024]{1,0:T(8,128)(2,1)}, bf16[512,1024]{1,0:T(8,128)(2,1)}, u32[]{:S(2)}, u32[]{:S(2)}) collective-permute-start(bf16[512,1024]{1,0:T(8,128)(2,1)} %collective-permute-done.8), channel_id=1, source_target_pairs={{1,2},{2,3},{5,6},{6,7},{9,10},{10,11},{13,14},{14,15},{17,18},{18... | collective-permute-start | bytes 3145736 | tf_op jit(solution)/shard_map/ppermute | solution.py:149
  152.3 14.6 %collective-permute-start.28 = (bf16[512,512]{1,0:T(8,128)(2,1)}, bf16[512,512]{1,0:T(8,128)(2,1)}, u32[]{:S(2)}, u32[]{:S(2)}) collective-permute-start(bf16[512,512]{1,0:T(8,128)(2,1)} %get-tuple-element.55), channel_id=1, source_target_pairs={{3,2},{7,6},{11,10},{15,14},{19,18},{23,22},{27,26},{31,30}} | collective-permute-start | bytes 1572872 | tf_op jit(solution)/shard_map/ppermute | solution.py:185
  153.8 18.5 %collective-permute-start.27 = (bf16[512,512]{1,0:T(8,128)(2,1)}, bf16[512,512]{1,0:T(8,128)(2,1)}, u32[]{:S(2)}, u32[]{:S(2)}) collective-permute-start(bf16[512,512]{1,0:T(8,128)(2,1)} %get-tuple-element.54), channel_id=1, source_target_pairs={{0,1},{4,5},{8,9},{12,13},{16,17},{20,21},{24,25},{28,29}} | collective-permute-start | bytes 1572872 | tf_op jit(solution)/shard_map/ppermute | solution.py:184
  165.6 20.7 %collective-permute-start.31 = (bf16[512,512]{1,0:T(8,128)(2,1)}, bf16[512,512]{1,0:T(8,128)(2,1)}, u32[]{:S(2)}, u32[]{:S(2)}) collective-permute-start(bf16[512,512]{1,0:T(8,128)(2,1)} %get-tuple-element.59), channel_id=1, source_target_pairs={{3,2},{2,1},{1,0},{7,6},{6,5},{5,4},{11,10},{10,9},{9,8},{15,14},{... | collective-permute-start | bytes 1572872 | tf_op jit(solution)/shard_map/ppermute | solution.py:185
  175.3 17.0 %collective-permute-start.29 = (bf16[512,512]{1,0:T(8,128)(2,1)}, bf16[512,512]{1,0:T(8,128)(2,1)}, u32[]{:S(2)}, u32[]{:S(2)}) collective-permute-start(bf16[512,512]{1,0:T(8,128)(2,1)} %get-tuple-element.56), channel_id=1, source_target_pairs={{0,1},{1,2},{4,5},{5,6},{8,9},{9,10},{12,13},{13,14},{16,17},{17,1... | collective-permute-start | bytes 1572872 | tf_op jit(solution)/shard_map/ppermute | solution.py:184
  180.5 11.8 %collective-permute-start.30 = (bf16[512,512]{1,0:T(8,128)(2,1)}, bf16[512,512]{1,0:T(8,128)(2,1)}, u32[]{:S(2)}, u32[]{:S(2)}) collective-permute-start(bf16[512,512]{1,0:T(8,128)(2,1)} %get-tuple-element.57), channel_id=1, source_target_pairs={{3,2},{2,1},{7,6},{6,5},{11,10},{10,9},{15,14},{14,13},{19,18},{18... | collective-permute-start | bytes 1572872 | tf_op jit(solution)/shard_map/ppermute | solution.py:185
  182.0 18.6 %collective-permute-start.26 = (bf16[512,512]{1,0:T(8,128)(2,1)}, bf16[512,512]{1,0:T(8,128)(2,1)}, u32[]{:S(2)}, u32[]{:S(2)}) collective-permute-start(bf16[512,512]{1,0:T(8,128)(2,1)} %get-tuple-element.50), channel_id=1, source_target_pairs={{0,1},{1,2},{2,3},{4,5},{5,6},{6,7},{8,9},{9,10},{10,11},{12,13},{... | collective-permute-start | bytes 1572872 | tf_op jit(solution)/shard_map/ppermute | solution.py:184
  184.1 16.5 %copy-start.5 = (bf16[512,3072]{1,0:T(8,128)(2,1)S(1)}, bf16[512,3072]{1,0:T(8,128)(2,1)}, u32[]{:S(2)}) copy-start(bf16[512,3072]{1,0:T(8,128)(2,1)} %copy-done.4) | copy-start | bytes 9437188
  184.1 28.4 %collective-permute-start.11 = (bf16[512,1024]{1,0:T(8,128)(2,1)}, bf16[512,1024]{1,0:T(8,128)(2,1)S(1)}, u32[]{:S(2)}, u32[]{:S(2)}) collective-permute-start(bf16[512,1024]{1,0:T(8,128)(2,1)} %collective-permute-done.10), channel_id=1, source_target_pairs={{1,0},{5,4},{9,8},{13,12},{17,16},{21,20},{25,24},{29,28}} | collective-permute-start | bytes 3145736 | tf_op jit(solution)/shard_map/ppermute | solution.py:151
  186.3 31.5 %collective-permute-start.13 = (bf16[512,1024]{1,0:T(8,128)(2,1)}, bf16[512,1024]{1,0:T(8,128)(2,1)S(1)}, u32[]{:S(2)}, u32[]{:S(2)}) collective-permute-start(bf16[512,1024]{1,0:T(8,128)(2,1)} %collective-permute-done.12), channel_id=1, source_target_pairs={{2,3},{6,7},{10,11},{14,15},{18,19},{22,23},{26,27},{30,31}} | collective-permute-start | bytes 3145736 | tf_op jit(solution)/shard_map/ppermute | solution.py:149
  202.4 29.4 %collective-permute-start.38 = (bf16[512,512]{1,0:T(8,128)(2,1)S(1)}, bf16[512,512]{1,0:T(8,128)(2,1)S(1)}, u32[]{:S(2)}, u32[]{:S(2)}) collective-permute-start(bf16[512,512]{1,0:T(8,128)(2,1)S(1)} %get-tuple-element.67), channel_id=1, source_target_pairs={{3,2},{2,1},{1,0},{7,6},{6,5},{5,4},{11,10},{10,9},{9,8},{15,14},{... | collective-permute-start | bytes 1572872 | tf_op jit(solution)/shard_map/ppermute | solution.py:185
  203.7 28.1 %collective-permute-start.37 = (bf16[512,512]{1,0:T(8,128)(2,1)S(1)}, bf16[512,512]{1,0:T(8,128)(2,1)}, u32[]{:S(2)}, u32[]{:S(2)}) collective-permute-start(bf16[512,512]{1,0:T(8,128)(2,1)S(1)} %get-tuple-element.66), channel_id=1, source_target_pairs={{0,1},{1,2},{2,3},{4,5},{5,6},{6,7},{8,9},{9,10},{10,11},{12,13},{... | collective-permute-start | bytes 1572872 | tf_op jit(solution)/shard_map/ppermute | solution.py:184
  209.5 13.6 %slice-start.6 = ((s8[6291456]{0:T(1024)(128)(4,1)}), s8[4194304]{0:T(1024)(128)(4,1)S(1)}, s32[]{:S(2)}) async-start(s8[6291456]{0:T(1024)(128)(4,1)} %bitcast.86), calls=%async_computation.6 | async-start | bytes 8388608
  213.7 6.7 %copy-start.15 = (bf16[512,1024]{1,0:T(8,128)(2,1)S(1)}, bf16[512,1024]{1,0:T(8,128)(2,1)}, u32[]{:S(2)}) copy-start(bf16[512,1024]{1,0:T(8,128)(2,1)} %copy-done.14) | copy-start | bytes 3145732
  220.4 7.0 %slice-start = ((s8[10485760]{0:T(1024)(128)(4,1)}), s8[4194304]{0:T(1024)(128)(4,1)S(1)}, s32[]{:S(2)}) async-start(s8[10485760]{0:T(1024)(128)(4,1)} %bitcast.82), calls=%async_computation | async-start | bytes 8388608
  223.1 4.3 %slice-start.1 = ((s8[10485760]{0:T(1024)(128)(4,1)}), s8[4194304]{0:T(1024)(128)(4,1)S(1)}, s32[]{:S(2)}) async-start(s8[10485760]{0:T(1024)(128)(4,1)} %bitcast.82), calls=%async_computation.1 | async-start | bytes 8388608
  231.7 14.1 %collective-permute-start.32 = (bf16[2560,512]{1,0:T(8,128)(2,1)}, bf16[2560,512]{1,0:T(8,128)(2,1)}, u32[]{:S(2)}, u32[]{:S(2)}) collective-permute-start(bf16[2560,512]{1,0:T(8,128)(2,1)} %fusion.8), channel_id=1, source_target_pairs={{0,4},{4,0},{8,12},{12,8},{16,20},{20,16},{24,28},{28,24},{1,5},{5... | collective-permute-start | bytes 7864328 | tf_op jit(solution)/shard_map/ppermute | solution.py:21
  231.7 8.0 %slice-start.3 = ((s8[10485760]{0:T(1024)(128)(4,1)}), s8[4194304]{0:T(1024)(128)(4,1)S(1)}, s32[]{:S(2)}) async-start(s8[10485760]{0:T(1024)(128)(4,1)} %bitcast.84), calls=%async_computation.3 | async-start | bytes 8388608
  233.5 6.3 %slice-start.4 = ((s8[10485760]{0:T(1024)(128)(4,1)}), s8[4194304]{0:T(1024)(128)(4,1)S(1)}, s32[]{:S(2)}) async-start(s8[10485760]{0:T(1024)(128)(4,1)} %bitcast.84), calls=%async_computation.4 | async-start | bytes 8388608
  233.5 6.3 %slice-start.5 = ((s8[10485760]{0:T(1024)(128)(4,1)}), s8[2097152]{0:T(1024)(128)(4,1)S(1)}, s32[]{:S(2)}) async-start(s8[10485760]{0:T(1024)(128)(4,1)} %bitcast.84), calls=%async_computation.5 | async-start | bytes 4194304
  233.5 6.3 %copy-start.11 = (bf16[512,512]{1,0:T(8,128)(2,1)S(1)}, bf16[512,512]{1,0:T(8,128)(2,1)}, u32[]{:S(2)}) copy-start(bf16[512,512]{1,0:T(8,128)(2,1)} %copy-done.10) | copy-start | bytes 1572868
  239.2 12.3 %collective-permute-start.39 = (bf16[2560,512]{1,0:T(8,128)(2,1)S(1)}, bf16[2560,512]{1,0:T(8,128)(2,1)S(1)}, u32[]{:S(2)}, u32[]{:S(2)}) collective-permute-start(bf16[2560,512]{1,0:T(8,128)(2,1)S(1)} %fusion.11), channel_id=1, source_target_pairs={{0,4},{4,0},{8,12},{12,8},{16,20},{20,16},{24,28},{28,24},{1,5},{5... | collective-permute-start | bytes 7864328 | tf_op jit(solution)/shard_map/ppermute | solution.py:21
  248.9 17.7 %collective-permute-start.33 = (bf16[2,640,256]{2,1,0:T(8,128)(2,1)S(1)}, bf16[2,640,256]{2,1,0:T(8,128)(2,1)S(1)}, u32[]{:S(2)}, u32[]{:S(2)}) collective-permute-start(bf16[2,640,256]{2,1,0:T(8,128)(2,1)S(1)} %pad_maximum_fusion.3), channel_id=1, source_target_pairs={{0,8},{4,12},{8,0},{12,4},{16,24},{20,28},{24,16},{28,20},{1,9},{5... | collective-permute-start | bytes 1966088 | tf_op jit(solution)/shard_map/ppermute | solution.py:21
  249.9 17.7 %collective-permute-start.34 = (bf16[2,640,256]{2,1,0:T(8,128)(2,1)S(1)}, bf16[2,640,256]{2,1,0:T(8,128)(2,1)S(1)}, u32[]{:S(2)}, u32[]{:S(2)}) collective-permute-start(bf16[2,640,256]{2,1,0:T(8,128)(2,1)S(1)} %pad_maximum_fusion.4), channel_id=1, source_target_pairs={{0,16},{4,20},{8,24},{12,28},{16,0},{20,4},{24,8},{28,12},{1,17},{... | collective-permute-start | bytes 1966088 | tf_op jit(solution)/shard_map/ppermute | solution.py:21
  252.5 29.3 %copy-start.6 = (bf16[2560,512]{1,0:T(8,128)(2,1)}, bf16[2560,512]{1,0:T(8,128)(2,1)S(1)}, u32[]{:S(2)}) copy-start(bf16[2560,512]{1,0:T(8,128)(2,1)S(1)} %add_convert_fusion) | copy-start | bytes 7864324
  252.7 27.9 %collective-permute-start.40 = (bf16[2,640,256]{2,1,0:T(8,128)(2,1)S(1)}, bf16[2,640,256]{2,1,0:T(8,128)(2,1)S(1)}, u32[]{:S(2)}, u32[]{:S(2)}) collective-permute-start(bf16[2,640,256]{2,1,0:T(8,128)(2,1)S(1)} %pad_maximum_fusion.5), channel_id=1, source_target_pairs={{0,8},{4,12},{8,0},{12,4},{16,24},{20,28},{24,16},{28,20},{1,9},{5... | collective-permute-start | bytes 1966088 | tf_op jit(solution)/shard_map/ppermute | solution.py:21
  253.4 28.3 %collective-permute-start.41 = (bf16[2,640,256]{2,1,0:T(8,128)(2,1)S(1)}, bf16[2,640,256]{2,1,0:T(8,128)(2,1)S(1)}, u32[]{:S(2)}, u32[]{:S(2)}) collective-permute-start(bf16[2,640,256]{2,1,0:T(8,128)(2,1)S(1)} %pad_maximum_fusion.6), channel_id=1, source_target_pairs={{0,16},{4,20},{8,24},{12,28},{16,0},{20,4},{24,8},{28,12},{1,17},{... | collective-permute-start | bytes 1966088 | tf_op jit(solution)/shard_map/ppermute | solution.py:21
  267.8 20.9 %collective-permute-start.35 = (bf16[1,640,256]{2,1,0:T(8,128)(2,1)S(1)}, bf16[1,640,256]{2,1,0:T(8,128)(2,1)S(1)}, u32[]{:S(2)}, u32[]{:S(2)}) collective-permute-start(bf16[1,640,256]{2,1,0:T(8,128)(2,1)S(1)} %get-tuple-element.104), channel_id=1, source_target_pairs={{0,16},{4,20},{8,24},{12,28},{16,0},{20,4},{24,8},{28,12},{1,17},{... | collective-permute-start | bytes 983048 | tf_op jit(solution)/shard_map/ppermute | solution.py:21
  269.4 19.3 %collective-permute-start.36 = (bf16[1,640,256]{2,1,0:T(8,128)(2,1)S(1)}, bf16[1,640,256]{2,1,0:T(8,128)(2,1)S(1)}, u32[]{:S(2)}, u32[]{:S(2)}) collective-permute-start(bf16[1,640,256]{2,1,0:T(8,128)(2,1)S(1)} %get-tuple-element.103), channel_id=1, source_target_pairs={{0,8},{4,12},{8,0},{12,4},{16,24},{20,28},{24,16},{28,20},{1,9},{5... | collective-permute-start | bytes 983048 | tf_op jit(solution)/shard_map/ppermute | solution.py:21
  281.7 8.0 %copy-start.8 = (bf16[2,640,256]{2,1,0:T(8,128)(2,1)}, bf16[2,640,256]{2,1,0:T(8,128)(2,1)S(1)}, u32[]{:S(2)}) copy-start(bf16[2,640,256]{2,1,0:T(8,128)(2,1)S(1)} %collective-permute-done.41) | copy-start | bytes 1966084
  281.9 12.6 %collective-permute-start.42 = (bf16[1,640,256]{2,1,0:T(8,128)(2,1)S(1)}, bf16[1,640,256]{2,1,0:T(8,128)(2,1)S(1)}, u32[]{:S(2)}, u32[]{:S(2)}) collective-permute-start(bf16[1,640,256]{2,1,0:T(8,128)(2,1)S(1)} %get-tuple-element.96), channel_id=1, source_target_pairs={{0,16},{4,20},{8,24},{12,28},{16,0},{20,4},{24,8},{28,12},{1,17},{... | collective-permute-start | bytes 983048 | tf_op jit(solution)/shard_map/ppermute | solution.py:21
  283.4 11.8 %collective-permute-start.43 = (bf16[1,640,256]{2,1,0:T(8,128)(2,1)S(1)}, bf16[1,640,256]{2,1,0:T(8,128)(2,1)}, u32[]{:S(2)}, u32[]{:S(2)}) collective-permute-start(bf16[1,640,256]{2,1,0:T(8,128)(2,1)S(1)} %get-tuple-element.95), channel_id=1, source_target_pairs={{0,8},{4,12},{8,0},{12,4},{16,24},{20,28},{24,16},{28,20},{1,9},{5... | collective-permute-start | bytes 983048 | tf_op jit(solution)/shard_map/ppermute | solution.py:21
  298.9 1.2 collective-permute-start.44
  300.1 4.5 %collective-permute-start.47 = (f32[8,128]{1,0:T(8,128)S(1)}, f32[8,128]{1,0:T(8,128)S(1)}, u32[]{:S(2)}, u32[]{:S(2)}) collective-permute-start(f32[8,128]{1,0:T(8,128)S(1)} %broadcast_add_fusion), channel_id=1, source_target_pairs={{0,24},{4,28},{8,16},{12,20},{16,8},{20,12},{24,0},{28,4},{1,25},{... | collective-permute-start | bytes 12296 | tf_op jit(solution)/shard_map/ppermute | solution.py:21
  301.6 3.6 %collective-permute-start.45 = (f32[8,128]{1,0:T(8,128)S(1)}, f32[8,128]{1,0:T(8,128)S(1)}, u32[]{:S(2)}, u32[]{:S(2)}) collective-permute-start(f32[8,128]{1,0:T(8,128)S(1)} %broadcast_add_fusion), channel_id=1, source_target_pairs={{0,8},{4,12},{8,0},{12,4},{16,24},{20,28},{24,16},{28,20},{1,9},{5... | collective-permute-start | bytes 12296 | tf_op jit(solution)/shard_map/ppermute | solution.py:21
  303.1 3.6 %collective-permute-start.46 = (f32[8,128]{1,0:T(8,128)S(1)}, f32[8,128]{1,0:T(8,128)S(1)}, u32[]{:S(2)}, u32[]{:S(2)}) collective-permute-start(f32[8,128]{1,0:T(8,128)S(1)} %broadcast_add_fusion), channel_id=1, source_target_pairs={{0,16},{4,20},{8,24},{12,28},{16,0},{20,4},{24,8},{28,12},{1,17},{... | collective-permute-start | bytes 12296 | tf_op jit(solution)/shard_map/ppermute | solution.py:21
  306.7 5.5 %collective-permute-start.50 = (f32[8,128]{1,0:T(8,128)S(1)}, f32[8,128]{1,0:T(8,128)S(1)}, u32[]{:S(2)}, u32[]{:S(2)}) collective-permute-start(f32[8,128]{1,0:T(8,128)S(1)} %add_add_fusion.1), channel_id=1, source_target_pairs={{0,3},{1,0},{2,1},{3,2},{4,7},{5,4},{6,5},{7,6},{8,11},{9,8},{10,9... | collective-permute-start | bytes 12296 | tf_op jit(solution)/shard_map/ppermute | solution.py:226
  310.9 5.4 %collective-permute-start.48 = (f32[8,128]{1,0:T(8,128)S(1)}, f32[8,128]{1,0:T(8,128)S(1)}, u32[]{:S(2)}, u32[]{:S(2)}) collective-permute-start(f32[8,128]{1,0:T(8,128)S(1)} %add_add_fusion.1), channel_id=1, source_target_pairs={{0,1},{1,2},{2,3},{3,0},{4,5},{5,6},{6,7},{7,4},{8,9},{9,10},{10,1... | collective-permute-start | bytes 12296 | tf_op jit(solution)/shard_map/ppermute | solution.py:226
  310.9 5.4 %collective-permute-start.49 = (f32[8,128]{1,0:T(8,128)S(1)}, f32[8,128]{1,0:T(8,128)S(1)}, u32[]{:S(2)}, u32[]{:S(2)}) collective-permute-start(f32[8,128]{1,0:T(8,128)S(1)} %add_add_fusion.1), channel_id=1, source_target_pairs={{0,2},{1,3},{2,0},{3,1},{4,6},{5,7},{6,4},{7,5},{8,10},{9,11},{10,... | collective-permute-start | bytes 12296 | tf_op jit(solution)/shard_map/ppermute | solution.py:226
  (11 other events, 31.8 us)

commit v2 on v1

--- a/solution.py
+++ b/solution.py
@@ -135,9 +135,15 @@
 
     r, _ = gather_far(r, n_fsdp, bits, forward)
 
-    r_near = jnp.concatenate([r[m] for m in range(close)], axis=0)
-    r_far = jnp.concatenate([r[close], r[close + 1]], axis=0)
-    product_near = dot(forward, r_near, (1, 1)).astype(BF)
+    assert chunks == 2
+    odd = me % 2
+    r_all = jnp.zeros((total_p, width), BF)
+    for m in range(close):
+        r_all = lax.dynamic_update_slice_in_dim(r_all, r[m], (m ^ odd) * depth, axis=0)
+    product_near = dot(forward, r_all[: close * depth], (1, 1)).astype(BF)
+    for m in range(close, n_fsdp):
+        block = after(r[m], product_near)
+        r_all = lax.dynamic_update_slice_in_dim(r_all, block, (m ^ odd) * depth, axis=0)
     product_far = [dot(forward, r[close + i], (1, 1)).astype(BF) for i in range(2)]
 
     def place(c, owner):
@@ -149,21 +155,18 @@
         from_low.append(lax.ppermute(from_low[-1], "tp", pairs))
         pairs = [(last - i, last - 1 - i) for i in range(hop, last)]
         from_high.append(lax.ppermute(from_high[-1], "tp", pairs))
-    back_all = jnp.zeros((tokens, total_p), BF)
-    for hop in range(n_tp):
+    delta = None
+    for hop in sorted(range(n_tp), key=lambda hop: max(hop, n_tp - hop) if hop else 0):
+        piece = from_low[hop] + from_high[n_tp - hop] if hop else back
         owner = lax.rem(at - hop + n_tp, n_tp)
-        for c in range(chunks):
-            span = slice(c * depth, (c + 1) * depth)
-            part = from_low[hop][:, span]
-            if hop:
-                part = part + from_high[n_tp - hop][:, span]
-            back_all = lax.dynamic_update_slice_in_dim(back_all, part, place(c, owner) * depth, axis=1)
-    delta = dot(back_all[:, : close * depth], r_near, (1, 0))
-    delta = (delta + dot(back_all[:, close * depth :], r_far, (1, 0))).astype(BF)
+        block = lax.dynamic_slice_in_dim(r_all, (me // 2 ^ owner) * width, width, axis=0)
+        part = dot(piece, block, (1, 0))
+        delta = part if delta is None else delta + part
+    delta = delta.astype(BF)
 
     def partial(products, c, owner):
         block = place(c, owner)
-        start = jnp.minimum(block, close - 1) * depth
+        start = (jnp.minimum(block, close - 1) ^ odd) * depth
         near = lax.dynamic_slice_in_dim(products[0], start, depth, axis=1)
         far = jnp.where(block == close, *products[1:])
         return jnp.where(block < close, near, far).astype(F32)
@@ -198,8 +201,8 @@
 
         send = dot(both[:, split:], values, (0, 0)).astype(BF)
         arrived = flip(send, "fsdp", n_fsdp, 1)
-        keep = after(dot(both[:, :split], values, (0, 0)), values)
-        pair = (keep + arrived.astype(F32)).astype(BF)
+        keep = after(dot(both[:, :split], values, (0, 0)).astype(BF), values)
+        pair = (keep.astype(F32) + arrived.astype(F32)).astype(BF)
         blocks = {m: pair[i * rows : (i + 1) * rows] for i, m in enumerate(keeps)}
         half = depth // 2
         halves = [

time: 319 us -> 301 us (0.944)
  other arithmetic: 32.4 us -> 13.3 us
  matrix products: 39.6 us -> 43.1 us
  starting transfers between devices: 82.4 us -> 78.9 us
    ppermute x6, waiting for transfers between devices: 24 us -> 3.62 us  [per_device(): up = lax.ppermute(send_up, 'tp', [(i, i + 1) for i in range(hop)])]
    ppermute x6, waiting for transfers between devices: 0.02 us -> 17.2 us  [per_device(): lax.ppermute(send_down, 'tp', [(last - i, last - 1 - i) for i in range(ho...]
    ppermute x3, waiting for transfers between devices: 7.29 us -> 16.9 us  [per_device(): from_high.append(lax.ppermute(from_high[-1], 'tp', pairs))]
    dynamic_update_slice x6 -> x0, other arithmetic: 7.87 us -> none  [per_device(): lax.dynamic_update_slice_in_dim(back_all, part, place(c, owner) * depth,...]
    dynamic_update_slice x2 -> x8, local copies, waits for them, and re-layouts: 0.1 us -> 7.77 us  [the longest x6 5.68 us: per_device(): lax.dynamic_update_slice_in_dim(r_all, r[m], (m ^ odd) * depth, axis=0)]
    convert_element_type x4, other arithmetic: 10.6 us -> 3.44 us  [per_device(): send_up, send_down = (send_up.astype(BF), send_down.astype(BF))]
    ppermute x3, waiting for transfers between devices: 5.51 us -> 0.01 us  [per_device(): from_low.append(lax.ppermute(from_low[-1], 'tp', pairs))]
    unnamed x62 -> x63, local copies, waits for them, and re-layouts: 13.4 us -> 9.57 us
  transfers between devices with their start and end apart: 51 -> 51, of which waited for: 26 -> 22; matrix products, arithmetic and copies ran while one was open for 26% -> 24% of each run, Pallas kernels for 1% -> 1%
where the time goes in v2:
time: 301 us; the launch traced here: 300 us
  waiting for transfers between devices  132 us (44%)
  starting transfers between devices  78.9 us (26%)
  matrix products  43.1 us (14%)
  local copies, waits for them, and re-layouts  23.9 us (8%)
  other arithmetic  13.3 us (4%)
  Pallas kernels  5.27 us (2%)
  between operations  3.6 us (1%)
    ppermute x30, waiting for transfers between devices, flip(): return lax.ppermute(value, axis, [(i, i ^ bit) for i in range(size)])  89.8 us
    dot_general x12, matrix products, dot(): lax.dot_general(left, right, ((dims[:1], dims[1:]), ((), ())), preferred_...  43.1 us
    ppermute x6, starting transfers between devices, per_device(): up = lax.ppermute(send_up, 'tp', [(i, i + 1) for i in range(hop)])  33.3 us
    ppermute x30, starting transfers between devices, flip(): return lax.ppermute(value, axis, [(i, i ^ bit) for i in range(size)])  22.8 us
    ppermute x6, waiting for transfers between devices, per_device(): lax.ppermute(send_down, 'tp', [(last - i, last - 1 - i) for i in range(ho...  17.2 us
    ppermute x3, waiting for transfers between devices, per_device(): from_high.append(lax.ppermute(from_high[-1], 'tp', pairs))  16.9 us
    unnamed x63, local copies, waits for them, and re-layouts  9.57 us
    ppermute x3, starting transfers between devices, per_device(): lax.ppermute(total, 'tp', [(i, (i + k) % n_tp) for i in range(n_tp)])  6.86 us
  transfers between devices with their start and end apart: 51, of which 22 were waited for; matrix products, arithmetic and copies ran while one was open for 24% of the time, Pallas kernels for 1%

profile of v2, /device:TPU:0, one launch (start us, length us, event | category | flops | bytes accessed | tf_op | source)
XLA Modules:
  0.0 300.4 jit_solution(15807903114752959103)
XLA Ops:
  0.0 3.0 collective-permute-start
  3.0 1.5 collective-permute-start.1
  4.6 2.5 copy-done.1
  7.1 2.5 copy-done.2
  10.2 4.0 %shard_map.55 = bf16[1024,5120]{1,0:T(8,128)(2,1)S(1)} custom-call(s32[8]{0:T(128)S(1)} %stack.83.places, s32[2]{0:T(128)S(1)} %copy-done.3, bf16[512,5120]{1,0:T(8,128)(2,1)S(1)} %copy-done.1, bf16[512,5120]{1,0:T(8,128)(2,1)S(1)} %copy-done.2), custom_call_target="tpu_custom_call" | custom-call | bytes 20971520 | tf_op jit(solution)/shard_map/pallas_call | solution.py:74
  14.2 17.8 %collective-permute-done = bf16[640,1024]{1,0:T(8,128)(2,1)} collective-permute-done((bf16[640,1024]{1,0:T(8,128)(2,1)}, bf16[640,1024]{1,0:T(8,128)(2,1)}, u32[]{:S(2)}, u32[]{:S(2)}) %collective-permute-start) | collective-permute-done | bytes 1310752 | tf_op jit(solution)/shard_map/ppermute | solution.py:21
  33.2 1.8 collective-permute-start.2
  35.1 1.6 collective-permute-start.3
  37.2 12.0 %collective-permute-done.2 = bf16[320,1024]{1,0:T(8,128)(2,1)S(1)} collective-permute-done((bf16[320,1024]{1,0:T(8,128)(2,1)S(1)}, bf16[320,1024]{1,0:T(8,128)(2,1)S(1)}, u32[]{:S(2)}, u32[]{:S(2)}) %collective-permute-start.2) | collective-permute-done | bytes 655392 | tf_op jit(solution)/shard_map/ppermute | solution.py:21
  49.2 1.3 collective-permute-done.3
  50.8 1.4 constant_dynamic-update-slice_fusion.7
  52.3 1.6 collective-permute-start.9
  55.0 11.2 %convolution_convert_fusion = bf16[1024,1024]{1,0:T(8,128)(2,1)S(1)} fusion(bf16[1024,5120]{1,0:T(8,128)(2,1)S(1)} %shard_map.55, bf16[5120,1024]{1,0:T(8,128)(2,1)S(1)} %constant_dynamic-update-slice_fusion), kind=kOutput, calls=%fused_computation.26 | convolution fusion | flops 10738466816 | bytes 23068672 | tf_op jit(solution)/shard_map/dot_general | solution.py:17
  66.2 1.2 fusion.56
  67.3 10.8 %collective-permute-done.9 = bf16[512,1024]{1,0:T(8,128)(2,1)S(1)} collective-permute-done((bf16[512,1024]{1,0:T(8,128)(2,1)}, bf16[512,1024]{1,0:T(8,128)(2,1)S(1)}, u32[]{:S(2)}, u32[]{:S(2)}) %collective-permute-start.9) | collective-permute-done | bytes 1048608 | tf_op jit(solution)/shard_map/ppermute | solution.py:21
  82.3 1.3 constant_dynamic-update-slice_fusion.18
  83.7 8.0 %collective-permute-done.13 = bf16[256,1024]{1,0:T(8,128)(2,1)S(1)} collective-permute-done((bf16[256,1024]{1,0:T(8,128)(2,1)S(1)}, bf16[256,1024]{1,0:T(8,128)(2,1)S(1)}, u32[]{:S(2)}, u32[]{:S(2)}) %collective-permute-start.13) | collective-permute-done | bytes 524320 | tf_op jit(solution)/shard_map/ppermute | solution.py:21
  92.5 4.5 %collective-permute-start.16 = (bf16[512,1024]{1,0:T(8,128)(2,1)}, bf16[512,1024]{1,0:T(8,128)(2,1)}, u32[]{:S(2)}, u32[]{:S(2)}) collective-permute-start(bf16[512,1024]{1,0:T(8,128)(2,1)} %fusion.56), channel_id=1, source_target_pairs={{0,1},{1,2},{2,3},{4,5},{5,6},{6,7},{8,9},{9,10},{10,11},{12,13},{... | collective-permute-start | bytes 3145736 | tf_op jit(solution)/shard_map/ppermute | solution.py:155
  98.1 1.3 collective-permute-start.18
  100.6 1.3 constant_dynamic-update-slice_fusion.17
  102.1 1.5 constant_dynamic-update-slice_fusion.15
  103.6 1.3 constant_dynamic-update-slice_fusion.13
  105.0 3.7 %fusion.22 = bf16[512,3072]{1,0:T(8,128)(2,1)S(1)} fusion(bf16[4096,1024]{1,0:T(8,128)(2,1)S(1)} %constant_dynamic-update-slice_fusion.13, bf16[1024,1024]{1,0:T(8,128)(2,1)S(1)} %copy-done.15), kind=kOutput, calls=%fused_computation.16 | convolution fusion | flops 3222798336 | bytes 10485760 | tf_op jit(solution)/shard_map/dot_general | solution.py:17
  109.5 2.0 select_select_fusion.2
  112.4 4.6 %collective-permute-start.22 = (bf16[512,512]{1,0:T(8,128)(2,1)}, bf16[512,512]{1,0:T(8,128)(2,1)S(1)}, u32[]{:S(2)}, u32[]{:S(2)}) collective-permute-start(bf16[512,512]{1,0:T(8,128)(2,1)} %get-tuple-element.50), channel_id=1, source_target_pairs={{0,1},{4,5},{8,9},{12,13},{16,17},{20,21},{24,25},{28,29}} | collective-permute-start | bytes 1572872 | tf_op jit(solution)/shard_map/ppermute | solution.py:187
  116.9 7.0 %collective-permute-done.18 = bf16[512,1024]{1,0:T(8,128)(2,1)} collective-permute-done((bf16[512,1024]{1,0:T(8,128)(2,1)}, bf16[512,1024]{1,0:T(8,128)(2,1)}, u32[]{:S(2)}, u32[]{:S(2)}) %collective-permute-start.18) | collective-permute-done | bytes 1048608 | tf_op jit(solution)/shard_map/ppermute | solution.py:157
  124.0 1.3 collective-permute-start.19
  126.4 2.6 collective-permute-done.22
  129.0 1.7 add_convert_fusion.11
  131.5 6.5 %collective-permute-start.24 = (bf16[512,512]{1,0:T(8,128)(2,1)S(1)}, bf16[512,512]{1,0:T(8,128)(2,1)S(1)}, u32[]{:S(2)}, u32[]{:S(2)}) collective-permute-start(bf16[512,512]{1,0:T(8,128)(2,1)S(1)} %get-tuple-element.52), channel_id=1, source_target_pairs={{0,1},{1,2},{4,5},{5,6},{8,9},{9,10},{12,13},{13,14},{16,17},{17,1... | collective-permute-start | bytes 1572872 | tf_op jit(solution)/shard_map/ppermute | solution.py:187
  139.1 9.9 %collective-permute-done.19 = bf16[512,1024]{1,0:T(8,128)(2,1)} collective-permute-done((bf16[512,1024]{1,0:T(8,128)(2,1)}, bf16[512,1024]{1,0:T(8,128)(2,1)}, u32[]{:S(2)}, u32[]{:S(2)}) %collective-permute-start.19) | collective-permute-done | bytes 1048608 | tf_op jit(solution)/shard_map/ppermute | solution.py:157
  149.0 7.0 %collective-permute-start.27 = (bf16[512,512]{1,0:T(8,128)(2,1)S(1)}, bf16[512,512]{1,0:T(8,128)(2,1)S(1)}, u32[]{:S(2)}, u32[]{:S(2)}) collective-permute-start(bf16[512,512]{1,0:T(8,128)(2,1)S(1)} %get-tuple-element.58), channel_id=1, source_target_pairs={{0,1},{4,5},{8,9},{12,13},{16,17},{20,21},{24,25},{28,29}} | collective-permute-start | bytes 1572872 | tf_op jit(solution)/shard_map/ppermute | solution.py:187
  158.1 1.5 collective-permute-start.20
  160.2 1.4 collective-permute-start.31
  163.2 4.9 %collective-permute-start.29 = (bf16[512,512]{1,0:T(8,128)(2,1)S(1)}, bf16[512,512]{1,0:T(8,128)(2,1)S(1)}, u32[]{:S(2)}, u32[]{:S(2)}) collective-permute-start(bf16[512,512]{1,0:T(8,128)(2,1)S(1)} %get-tuple-element.60), channel_id=1, source_target_pairs={{0,1},{1,2},{4,5},{5,6},{8,9},{9,10},{12,13},{13,14},{16,17},{17,1... | collective-permute-start | bytes 1572872 | tf_op jit(solution)/shard_map/ppermute | solution.py:187
  168.8 5.0 %collective-permute-start.26 = (bf16[512,512]{1,0:T(8,128)(2,1)S(1)}, bf16[512,512]{1,0:T(8,128)(2,1)S(1)}, u32[]{:S(2)}, u32[]{:S(2)}) collective-permute-start(bf16[512,512]{1,0:T(8,128)(2,1)S(1)} %get-tuple-element.54), channel_id=1, source_target_pairs={{0,1},{1,2},{2,3},{4,5},{5,6},{6,7},{8,9},{9,10},{10,11},{12,13},{... | collective-permute-start | bytes 1572872 | tf_op jit(solution)/shard_map/ppermute | solution.py:187
  173.8 1.3 fusion.31
  175.1 17.2 %collective-permute-done.31 = bf16[512,512]{1,0:T(8,128)(2,1)S(1)} collective-permute-done((bf16[512,512]{1,0:T(8,128)(2,1)S(1)}, bf16[512,512]{1,0:T(8,128)(2,1)S(1)}, u32[]{:S(2)}, u32[]{:S(2)}) %collective-permute-start.31) | collective-permute-done | bytes 524320 | tf_op jit(solution)/shard_map/ppermute | solution.py:188
  193.0 2.5 fusion.29
  196.1 1.3 collective-permute-start.38
  197.4 5.4 %collective-permute-start.37 = (bf16[512,512]{1,0:T(8,128)(2,1)S(1)}, bf16[512,512]{1,0:T(8,128)(2,1)}, u32[]{:S(2)}, u32[]{:S(2)}) collective-permute-start(bf16[512,512]{1,0:T(8,128)(2,1)S(1)} %get-tuple-element.70), channel_id=1, source_target_pairs={{0,1},{1,2},{2,3},{4,5},{5,6},{6,7},{8,9},{9,10},{10,11},{12,13},{... | collective-permute-start | bytes 1572872 | tf_op jit(solution)/shard_map/ppermute | solution.py:187
  203.2 2.6 fusion.27
  205.8 2.7 add_convert_fusion.2
  209.4 4.5 %fusion.16 = bf16[2560,512]{1,0:T(8,128)(2,1)} fusion(bf16[1024,5120]{1,0:T(8,128)(2,1)S(1)} %bitcast.81, bf16[512,512]{1,0:T(8,128)(2,1)S(1)} %add_convert_fusion.6, bf16[512,512]{1,0:T(8,128)(2,1)S(1)} %get-tuple-element.116), kind=kOutput, calls=%fused_computation.14 | convolution fusion | flops 2687762432 | bytes 8912896 | tf_op jit(solution)/shard_map/dot_general | solution.py:17
  213.9 1.7 add_convert_fusion.3
  215.6 5.7 %fusion.19 = bf16[2560,512]{1,0:T(8,128)(2,1)S(1)} fusion(bf16[1024,5120]{1,0:T(8,128)(2,1)} %copy-done, bf16[512,512]{1,0:T(8,128)(2,1)S(1)} %add_convert_fusion.3, bf16[512,512]{1,0:T(8,128)(2,1)} %get-tuple-element.115), kind=kOutput, calls=%fused_computation.15 | convolution fusion | flops 2687762432 | bytes 8912896 | tf_op jit(solution)/shard_map/dot_general | solution.py:17
  221.9 3.2 %fusion.10 = bf16[2560,512]{1,0:T(8,128)(2,1)S(1)} fusion(bf16[1024,5120]{1,0:T(8,128)(2,1)S(1)} %bitcast.83, bf16[512,512]{1,0:T(8,128)(2,1)S(1)} %add_convert_fusion.6, bf16[512,512]{1,0:T(8,128)(2,1)S(1)} %copy-done.20), kind=kOutput, calls=%fused_computation.12 | convolution fusion | flops 2687762432 | bytes 8912896 | tf_op jit(solution)/shard_map/dot_general | solution.py:17
  225.1 3.2 %fusion.13 = bf16[2560,512]{1,0:T(8,128)(2,1)S(1)} fusion(bf16[1024,5120]{1,0:T(8,128)(2,1)S(1)} %bitcast.83, bf16[512,512]{1,0:T(8,128)(2,1)S(1)} %add_convert_fusion.3, bf16[512,512]{1,0:T(8,128)(2,1)S(1)} %copy-done.18), kind=kOutput, calls=%fused_computation.13 | convolution fusion | flops 2687762432 | bytes 8912896 | tf_op jit(solution)/shard_map/dot_general | solution.py:17
  228.3 2.5 add_convert_fusion.1
  231.0 1.6 collective-permute-start.33
  234.9 1.6 collective-permute-start.41
  236.5 12.2 %collective-permute-done.33 = bf16[2,640,256]{2,1,0:T(8,128)(2,1)S(1)} collective-permute-done((bf16[2,640,256]{2,1,0:T(8,128)(2,1)S(1)}, bf16[2,640,256]{2,1,0:T(8,128)(2,1)S(1)}, u32[]{:S(2)}, u32[]{:S(2)}) %collective-permute-start.33) | collective-permute-done | bytes 655392 | tf_op jit(solution)/shard_map/ppermute | solution.py:21
  248.6 1.6 collective-permute-done.34
  251.6 11.1 %collective-permute-done.40 = bf16[2,640,256]{2,1,0:T(8,128)(2,1)S(1)} collective-permute-done((bf16[2,640,256]{2,1,0:T(8,128)(2,1)S(1)}, bf16[2,640,256]{2,1,0:T(8,128)(2,1)S(1)}, u32[]{:S(2)}, u32[]{:S(2)}) %collective-permute-start.40) | collective-permute-done | bytes 655392 | tf_op jit(solution)/shard_map/ppermute | solution.py:21
  262.7 1.6 collective-permute-done.41
  265.6 5.7 %collective-permute-done.35 = bf16[1,640,256]{2,1,0:T(8,128)(2,1)S(1)} collective-permute-done((bf16[1,640,256]{2,1,0:T(8,128)(2,1)S(1)}, bf16[1,640,256]{2,1,0:T(8,128)(2,1)S(1)}, u32[]{:S(2)}, u32[]{:S(2)}) %collective-permute-start.35) | collective-permute-done | bytes 327712 | tf_op jit(solution)/shard_map/ppermute | solution.py:21
  273.6 3.6 %collective-permute-done.42 = bf16[1,640,256]{2,1,0:T(8,128)(2,1)S(1)} collective-permute-done((bf16[1,640,256]{2,1,0:T(8,128)(2,1)S(1)}, bf16[1,640,256]{2,1,0:T(8,128)(2,1)S(1)}, u32[]{:S(2)}, u32[]{:S(2)}) %collective-permute-start.42) | collective-permute-done | bytes 327712 | tf_op jit(solution)/shard_map/ppermute | solution.py:21
  277.2 2.2 multiply_reduce_fusion
  280.7 1.2 collective-permute-done.44
  282.4 1.5 collective-permute-start.45
  283.9 1.5 collective-permute-start.46
  287.5 6.2 %collective-permute-start.50 = (f32[8,128]{1,0:T(8,128)S(1)}, f32[8,128]{1,0:T(8,128)S(1)}, u32[]{:S(2)}, u32[]{:S(2)}) collective-permute-start(f32[8,128]{1,0:T(8,128)S(1)} %add_add_fusion.1), channel_id=1, source_target_pairs={{0,3},{1,0},{2,1},{3,2},{4,7},{5,4},{6,5},{7,6},{8,11},{9,8},{10,9... | collective-permute-start | bytes 12296 | tf_op jit(solution)/shard_map/ppermute | solution.py:229
  295.0 4.1 %collective-permute-done.48 = f32[8,128]{1,0:T(8,128)S(1)} collective-permute-done((f32[8,128]{1,0:T(8,128)S(1)}, f32[8,128]{1,0:T(8,128)S(1)}, u32[]{:S(2)}, u32[]{:S(2)}) %collective-permute-start.48) | collective-permute-done | bytes 4128 | tf_op jit(solution)/shard_map/ppermute | solution.py:229
  299.1 1.3 shard_map.56
  (159 shorter events, 33.6 us)
Async XLA Ops:
  0.0 32.1 %collective-permute-start = (bf16[640,1024]{1,0:T(8,128)(2,1)}, bf16[640,1024]{1,0:T(8,128)(2,1)}, u32[]{:S(2)}, u32[]{:S(2)}) collective-permute-start(bf16[640,1024]{1,0:T(8,128)(2,1)} %param.8), channel_id=1, source_target_pairs={{0,8},{4,12},{8,0},{12,4},{16,24},{20,28},{24,16},{28,20},{1,9},{5... | collective-permute-start | bytes 3932168 | tf_op jit(solution)/shard_map/ppermute | solution.py:21
  3.0 32.1 %collective-permute-start.1 = (bf16[640,1024]{1,0:T(8,128)(2,1)}, bf16[640,1024]{1,0:T(8,128)(2,1)S(1)}, u32[]{:S(2)}, u32[]{:S(2)}) collective-permute-start(bf16[640,1024]{1,0:T(8,128)(2,1)} %param.8), channel_id=1, source_target_pairs={{0,16},{4,20},{8,24},{12,28},{16,0},{20,4},{24,8},{28,12},{1,17},{... | collective-permute-start | bytes 3932168 | tf_op jit(solution)/shard_map/ppermute | solution.py:21
  10.2 26.4 %copy-start.9 = (bf16[640,1024]{1,0:T(8,128)(2,1)S(1)}, bf16[640,1024]{1,0:T(8,128)(2,1)}, u32[]{:S(2)}) copy-start(bf16[640,1024]{1,0:T(8,128)(2,1)} %param.8) | copy-start | bytes 3932164
  14.2 40.7 %copy-start = (bf16[1024,5120]{1,0:T(8,128)(2,1)}, bf16[1024,5120]{1,0:T(8,128)(2,1)S(1)}, u32[]{:S(2)}) copy-start(bf16[1024,5120]{1,0:T(8,128)(2,1)S(1)} %shard_map.55) | copy-start | bytes 31457284
  33.2 16.0 %collective-permute-start.2 = (bf16[320,1024]{1,0:T(8,128)(2,1)S(1)}, bf16[320,1024]{1,0:T(8,128)(2,1)S(1)}, u32[]{:S(2)}, u32[]{:S(2)}) collective-permute-start(bf16[320,1024]{1,0:T(8,128)(2,1)S(1)} %slice.134), channel_id=1, source_target_pairs={{0,16},{4,20},{8,24},{12,28},{16,0},{20,4},{24,8},{28,12},{1,17},{... | collective-permute-start | bytes 1966088 | tf_op jit(solution)/shard_map/ppermute | solution.py:21
  35.1 15.4 %collective-permute-start.3 = (bf16[320,1024]{1,0:T(8,128)(2,1)S(1)}, bf16[320,1024]{1,0:T(8,128)(2,1)S(1)}, u32[]{:S(2)}, u32[]{:S(2)}) collective-permute-start(bf16[320,1024]{1,0:T(8,128)(2,1)S(1)} %slice.135), channel_id=1, source_target_pairs={{0,8},{4,12},{8,0},{12,4},{16,24},{20,28},{24,16},{28,20},{1,9},{5... | collective-permute-start | bytes 1966088 | tf_op jit(solution)/shard_map/ppermute | solution.py:21
  36.6 17.3 %collective-permute-start.4 = (bf16[640,1024]{1,0:T(8,128)(2,1)S(1)}, bf16[640,1024]{1,0:T(8,128)(2,1)S(1)}, u32[]{:S(2)}, u32[]{:S(2)}) collective-permute-start(bf16[640,1024]{1,0:T(8,128)(2,1)S(1)} %copy-done.9), channel_id=1, source_target_pairs={{0,4},{4,0},{8,12},{12,8},{16,20},{20,16},{24,28},{28,24},{1,5},{5... | collective-permute-start | bytes 3932168 | tf_op jit(solution)/shard_map/ppermute | solution.py:21
  36.6 18.0 %collective-permute-start.5 = (bf16[640,1024]{1,0:T(8,128)(2,1)}, bf16[640,1024]{1,0:T(8,128)(2,1)S(1)}, u32[]{:S(2)}, u32[]{:S(2)}) collective-permute-start(bf16[640,1024]{1,0:T(8,128)(2,1)} %collective-permute-done), channel_id=1, source_target_pairs={{0,4},{4,0},{8,12},{12,8},{16,20},{20,16},{24,28},{28,24},{1,5},{5... | collective-permute-start | bytes 3932168 | tf_op jit(solution)/shard_map/ppermute | solution.py:21
  37.1 17.6 %collective-permute-start.6 = (bf16[640,1024]{1,0:T(8,128)(2,1)S(1)}, bf16[640,1024]{1,0:T(8,128)(2,1)S(1)}, u32[]{:S(2)}, u32[]{:S(2)}) collective-permute-start(bf16[640,1024]{1,0:T(8,128)(2,1)S(1)} %collective-permute-done.1), channel_id=1, source_target_pairs={{0,4},{4,0},{8,12},{12,8},{16,20},{20,16},{24,28},{28,24},{1,5},{5... | collective-permute-start | bytes 3932168 | tf_op jit(solution)/shard_map/ppermute | solution.py:21
  50.6 4.3 %collective-permute-start.7 = (bf16[640,1024]{1,0:T(8,128)(2,1)S(1)}, bf16[640,1024]{1,0:T(8,128)(2,1)S(1)}, u32[]{:S(2)}, u32[]{:S(2)}) collective-permute-start(bf16[640,1024]{1,0:T(8,128)(2,1)S(1)} %pad_maximum_fusion), channel_id=1, source_target_pairs={{0,4},{4,0},{8,12},{12,8},{16,20},{20,16},{24,28},{28,24},{1,5},{5... | collective-permute-start | bytes 3932168 | tf_op jit(solution)/shard_map/ppermute | solution.py:21
  52.3 25.8 %collective-permute-start.9 = (bf16[512,1024]{1,0:T(8,128)(2,1)}, bf16[512,1024]{1,0:T(8,128)(2,1)S(1)}, u32[]{:S(2)}, u32[]{:S(2)}) collective-permute-start(bf16[512,1024]{1,0:T(8,128)(2,1)} %param.9), channel_id=1, source_target_pairs={{0,8},{4,12},{8,0},{12,4},{16,24},{20,28},{24,16},{28,20},{1,9},{5... | collective-permute-start | bytes 3145736 | tf_op jit(solution)/shard_map/ppermute | solution.py:21
  53.9 25.6 %collective-permute-start.11 = (bf16[512,1024]{1,0:T(8,128)(2,1)}, bf16[512,1024]{1,0:T(8,128)(2,1)S(1)}, u32[]{:S(2)}, u32[]{:S(2)}) collective-permute-start(bf16[512,1024]{1,0:T(8,128)(2,1)} %param.9), channel_id=1, source_target_pairs={{0,16},{4,20},{8,24},{12,28},{16,0},{20,4},{24,8},{28,12},{1,17},{... | collective-permute-start | bytes 3145736 | tf_op jit(solution)/shard_map/ppermute | solution.py:21
  66.2 14.2 %copy-start.14 = (bf16[1024,1024]{1,0:T(8,128)(2,1)}, bf16[1024,1024]{1,0:T(8,128)(2,1)S(1)}, u32[]{:S(2)}) copy-start(bf16[1024,1024]{1,0:T(8,128)(2,1)S(1)} %convolution_convert_fusion) | copy-start | bytes 6291460
  67.3 33.1 %collective-permute-start.8 = (bf16[512,1024]{1,0:T(8,128)(2,1)}, bf16[512,1024]{1,0:T(8,128)(2,1)}, u32[]{:S(2)}, u32[]{:S(2)}) collective-permute-start(bf16[512,1024]{1,0:T(8,128)(2,1)} %param.9), channel_id=1, source_target_pairs={{0,4},{4,0},{8,12},{12,8},{16,20},{20,16},{24,28},{28,24},{1,5},{5... | collective-permute-start | bytes 3145736 | tf_op jit(solution)/shard_map/ppermute | solution.py:21
  78.2 13.5 %collective-permute-start.13 = (bf16[256,1024]{1,0:T(8,128)(2,1)S(1)}, bf16[256,1024]{1,0:T(8,128)(2,1)S(1)}, u32[]{:S(2)}, u32[]{:S(2)}) collective-permute-start(bf16[256,1024]{1,0:T(8,128)(2,1)S(1)} %slice.138), channel_id=1, source_target_pairs={{0,16},{4,20},{8,24},{12,28},{16,0},{20,4},{24,8},{28,12},{1,17},{... | collective-permute-start | bytes 1572872 | tf_op jit(solution)/shard_map/ppermute | solution.py:21
  78.8 23.3 %collective-permute-start.10 = (bf16[512,1024]{1,0:T(8,128)(2,1)S(1)}, bf16[512,1024]{1,0:T(8,128)(2,1)}, u32[]{:S(2)}, u32[]{:S(2)}) collective-permute-start(bf16[512,1024]{1,0:T(8,128)(2,1)S(1)} %collective-permute-done.9), channel_id=1, source_target_pairs={{0,4},{4,0},{8,12},{12,8},{16,20},{20,16},{24,28},{28,24},{1,5},{5... | collective-permute-start | bytes 3145736 | tf_op jit(solution)/shard_map/ppermute | solution.py:21
  80.3 17.8 %collective-permute-start.14 = (bf16[256,1024]{1,0:T(8,128)(2,1)}, bf16[256,1024]{1,0:T(8,128)(2,1)}, u32[]{:S(2)}, u32[]{:S(2)}) collective-permute-start(bf16[256,1024]{1,0:T(8,128)(2,1)} %slice.139), channel_id=1, source_target_pairs={{0,8},{4,12},{8,0},{12,4},{16,24},{20,28},{24,16},{28,20},{1,9},{5... | collective-permute-start | bytes 1572872 | tf_op jit(solution)/shard_map/ppermute | solution.py:21
  81.0 22.6 %collective-permute-start.12 = (bf16[512,1024]{1,0:T(8,128)(2,1)S(1)}, bf16[512,1024]{1,0:T(8,128)(2,1)}, u32[]{:S(2)}, u32[]{:S(2)}) collective-permute-start(bf16[512,1024]{1,0:T(8,128)(2,1)S(1)} %collective-permute-done.11), channel_id=1, source_target_pairs={{0,4},{4,0},{8,12},{12,8},{16,20},{20,16},{24,28},{28,24},{1,5},{5... | collective-permute-start | bytes 3145736 | tf_op jit(solution)/shard_map/ppermute | solution.py:21
  92.5 33.0 %collective-permute-start.16 = (bf16[512,1024]{1,0:T(8,128)(2,1)}, bf16[512,1024]{1,0:T(8,128)(2,1)}, u32[]{:S(2)}, u32[]{:S(2)}) collective-permute-start(bf16[512,1024]{1,0:T(8,128)(2,1)} %fusion.56), channel_id=1, source_target_pairs={{0,1},{1,2},{2,3},{4,5},{5,6},{6,7},{8,9},{9,10},{10,11},{12,13},{... | collective-permute-start | bytes 3145736 | tf_op jit(solution)/shard_map/ppermute | solution.py:155
  98.1 25.9 %collective-permute-start.18 = (bf16[512,1024]{1,0:T(8,128)(2,1)}, bf16[512,1024]{1,0:T(8,128)(2,1)}, u32[]{:S(2)}, u32[]{:S(2)}) collective-permute-start(bf16[512,1024]{1,0:T(8,128)(2,1)} %fusion.56), channel_id=1, source_target_pairs={{3,2},{2,1},{1,0},{7,6},{6,5},{5,4},{11,10},{10,9},{9,8},{15,14},{... | collective-permute-start | bytes 3145736 | tf_op jit(solution)/shard_map/ppermute | solution.py:157
  100.5 8.3 %collective-permute-start.15 = (bf16[512,1024]{1,0:T(8,128)(2,1)S(1)}, bf16[512,1024]{1,0:T(8,128)(2,1)S(1)}, u32[]{:S(2)}, u32[]{:S(2)}) collective-permute-start(bf16[512,1024]{1,0:T(8,128)(2,1)S(1)} %constant_dynamic-update-slice_fusion.9), channel_id=1, source_target_pairs={{0,4},{4,0},{8,12},{12,8},{16,20},{20,16},{24,28},{28,24},{1,5},{5... | collective-permute-start | bytes 3145736 | tf_op jit(solution)/shard_map/ppermute | solution.py:21
  111.5 14.9 %collective-permute-start.23 = (bf16[512,512]{1,0:T(8,128)(2,1)}, bf16[512,512]{1,0:T(8,128)(2,1)S(1)}, u32[]{:S(2)}, u32[]{:S(2)}) collective-permute-start(bf16[512,512]{1,0:T(8,128)(2,1)} %get-tuple-element.51), channel_id=1, source_target_pairs={{3,2},{7,6},{11,10},{15,14},{19,18},{23,22},{27,26},{31,30}} | collective-permute-start | bytes 1572872 | tf_op jit(solution)/shard_map/ppermute | solution.py:188
  112.4 16.7 %collective-permute-start.22 = (bf16[512,512]{1,0:T(8,128)(2,1)}, bf16[512,512]{1,0:T(8,128)(2,1)S(1)}, u32[]{:S(2)}, u32[]{:S(2)}) collective-permute-start(bf16[512,512]{1,0:T(8,128)(2,1)} %get-tuple-element.50), channel_id=1, source_target_pairs={{0,1},{4,5},{8,9},{12,13},{16,17},{20,21},{24,25},{28,29}} | collective-permute-start | bytes 1572872 | tf_op jit(solution)/shard_map/ppermute | solution.py:187
  124.0 25.0 %collective-permute-start.19 = (bf16[512,1024]{1,0:T(8,128)(2,1)}, bf16[512,1024]{1,0:T(8,128)(2,1)}, u32[]{:S(2)}, u32[]{:S(2)}) collective-permute-start(bf16[512,1024]{1,0:T(8,128)(2,1)} %collective-permute-done.18), channel_id=1, source_target_pairs={{2,1},{1,0},{6,5},{5,4},{10,9},{9,8},{14,13},{13,12},{18,17},{17,1... | collective-permute-start | bytes 3145736 | tf_op jit(solution)/shard_map/ppermute | solution.py:157
  125.5 12.5 %copy-start.7 = (bf16[512,3072]{1,0:T(8,128)(2,1)S(1)}, bf16[512,3072]{1,0:T(8,128)(2,1)}, u32[]{:S(2)}) copy-start(bf16[512,3072]{1,0:T(8,128)(2,1)} %copy-done.6) | copy-start | bytes 9437188
  125.5 43.3 %collective-permute-start.17 = (bf16[512,1024]{1,0:T(8,128)(2,1)}, bf16[512,1024]{1,0:T(8,128)(2,1)S(1)}, u32[]{:S(2)}, u32[]{:S(2)}) collective-permute-start(bf16[512,1024]{1,0:T(8,128)(2,1)} %collective-permute-done.16), channel_id=1, source_target_pairs={{1,2},{2,3},{5,6},{6,7},{9,10},{10,11},{13,14},{14,15},{17,18},{18... | collective-permute-start | bytes 3145736 | tf_op jit(solution)/shard_map/ppermute | solution.py:155
  129.0 28.0 %copy-start.11 = (bf16[512,1024]{1,0:T(8,128)(2,1)S(1)}, bf16[512,1024]{1,0:T(8,128)(2,1)}, u32[]{:S(2)}) copy-start(bf16[512,1024]{1,0:T(8,128)(2,1)} %copy-done.10) | copy-start | bytes 3145732
  130.8 27.3 %collective-permute-start.25 = (bf16[512,512]{1,0:T(8,128)(2,1)S(1)}, bf16[512,512]{1,0:T(8,128)(2,1)S(1)}, u32[]{:S(2)}, u32[]{:S(2)}) collective-permute-start(bf16[512,512]{1,0:T(8,128)(2,1)S(1)} %get-tuple-element.53), channel_id=1, source_target_pairs={{3,2},{2,1},{7,6},{6,5},{11,10},{10,9},{15,14},{14,13},{19,18},{18... | collective-permute-start | bytes 1572872 | tf_op jit(solution)/shard_map/ppermute | solution.py:188
  131.5 28.1 %collective-permute-start.24 = (bf16[512,512]{1,0:T(8,128)(2,1)S(1)}, bf16[512,512]{1,0:T(8,128)(2,1)S(1)}, u32[]{:S(2)}, u32[]{:S(2)}) collective-permute-start(bf16[512,512]{1,0:T(8,128)(2,1)S(1)} %get-tuple-element.52), channel_id=1, source_target_pairs={{0,1},{1,2},{4,5},{5,6},{8,9},{9,10},{12,13},{13,14},{16,17},{17,1... | collective-permute-start | bytes 1572872 | tf_op jit(solution)/shard_map/ppermute | solution.py:187
  138.4 23.2 %collective-permute-start.28 = (bf16[512,512]{1,0:T(8,128)(2,1)S(1)}, bf16[512,512]{1,0:T(8,128)(2,1)S(1)}, u32[]{:S(2)}, u32[]{:S(2)}) collective-permute-start(bf16[512,512]{1,0:T(8,128)(2,1)S(1)} %get-tuple-element.59), channel_id=1, source_target_pairs={{3,2},{7,6},{11,10},{15,14},{19,18},{23,22},{27,26},{31,30}} | collective-permute-start | bytes 1572872 | tf_op jit(solution)/shard_map/ppermute | solution.py:188
  149.0 13.6 %collective-permute-start.27 = (bf16[512,512]{1,0:T(8,128)(2,1)S(1)}, bf16[512,512]{1,0:T(8,128)(2,1)S(1)}, u32[]{:S(2)}, u32[]{:S(2)}) collective-permute-start(bf16[512,512]{1,0:T(8,128)(2,1)S(1)} %get-tuple-element.58), channel_id=1, source_target_pairs={{0,1},{4,5},{8,9},{12,13},{16,17},{20,21},{24,25},{28,29}} | collective-permute-start | bytes 1572872 | tf_op jit(solution)/shard_map/ppermute | solution.py:187
  157.0 16.8 %copy-start.16 = (bf16[1024,1024]{1,0:T(8,128)(2,1)S(1)}, bf16[1024,1024]{1,0:T(8,128)(2,1)}, u32[]{:S(2)}) copy-start(bf16[1024,1024]{1,0:T(8,128)(2,1)} %copy-done.14) | copy-start | bytes 6291460
  158.1 15.8 %copy-start.5 = (bf16[4096,1024]{1,0:T(8,128)(2,1)S(1)}, bf16[4096,1024]{1,0:T(8,128)(2,1)}, u32[]{:S(2)}) copy-start(bf16[4096,1024]{1,0:T(8,128)(2,1)} %constant_dynamic-update-slice_fusion.11) | copy-start | bytes 25165828
  158.1 45.1 %collective-permute-start.20 = (bf16[512,1024]{1,0:T(8,128)(2,1)}, bf16[512,1024]{1,0:T(8,128)(2,1)S(1)}, u32[]{:S(2)}, u32[]{:S(2)}) collective-permute-start(bf16[512,1024]{1,0:T(8,128)(2,1)} %collective-permute-done.19), channel_id=1, source_target_pairs={{1,0},{5,4},{9,8},{13,12},{17,16},{21,20},{25,24},{29,28}} | collective-permute-start | bytes 3145736 | tf_op jit(solution)/shard_map/ppermute | solution.py:157
  160.2 32.1 %collective-permute-start.31 = (bf16[512,512]{1,0:T(8,128)(2,1)S(1)}, bf16[512,512]{1,0:T(8,128)(2,1)S(1)}, u32[]{:S(2)}, u32[]{:S(2)}) collective-permute-start(bf16[512,512]{1,0:T(8,128)(2,1)S(1)} %get-tuple-element.63), channel_id=1, source_target_pairs={{3,2},{2,1},{1,0},{7,6},{6,5},{5,4},{11,10},{10,9},{9,8},{15,14},{... | collective-permute-start | bytes 1572872 | tf_op jit(solution)/shard_map/ppermute | solution.py:188
  163.2 32.3 %collective-permute-start.29 = (bf16[512,512]{1,0:T(8,128)(2,1)S(1)}, bf16[512,512]{1,0:T(8,128)(2,1)S(1)}, u32[]{:S(2)}, u32[]{:S(2)}) collective-permute-start(bf16[512,512]{1,0:T(8,128)(2,1)S(1)} %get-tuple-element.60), channel_id=1, source_target_pairs={{0,1},{1,2},{4,5},{5,6},{8,9},{9,10},{12,13},{13,14},{16,17},{17,1... | collective-permute-start | bytes 1572872 | tf_op jit(solution)/shard_map/ppermute | solution.py:187
  168.1 27.4 %collective-permute-start.30 = (bf16[512,512]{1,0:T(8,128)(2,1)S(1)}, bf16[512,512]{1,0:T(8,128)(2,1)S(1)}, u32[]{:S(2)}, u32[]{:S(2)}) collective-permute-start(bf16[512,512]{1,0:T(8,128)(2,1)S(1)} %get-tuple-element.61), channel_id=1, source_target_pairs={{3,2},{2,1},{7,6},{6,5},{11,10},{10,9},{15,14},{14,13},{19,18},{18... | collective-permute-start | bytes 1572872 | tf_op jit(solution)/shard_map/ppermute | solution.py:188
  168.8 26.7 %collective-permute-start.26 = (bf16[512,512]{1,0:T(8,128)(2,1)S(1)}, bf16[512,512]{1,0:T(8,128)(2,1)S(1)}, u32[]{:S(2)}, u32[]{:S(2)}) collective-permute-start(bf16[512,512]{1,0:T(8,128)(2,1)S(1)} %get-tuple-element.54), channel_id=1, source_target_pairs={{0,1},{1,2},{2,3},{4,5},{5,6},{6,7},{8,9},{9,10},{10,11},{12,13},{... | collective-permute-start | bytes 1572872 | tf_op jit(solution)/shard_map/ppermute | solution.py:187
  192.3 13.5 %collective-permute-start.21 = (bf16[512,1024]{1,0:T(8,128)(2,1)S(1)}, bf16[512,1024]{1,0:T(8,128)(2,1)S(1)}, u32[]{:S(2)}, u32[]{:S(2)}) collective-permute-start(bf16[512,1024]{1,0:T(8,128)(2,1)S(1)} %collective-permute-done.17), channel_id=1, source_target_pairs={{2,3},{6,7},{10,11},{14,15},{18,19},{22,23},{26,27},{30,31}} | collective-permute-start | bytes 3145736 | tf_op jit(solution)/shard_map/ppermute | solution.py:155
  196.1 17.8 %collective-permute-start.38 = (bf16[512,512]{1,0:T(8,128)(2,1)S(1)}, bf16[512,512]{1,0:T(8,128)(2,1)S(1)}, u32[]{:S(2)}, u32[]{:S(2)}) collective-permute-start(bf16[512,512]{1,0:T(8,128)(2,1)S(1)} %get-tuple-element.71), channel_id=1, source_target_pairs={{3,2},{2,1},{1,0},{7,6},{6,5},{5,4},{11,10},{10,9},{9,8},{15,14},{... | collective-permute-start | bytes 1572872 | tf_op jit(solution)/shard_map/ppermute | solution.py:188
  197.4 16.5 %collective-permute-start.37 = (bf16[512,512]{1,0:T(8,128)(2,1)S(1)}, bf16[512,512]{1,0:T(8,128)(2,1)}, u32[]{:S(2)}, u32[]{:S(2)}) collective-permute-start(bf16[512,512]{1,0:T(8,128)(2,1)S(1)} %get-tuple-element.70), channel_id=1, source_target_pairs={{0,1},{1,2},{2,3},{4,5},{5,6},{6,7},{8,9},{9,10},{10,11},{12,13},{... | collective-permute-start | bytes 1572872 | tf_op jit(solution)/shard_map/ppermute | solution.py:187
  213.8 14.4 %collective-permute-start.32 = (bf16[2560,512]{1,0:T(8,128)(2,1)}, bf16[2560,512]{1,0:T(8,128)(2,1)}, u32[]{:S(2)}, u32[]{:S(2)}) collective-permute-start(bf16[2560,512]{1,0:T(8,128)(2,1)} %fusion.16), channel_id=1, source_target_pairs={{0,4},{4,0},{8,12},{12,8},{16,20},{20,16},{24,28},{28,24},{1,5},{5... | collective-permute-start | bytes 7864328 | tf_op jit(solution)/shard_map/ppermute | solution.py:21
  213.8 8.0 %slice-start.3 = ((s8[10485760]{0:T(1024)(128)(4,1)}), s8[4194304]{0:T(1024)(128)(4,1)S(1)}, s32[]{:S(2)}) async-start(s8[10485760]{0:T(1024)(128)(4,1)} %bitcast.82), calls=%async_computation.3 | async-start | bytes 8388608
  215.6 6.3 %slice-start.4 = ((s8[10485760]{0:T(1024)(128)(4,1)}), s8[4194304]{0:T(1024)(128)(4,1)S(1)}, s32[]{:S(2)}) async-start(s8[10485760]{0:T(1024)(128)(4,1)} %bitcast.82), calls=%async_computation.4 | async-start | bytes 8388608
  215.6 6.3 %slice-start.5 = ((s8[10485760]{0:T(1024)(128)(4,1)}), s8[2097152]{0:T(1024)(128)(4,1)S(1)}, s32[]{:S(2)}) async-start(s8[10485760]{0:T(1024)(128)(4,1)} %bitcast.82), calls=%async_computation.5 | async-start | bytes 4194304
  221.3 11.9 %collective-permute-start.39 = (bf16[2560,512]{1,0:T(8,128)(2,1)S(1)}, bf16[2560,512]{1,0:T(8,128)(2,1)S(1)}, u32[]{:S(2)}, u32[]{:S(2)}) collective-permute-start(bf16[2560,512]{1,0:T(8,128)(2,1)S(1)} %fusion.19), channel_id=1, source_target_pairs={{0,4},{4,0},{8,12},{12,8},{16,20},{20,16},{24,28},{28,24},{1,5},{5... | collective-permute-start | bytes 7864328 | tf_op jit(solution)/shard_map/ppermute | solution.py:21
  231.0 17.7 %collective-permute-start.33 = (bf16[2,640,256]{2,1,0:T(8,128)(2,1)S(1)}, bf16[2,640,256]{2,1,0:T(8,128)(2,1)S(1)}, u32[]{:S(2)}, u32[]{:S(2)}) collective-permute-start(bf16[2,640,256]{2,1,0:T(8,128)(2,1)S(1)} %pad_maximum_fusion.3), channel_id=1, source_target_pairs={{0,8},{4,12},{8,0},{12,4},{16,24},{20,28},{24,16},{28,20},{1,9},{5... | collective-permute-start | bytes 1966088 | tf_op jit(solution)/shard_map/ppermute | solution.py:21
  232.6 17.7 %collective-permute-start.34 = (bf16[2,640,256]{2,1,0:T(8,128)(2,1)S(1)}, bf16[2,640,256]{2,1,0:T(8,128)(2,1)S(1)}, u32[]{:S(2)}, u32[]{:S(2)}) collective-permute-start(bf16[2,640,256]{2,1,0:T(8,128)(2,1)S(1)} %pad_maximum_fusion.4), channel_id=1, source_target_pairs={{0,16},{4,20},{8,24},{12,28},{16,0},{20,4},{24,8},{28,12},{1,17},{... | collective-permute-start | bytes 1966088 | tf_op jit(solution)/shard_map/ppermute | solution.py:21
  234.1 30.5 %copy-start.8 = (bf16[2560,512]{1,0:T(8,128)(2,1)}, bf16[2560,512]{1,0:T(8,128)(2,1)S(1)}, u32[]{:S(2)}) copy-start(bf16[2560,512]{1,0:T(8,128)(2,1)S(1)} %add_convert_fusion) | copy-start | bytes 7864324
  234.2 28.5 %collective-permute-start.40 = (bf16[2,640,256]{2,1,0:T(8,128)(2,1)S(1)}, bf16[2,640,256]{2,1,0:T(8,128)(2,1)S(1)}, u32[]{:S(2)}, u32[]{:S(2)}) collective-permute-start(bf16[2,640,256]{2,1,0:T(8,128)(2,1)S(1)} %pad_maximum_fusion.5), channel_id=1, source_target_pairs={{0,8},{4,12},{8,0},{12,4},{16,24},{20,28},{24,16},{28,20},{1,9},{5... | collective-permute-start | bytes 1966088 | tf_op jit(solution)/shard_map/ppermute | solution.py:21
  234.9 29.4 %collective-permute-start.41 = (bf16[2,640,256]{2,1,0:T(8,128)(2,1)S(1)}, bf16[2,640,256]{2,1,0:T(8,128)(2,1)S(1)}, u32[]{:S(2)}, u32[]{:S(2)}) collective-permute-start(bf16[2,640,256]{2,1,0:T(8,128)(2,1)S(1)} %pad_maximum_fusion.6), channel_id=1, source_target_pairs={{0,16},{4,20},{8,24},{12,28},{16,0},{20,4},{24,8},{28,12},{1,17},{... | collective-permute-start | bytes 1966088 | tf_op jit(solution)/shard_map/ppermute | solution.py:21
  250.5 20.9 %collective-permute-start.35 = (bf16[1,640,256]{2,1,0:T(8,128)(2,1)S(1)}, bf16[1,640,256]{2,1,0:T(8,128)(2,1)S(1)}, u32[]{:S(2)}, u32[]{:S(2)}) collective-permute-start(bf16[1,640,256]{2,1,0:T(8,128)(2,1)S(1)} %get-tuple-element.108), channel_id=1, source_target_pairs={{0,16},{4,20},{8,24},{12,28},{16,0},{20,4},{24,8},{28,12},{1,17},{... | collective-permute-start | bytes 983048 | tf_op jit(solution)/shard_map/ppermute | solution.py:21
  251.0 20.3 %collective-permute-start.36 = (bf16[1,640,256]{2,1,0:T(8,128)(2,1)S(1)}, bf16[1,640,256]{2,1,0:T(8,128)(2,1)S(1)}, u32[]{:S(2)}, u32[]{:S(2)}) collective-permute-start(bf16[1,640,256]{2,1,0:T(8,128)(2,1)S(1)} %get-tuple-element.107), channel_id=1, source_target_pairs={{0,8},{4,12},{8,0},{12,4},{16,24},{20,28},{24,16},{28,20},{1,9},{5... | collective-permute-start | bytes 983048 | tf_op jit(solution)/shard_map/ppermute | solution.py:21
  262.7 8.7 %copy-start.12 = (bf16[2,640,256]{2,1,0:T(8,128)(2,1)}, bf16[2,640,256]{2,1,0:T(8,128)(2,1)S(1)}, u32[]{:S(2)}) copy-start(bf16[2,640,256]{2,1,0:T(8,128)(2,1)S(1)} %collective-permute-done.40) | copy-start | bytes 1966084
  264.3 7.0 %copy-start.13 = (bf16[2,640,256]{2,1,0:T(8,128)(2,1)}, bf16[2,640,256]{2,1,0:T(8,128)(2,1)S(1)}, u32[]{:S(2)}) copy-start(bf16[2,640,256]{2,1,0:T(8,128)(2,1)S(1)} %collective-permute-done.41) | copy-start | bytes 1966084
  264.5 12.6 %collective-permute-start.42 = (bf16[1,640,256]{2,1,0:T(8,128)(2,1)S(1)}, bf16[1,640,256]{2,1,0:T(8,128)(2,1)S(1)}, u32[]{:S(2)}, u32[]{:S(2)}) collective-permute-start(bf16[1,640,256]{2,1,0:T(8,128)(2,1)S(1)} %get-tuple-element.100), channel_id=1, source_target_pairs={{0,16},{4,20},{8,24},{12,28},{16,0},{20,4},{24,8},{28,12},{1,17},{... | collective-permute-start | bytes 983048 | tf_op jit(solution)/shard_map/ppermute | solution.py:21
  265.1 12.1 %collective-permute-start.43 = (bf16[1,640,256]{2,1,0:T(8,128)(2,1)S(1)}, bf16[1,640,256]{2,1,0:T(8,128)(2,1)S(1)}, u32[]{:S(2)}, u32[]{:S(2)}) collective-permute-start(bf16[1,640,256]{2,1,0:T(8,128)(2,1)S(1)} %get-tuple-element.99), channel_id=1, source_target_pairs={{0,8},{4,12},{8,0},{12,4},{16,24},{20,28},{24,16},{28,20},{1,9},{5... | collective-permute-start | bytes 983048 | tf_op jit(solution)/shard_map/ppermute | solution.py:21
  280.7 1.2 collective-permute-start.44
  281.9 4.5 %collective-permute-start.47 = (f32[8,128]{1,0:T(8,128)S(1)}, f32[8,128]{1,0:T(8,128)S(1)}, u32[]{:S(2)}, u32[]{:S(2)}) collective-permute-start(f32[8,128]{1,0:T(8,128)S(1)} %broadcast_add_fusion), channel_id=1, source_target_pairs={{0,24},{4,28},{8,16},{12,20},{16,8},{20,12},{24,0},{28,4},{1,25},{... | collective-permute-start | bytes 12296 | tf_op jit(solution)/shard_map/ppermute | solution.py:21
  282.4 4.0 %collective-permute-start.45 = (f32[8,128]{1,0:T(8,128)S(1)}, f32[8,128]{1,0:T(8,128)S(1)}, u32[]{:S(2)}, u32[]{:S(2)}) collective-permute-start(f32[8,128]{1,0:T(8,128)S(1)} %broadcast_add_fusion), channel_id=1, source_target_pairs={{0,8},{4,12},{8,0},{12,4},{16,24},{20,28},{24,16},{28,20},{1,9},{5... | collective-permute-start | bytes 12296 | tf_op jit(solution)/shard_map/ppermute | solution.py:21
  283.9 3.6 %collective-permute-start.46 = (f32[8,128]{1,0:T(8,128)S(1)}, f32[8,128]{1,0:T(8,128)S(1)}, u32[]{:S(2)}, u32[]{:S(2)}) collective-permute-start(f32[8,128]{1,0:T(8,128)S(1)} %broadcast_add_fusion), channel_id=1, source_target_pairs={{0,16},{4,20},{8,24},{12,28},{16,0},{20,4},{24,8},{28,12},{1,17},{... | collective-permute-start | bytes 12296 | tf_op jit(solution)/shard_map/ppermute | solution.py:21
  287.5 7.6 %collective-permute-start.50 = (f32[8,128]{1,0:T(8,128)S(1)}, f32[8,128]{1,0:T(8,128)S(1)}, u32[]{:S(2)}, u32[]{:S(2)}) collective-permute-start(f32[8,128]{1,0:T(8,128)S(1)} %add_add_fusion.1), channel_id=1, source_target_pairs={{0,3},{1,0},{2,1},{3,2},{4,7},{5,4},{6,5},{7,6},{8,11},{9,8},{10,9... | collective-permute-start | bytes 12296 | tf_op jit(solution)/shard_map/ppermute | solution.py:229
  293.7 5.4 %collective-permute-start.48 = (f32[8,128]{1,0:T(8,128)S(1)}, f32[8,128]{1,0:T(8,128)S(1)}, u32[]{:S(2)}, u32[]{:S(2)}) collective-permute-start(f32[8,128]{1,0:T(8,128)S(1)} %add_add_fusion.1), channel_id=1, source_target_pairs={{0,1},{1,2},{2,3},{3,0},{4,5},{5,6},{6,7},{7,4},{8,9},{9,10},{10,1... | collective-permute-start | bytes 12296 | tf_op jit(solution)/shard_map/ppermute | solution.py:229
  293.7 5.4 %collective-permute-start.49 = (f32[8,128]{1,0:T(8,128)S(1)}, f32[8,128]{1,0:T(8,128)S(1)}, u32[]{:S(2)}, u32[]{:S(2)}) collective-permute-start(f32[8,128]{1,0:T(8,128)S(1)} %add_add_fusion.1), channel_id=1, source_target_pairs={{0,2},{1,3},{2,0},{3,1},{4,6},{5,7},{6,4},{7,5},{8,10},{9,11},{10,... | collective-permute-start | bytes 12296 | tf_op jit(solution)/shard_map/ppermute | solution.py:229
  (14 other events, 49.2 us)

commit v3 on v2

--- a/solution.py
+++ b/solution.py
@@ -106,6 +106,15 @@
     )(total, *pieces)
 
 
+def unset(rows, cols):
+    return pl.pallas_call(
+        lambda out_ref: None,
+        out_shape=jax.ShapeDtypeStruct((rows, cols), BF),
+        out_specs=pl.BlockSpec(memory_space=pl.ANY),
+        name="unset",
+    )()
+
+
 def per_device(n_fsdp, n_tp, activations, cotangent, lengths, grow_operator, proxy_weight):
     me = lax.axis_index("fsdp")
     at = lax.axis_index("tp")
@@ -137,14 +146,13 @@
 
     assert chunks == 2
     odd = me % 2
-    r_all = jnp.zeros((total_p, width), BF)
-    for m in range(close):
-        r_all = lax.dynamic_update_slice_in_dim(r_all, r[m], (m ^ odd) * depth, axis=0)
-    product_near = dot(forward, r_all[: close * depth], (1, 1)).astype(BF)
-    for m in range(close, n_fsdp):
-        block = after(r[m], product_near)
+    r_near = jnp.concatenate([r[m] for m in range(close)], axis=0)
+    product_near = dot(forward, r_near, (1, 1)).astype(BF)
+    product_far = [dot(forward, r[close + i], (1, 1)).astype(BF) for i in range(2)]
+    r_all = unset(total_p, width)
+    for m in range(n_fsdp):
+        block = after(r[m], product_far[0])
         r_all = lax.dynamic_update_slice_in_dim(r_all, block, (m ^ odd) * depth, axis=0)
-    product_far = [dot(forward, r[close + i], (1, 1)).astype(BF) for i in range(2)]
 
     def place(c, owner):
         return me ^ (jnp.clip(owner, 0, last) * chunks + c)
@@ -166,7 +174,7 @@
 
     def partial(products, c, owner):
         block = place(c, owner)
-        start = (jnp.minimum(block, close - 1) ^ odd) * depth
+        start = jnp.minimum(block, close - 1) * depth
         near = lax.dynamic_slice_in_dim(products[0], start, depth, axis=1)
         far = jnp.where(block == close, *products[1:])
         return jnp.where(block < close, near, far).astype(F32)

time: 301 us -> 315 us (1.047)
  starting transfers between devices: 78.9 us -> 87.8 us
  local copies, waits for them, and re-layouts: 23.9 us -> 32.4 us
  waiting for transfers between devices: 132 us -> 127 us
    ppermute x3, waiting for transfers between devices: 16.9 us -> 2.41 us  [per_device(): from_high.append(lax.ppermute(from_high[-1], 'tp', pairs))]
    ppermute x6, waiting for transfers between devices: 3.62 us -> 17.5 us  [per_device(): up = lax.ppermute(send_up, 'tp', [(i, i + 1) for i in range(hop)])]
    unnamed x63 -> x68, local copies, waits for them, and re-layouts: 9.57 us -> 19.6 us
    ppermute x3, starting transfers between devices: 6.86 us -> 13.3 us  [per_device(): lax.ppermute(total, 'tp', [(i, (i + k) % n_tp) for i in range(n_tp)])]
    ppermute x6, waiting for transfers between devices: 17.2 us -> 11 us  [per_device(): lax.ppermute(send_down, 'tp', [(last - i, last - 1 - i) for i in range(ho...]
    dynamic_update_slice x6 -> x0, local copies, waits for them, and re-layouts: 5.68 us -> none  [per_device(): lax.dynamic_update_slice_in_dim(r_all, r[m], (m ^ odd) * depth, axis=0)]
  transfers between devices with their start and end apart: 51 -> 51, of which waited for: 22 -> 23; matrix products, arithmetic and copies ran while one was open for 24% -> 26% of each run, Pallas kernels for 1% -> 1%
where the time goes in v3:
time: 315 us; the launch traced here: 314 us
  waiting for transfers between devices  127 us (40%)
  starting transfers between devices  87.8 us (28%)
  matrix products  45 us (14%)
  local copies, waits for them, and re-layouts  32.4 us (10%)
  other arithmetic  13.1 us (4%)
  Pallas kernels  5.27 us (2%)
  between operations  3.34 us (1%)
    ppermute x30, waiting for transfers between devices, flip(): return lax.ppermute(value, axis, [(i, i ^ bit) for i in range(size)])  91.4 us
    dot_general x12, matrix products, dot(): lax.dot_general(left, right, ((dims[:1], dims[1:]), ((), ())), preferred_...  45 us
    ppermute x6, starting transfers between devices, per_device(): up = lax.ppermute(send_up, 'tp', [(i, i + 1) for i in range(hop)])  32.3 us
    ppermute x30, starting transfers between devices, flip(): return lax.ppermute(value, axis, [(i, i ^ bit) for i in range(size)])  25.9 us
    unnamed x68, local copies, waits for them, and re-layouts  19.6 us
    ppermute x6, waiting for transfers between devices, per_device(): up = lax.ppermute(send_up, 'tp', [(i, i + 1) for i in range(hop)])  17.5 us
    ppermute x3, starting transfers between devices, per_device(): lax.ppermute(total, 'tp', [(i, (i + k) % n_tp) for i in range(n_tp)])  13.3 us
    ppermute x6, waiting for transfers between devices, per_device(): lax.ppermute(send_down, 'tp', [(last - i, last - 1 - i) for i in range(ho...  11 us
  transfers between devices with their start and end apart: 51, of which 23 were waited for; matrix products, arithmetic and copies ran while one was open for 26% of the time, Pallas kernels for 1%

profile of v3, /device:TPU:0, one launch (start us, length us, event | category | flops | bytes accessed | tf_op | source)
XLA Modules:
  0.0 314.1 jit_solution(4535019713946461610)
XLA Ops:
  0.0 3.0 collective-permute-start
  3.0 1.5 collective-permute-start.1
  4.6 2.5 copy-done.1
  7.1 2.5 copy-done.2
  10.2 4.0 %shard_map.55 = bf16[1024,5120]{1,0:T(8,128)(2,1)S(1)} custom-call(s32[8]{0:T(128)S(1)} %stack.83.places, s32[2]{0:T(128)S(1)} %copy-done.3, bf16[512,5120]{1,0:T(8,128)(2,1)S(1)} %copy-done.1, bf16[512,5120]{1,0:T(8,128)(2,1)S(1)} %copy-done.2), custom_call_target="tpu_custom_call" | custom-call | bytes 20971520 | tf_op jit(solution)/shard_map/pallas_call | solution.py:74
  14.2 17.8 %collective-permute-done = bf16[640,1024]{1,0:T(8,128)(2,1)} collective-permute-done((bf16[640,1024]{1,0:T(8,128)(2,1)}, bf16[640,1024]{1,0:T(8,128)(2,1)}, u32[]{:S(2)}, u32[]{:S(2)}) %collective-permute-start) | collective-permute-done | bytes 1310752 | tf_op jit(solution)/shard_map/ppermute | solution.py:21
  33.2 1.8 collective-permute-start.2
  36.2 1.6 collective-permute-start.3
  38.3 10.9 %collective-permute-done.2 = bf16[320,1024]{1,0:T(8,128)(2,1)S(1)} collective-permute-done((bf16[320,1024]{1,0:T(8,128)(2,1)S(1)}, bf16[320,1024]{1,0:T(8,128)(2,1)S(1)}, u32[]{:S(2)}, u32[]{:S(2)}) %collective-permute-start.2) | collective-permute-done | bytes 655392 | tf_op jit(solution)/shard_map/ppermute | solution.py:21
  49.2 2.4 collective-permute-done.3
  51.9 1.4 constant_dynamic-update-slice_fusion.7
  53.3 1.4 constant_dynamic-update-slice_fusion.6
  54.7 1.6 collective-permute-start.8
  57.4 11.2 %convolution_convert_fusion.1 = bf16[1024,1024]{1,0:T(8,128)(2,1)S(1)} fusion(bf16[1024,5120]{1,0:T(8,128)(2,1)S(1)} %shard_map.55, bf16[5120,1024]{1,0:T(8,128)(2,1)S(1)} %constant_dynamic-update-slice_fusion), kind=kOutput, calls=%fused_computation.24 | convolution fusion | flops 10738466816 | bytes 23068672 | tf_op jit(solution)/shard_map/dot_general | solution.py:17
  69.7 10.6 %collective-permute-done.8 = bf16[512,1024]{1,0:T(8,128)(2,1)S(1)} collective-permute-done((bf16[512,1024]{1,0:T(8,128)(2,1)S(1)}, bf16[512,1024]{1,0:T(8,128)(2,1)S(1)}, u32[]{:S(2)}, u32[]{:S(2)}) %collective-permute-start.8) | collective-permute-done | bytes 1048608 | tf_op jit(solution)/shard_map/ppermute | solution.py:21
  82.3 5.6 %collective-permute-start.16 = (bf16[512,1024]{1,0:T(8,128)(2,1)}, bf16[512,1024]{1,0:T(8,128)(2,1)}, u32[]{:S(2)}, u32[]{:S(2)}) collective-permute-start(bf16[512,1024]{1,0:T(8,128)(2,1)} %fusion.51), channel_id=1, source_target_pairs={{0,1},{1,2},{2,3},{4,5},{5,6},{6,7},{8,9},{9,10},{10,11},{12,13},{... | collective-permute-start | bytes 3145736 | tf_op jit(solution)/shard_map/ppermute | solution.py:163
  87.9 1.5 collective-permute-start.11
  89.4 4.5 %collective-permute-done.9 = bf16[256,1024]{1,0:T(8,128)(2,1)S(1)} collective-permute-done((bf16[256,1024]{1,0:T(8,128)(2,1)S(1)}, bf16[256,1024]{1,0:T(8,128)(2,1)S(1)}, u32[]{:S(2)}, u32[]{:S(2)}) %collective-permute-start.9) | collective-permute-done | bytes 524320 | tf_op jit(solution)/shard_map/ppermute | solution.py:21
  93.9 7.8 %collective-permute-done.11 = bf16[256,1024]{1,0:T(8,128)(2,1)S(1)} collective-permute-done((bf16[256,1024]{1,0:T(8,128)(2,1)S(1)}, bf16[256,1024]{1,0:T(8,128)(2,1)S(1)}, u32[]{:S(2)}, u32[]{:S(2)}) %collective-permute-start.11) | collective-permute-done | bytes 524320 | tf_op jit(solution)/shard_map/ppermute | solution.py:21
  106.3 2.4 collective-permute-done.18
  110.8 2.3 constant_dynamic-update-slice_fusion.15
  114.1 2.3 constant_dynamic-update-slice_fusion.13
  117.5 2.5 constant_dynamic-update-slice_fusion.11
  120.0 6.6 %convolution_convert_fusion = bf16[512,3072]{1,0:T(8,128)(2,1)S(1)} fusion(bf16[3072,1024]{1,0:T(8,128)(2,1)} %constant_dynamic-update-slice_fusion.11, bf16[1024,1024]{1,0:T(8,128)(2,1)S(1)} %copy-done.11), kind=kOutput, calls=%fused_computation.14 | convolution fusion | flops 3222798336 | bytes 10485760 | tf_op jit(solution)/shard_map/dot_general | solution.py:17
  129.0 8.5 %collective-permute-start.22 = (bf16[512,512]{1,0:T(8,128)(2,1)S(1)}, bf16[512,512]{1,0:T(8,128)(2,1)S(1)}, u32[]{:S(2)}, u32[]{:S(2)}) collective-permute-start(bf16[512,512]{1,0:T(8,128)(2,1)S(1)} %get-tuple-element.62), channel_id=1, source_target_pairs={{0,1},{4,5},{8,9},{12,13},{16,17},{20,21},{24,25},{28,29}} | collective-permute-start | bytes 1572872 | tf_op jit(solution)/shard_map/ppermute | solution.py:195
  137.7 1.3 constant_dynamic-update-slice_fusion.23
  139.2 1.3 constant_dynamic-update-slice_fusion.21
  140.6 1.3 constant_dynamic-update-slice_fusion.19
  142.0 5.8 %collective-permute-done.22 = bf16[512,512]{1,0:T(8,128)(2,1)S(1)} collective-permute-done((bf16[512,512]{1,0:T(8,128)(2,1)S(1)}, bf16[512,512]{1,0:T(8,128)(2,1)S(1)}, u32[]{:S(2)}, u32[]{:S(2)}) %collective-permute-start.22) | collective-permute-done | bytes 524320 | tf_op jit(solution)/shard_map/ppermute | solution.py:195
  149.0 5.0 %collective-permute-start.24 = (bf16[512,512]{1,0:T(8,128)(2,1)S(1)}, bf16[512,512]{1,0:T(8,128)(2,1)S(1)}, u32[]{:S(2)}, u32[]{:S(2)}) collective-permute-start(bf16[512,512]{1,0:T(8,128)(2,1)S(1)} %get-tuple-element.64), channel_id=1, source_target_pairs={{0,1},{1,2},{4,5},{5,6},{8,9},{9,10},{12,13},{13,14},{16,17},{17,1... | collective-permute-start | bytes 1572872 | tf_op jit(solution)/shard_map/ppermute | solution.py:195
  155.2 4.6 %collective-permute-start.27 = (bf16[512,512]{1,0:T(8,128)(2,1)S(1)}, bf16[512,512]{1,0:T(8,128)(2,1)S(1)}, u32[]{:S(2)}, u32[]{:S(2)}) collective-permute-start(bf16[512,512]{1,0:T(8,128)(2,1)S(1)} %get-tuple-element.70), channel_id=1, source_target_pairs={{0,1},{4,5},{8,9},{12,13},{16,17},{20,21},{24,25},{28,29}} | collective-permute-start | bytes 1572872 | tf_op jit(solution)/shard_map/ppermute | solution.py:195
  160.0 1.3 collective-permute-start.20
  161.3 5.0 %collective-permute-done.24 = bf16[512,512]{1,0:T(8,128)(2,1)S(1)} collective-permute-done((bf16[512,512]{1,0:T(8,128)(2,1)S(1)}, bf16[512,512]{1,0:T(8,128)(2,1)S(1)}, u32[]{:S(2)}, u32[]{:S(2)}) %collective-permute-start.24) | collective-permute-done | bytes 524320 | tf_op jit(solution)/shard_map/ppermute | solution.py:195
  166.9 1.3 collective-permute-start.31
  168.2 6.7 %collective-permute-done.27 = bf16[512,512]{1,0:T(8,128)(2,1)S(1)} collective-permute-done((bf16[512,512]{1,0:T(8,128)(2,1)S(1)}, bf16[512,512]{1,0:T(8,128)(2,1)S(1)}, u32[]{:S(2)}, u32[]{:S(2)}) %collective-permute-start.27) | collective-permute-done | bytes 524320 | tf_op jit(solution)/shard_map/ppermute | solution.py:195
  175.4 4.4 %collective-permute-start.29 = (bf16[512,512]{1,0:T(8,128)(2,1)S(1)}, bf16[512,512]{1,0:T(8,128)(2,1)S(1)}, u32[]{:S(2)}, u32[]{:S(2)}) collective-permute-start(bf16[512,512]{1,0:T(8,128)(2,1)S(1)} %get-tuple-element.72), channel_id=1, source_target_pairs={{0,1},{1,2},{4,5},{5,6},{8,9},{9,10},{12,13},{13,14},{16,17},{17,1... | collective-permute-start | bytes 1572872 | tf_op jit(solution)/shard_map/ppermute | solution.py:195
  181.5 4.4 %collective-permute-start.26 = (bf16[512,512]{1,0:T(8,128)(2,1)S(1)}, bf16[512,512]{1,0:T(8,128)(2,1)S(1)}, u32[]{:S(2)}, u32[]{:S(2)}) collective-permute-start(bf16[512,512]{1,0:T(8,128)(2,1)S(1)} %get-tuple-element.66), channel_id=1, source_target_pairs={{0,1},{1,2},{2,3},{4,5},{5,6},{6,7},{8,9},{9,10},{10,11},{12,13},{... | collective-permute-start | bytes 1572872 | tf_op jit(solution)/shard_map/ppermute | solution.py:195
  187.2 11.0 %collective-permute-done.31 = bf16[512,512]{1,0:T(8,128)(2,1)S(1)} collective-permute-done((bf16[512,512]{1,0:T(8,128)(2,1)S(1)}, bf16[512,512]{1,0:T(8,128)(2,1)S(1)}, u32[]{:S(2)}, u32[]{:S(2)}) %collective-permute-start.31) | collective-permute-done | bytes 524320 | tf_op jit(solution)/shard_map/ppermute | solution.py:196
  199.0 2.5 fusion.24
  203.4 5.4 %collective-permute-start.37 = (bf16[512,512]{1,0:T(8,128)(2,1)S(1)}, bf16[512,512]{1,0:T(8,128)(2,1)}, u32[]{:S(2)}, u32[]{:S(2)}) collective-permute-start(bf16[512,512]{1,0:T(8,128)(2,1)S(1)} %get-tuple-element.82), channel_id=1, source_target_pairs={{0,1},{1,2},{2,3},{4,5},{5,6},{6,7},{8,9},{9,10},{10,11},{12,13},{... | collective-permute-start | bytes 1572872 | tf_op jit(solution)/shard_map/ppermute | solution.py:195
  209.2 2.7 fusion.22
  211.8 2.7 add_convert_fusion.2
  215.4 4.5 %fusion.14 = bf16[2560,512]{1,0:T(8,128)(2,1)} fusion(bf16[1024,5120]{1,0:T(8,128)(2,1)S(1)} %bitcast.82, bf16[512,512]{1,0:T(8,128)(2,1)S(1)} %add_convert_fusion.6, bf16[512,512]{1,0:T(8,128)(2,1)S(1)} %get-tuple-element.128), kind=kOutput, calls=%fused_computation.12 | convolution fusion | flops 2687762432 | bytes 8912896 | tf_op jit(solution)/shard_map/dot_general | solution.py:17
  219.9 1.7 add_convert_fusion.3
  221.7 5.7 %fusion.17 = bf16[2560,512]{1,0:T(8,128)(2,1)S(1)} fusion(bf16[1024,5120]{1,0:T(8,128)(2,1)} %copy-done, bf16[512,512]{1,0:T(8,128)(2,1)S(1)} %add_convert_fusion.3, bf16[512,512]{1,0:T(8,128)(2,1)} %get-tuple-element.127), kind=kOutput, calls=%fused_computation.13 | convolution fusion | flops 2687762432 | bytes 8912896 | tf_op jit(solution)/shard_map/dot_general | solution.py:17
  227.9 3.2 %fusion.8 = bf16[2560,512]{1,0:T(8,128)(2,1)S(1)} fusion(bf16[1024,5120]{1,0:T(8,128)(2,1)S(1)} %bitcast.84, bf16[512,512]{1,0:T(8,128)(2,1)S(1)} %add_convert_fusion.6, bf16[512,512]{1,0:T(8,128)(2,1)S(1)} %copy-done.16), kind=kOutput, calls=%fused_computation.10 | convolution fusion | flops 2687762432 | bytes 8912896 | tf_op jit(solution)/shard_map/dot_general | solution.py:17
  231.1 3.2 %fusion.11 = bf16[2560,512]{1,0:T(8,128)(2,1)S(1)} fusion(bf16[1024,5120]{1,0:T(8,128)(2,1)S(1)} %bitcast.84, bf16[512,512]{1,0:T(8,128)(2,1)S(1)} %add_convert_fusion.3, bf16[512,512]{1,0:T(8,128)(2,1)S(1)} %copy-done.14), kind=kOutput, calls=%fused_computation.11 | convolution fusion | flops 2687762432 | bytes 8912896 | tf_op jit(solution)/shard_map/dot_general | solution.py:17
  234.3 2.5 add_convert_fusion.1
  237.0 1.6 collective-permute-start.33
  238.7 1.6 collective-permute-start.34
  242.5 12.2 %collective-permute-done.33 = bf16[2,640,256]{2,1,0:T(8,128)(2,1)S(1)} collective-permute-done((bf16[2,640,256]{2,1,0:T(8,128)(2,1)S(1)}, bf16[2,640,256]{2,1,0:T(8,128)(2,1)S(1)}, u32[]{:S(2)}, u32[]{:S(2)}) %collective-permute-start.33) | collective-permute-done | bytes 655392 | tf_op jit(solution)/shard_map/ppermute | solution.py:21
  254.7 1.6 collective-permute-done.34
  256.5 1.6 collective-permute-start.35
  258.6 10.1 %collective-permute-done.40 = bf16[2,640,256]{2,1,0:T(8,128)(2,1)S(1)} collective-permute-done((bf16[2,640,256]{2,1,0:T(8,128)(2,1)S(1)}, bf16[2,640,256]{2,1,0:T(8,128)(2,1)S(1)}, u32[]{:S(2)}, u32[]{:S(2)}) %collective-permute-start.40) | collective-permute-done | bytes 655392 | tf_op jit(solution)/shard_map/ppermute | solution.py:21
  268.7 1.6 collective-permute-done.41
  271.4 1.5 collective-permute-start.42
  273.5 3.9 %collective-permute-done.35 = bf16[1,640,256]{2,1,0:T(8,128)(2,1)S(1)} collective-permute-done((bf16[1,640,256]{2,1,0:T(8,128)(2,1)S(1)}, bf16[1,640,256]{2,1,0:T(8,128)(2,1)S(1)}, u32[]{:S(2)}, u32[]{:S(2)}) %collective-permute-start.35) | collective-permute-done | bytes 327712 | tf_op jit(solution)/shard_map/ppermute | solution.py:21
  279.7 3.6 %collective-permute-done.42 = bf16[1,640,256]{2,1,0:T(8,128)(2,1)} collective-permute-done((bf16[1,640,256]{2,1,0:T(8,128)(2,1)}, bf16[1,640,256]{2,1,0:T(8,128)(2,1)}, u32[]{:S(2)}, u32[]{:S(2)}) %collective-permute-start.42) | collective-permute-done | bytes 327712 | tf_op jit(solution)/shard_map/ppermute | solution.py:21
  283.3 2.3 multiply_reduce_fusion
  288.1 1.5 collective-permute-start.47
  289.6 1.5 collective-permute-start.45
  293.2 1.5 collective-permute-done.46
  294.7 12.7 %collective-permute-start.50 = (f32[8,128]{1,0:T(8,128)S(1)}, f32[8,128]{1,0:T(8,128)S(1)}, u32[]{:S(2)}, u32[]{:S(2)}) collective-permute-start(f32[8,128]{1,0:T(8,128)S(1)} %add_add_fusion.1), channel_id=1, source_target_pairs={{0,3},{1,0},{2,1},{3,2},{4,7},{5,4},{6,5},{7,6},{8,11},{9,8},{10,9... | collective-permute-start | bytes 12296 | tf_op jit(solution)/shard_map/ppermute | solution.py:237
  308.7 4.1 %collective-permute-done.48 = f32[8,128]{1,0:T(8,128)S(1)} collective-permute-done((f32[8,128]{1,0:T(8,128)S(1)}, f32[8,128]{1,0:T(8,128)S(1)}, u32[]{:S(2)}, u32[]{:S(2)}) %collective-permute-start.48) | collective-permute-done | bytes 4128 | tf_op jit(solution)/shard_map/ppermute | solution.py:237
  (166 shorter events, 42.3 us)
Async XLA Ops:
  0.0 32.1 %collective-permute-start = (bf16[640,1024]{1,0:T(8,128)(2,1)}, bf16[640,1024]{1,0:T(8,128)(2,1)}, u32[]{:S(2)}, u32[]{:S(2)}) collective-permute-start(bf16[640,1024]{1,0:T(8,128)(2,1)} %param.8), channel_id=1, source_target_pairs={{0,8},{4,12},{8,0},{12,4},{16,24},{20,28},{24,16},{28,20},{1,9},{5... | collective-permute-start | bytes 3932168 | tf_op jit(solution)/shard_map/ppermute | solution.py:21
  3.0 32.1 %collective-permute-start.1 = (bf16[640,1024]{1,0:T(8,128)(2,1)}, bf16[640,1024]{1,0:T(8,128)(2,1)}, u32[]{:S(2)}, u32[]{:S(2)}) collective-permute-start(bf16[640,1024]{1,0:T(8,128)(2,1)} %param.8), channel_id=1, source_target_pairs={{0,16},{4,20},{8,24},{12,28},{16,0},{20,4},{24,8},{28,12},{1,17},{... | collective-permute-start | bytes 3932168 | tf_op jit(solution)/shard_map/ppermute | solution.py:21
  10.2 27.5 %copy-start.8 = (bf16[640,1024]{1,0:T(8,128)(2,1)S(1)}, bf16[640,1024]{1,0:T(8,128)(2,1)}, u32[]{:S(2)}) copy-start(bf16[640,1024]{1,0:T(8,128)(2,1)} %param.8) | copy-start | bytes 3932164
  14.2 43.2 %copy-start = (bf16[1024,5120]{1,0:T(8,128)(2,1)}, bf16[1024,5120]{1,0:T(8,128)(2,1)S(1)}, u32[]{:S(2)}) copy-start(bf16[1024,5120]{1,0:T(8,128)(2,1)S(1)} %shard_map.55) | copy-start | bytes 31457284
  33.2 16.0 %collective-permute-start.2 = (bf16[320,1024]{1,0:T(8,128)(2,1)S(1)}, bf16[320,1024]{1,0:T(8,128)(2,1)S(1)}, u32[]{:S(2)}, u32[]{:S(2)}) collective-permute-start(bf16[320,1024]{1,0:T(8,128)(2,1)S(1)} %slice.131), channel_id=1, source_target_pairs={{0,16},{4,20},{8,24},{12,28},{16,0},{20,4},{24,8},{28,12},{1,17},{... | collective-permute-start | bytes 1966088 | tf_op jit(solution)/shard_map/ppermute | solution.py:21
  36.2 18.5 %copy-start.6 = (bf16[512,1024]{1,0:T(8,128)(2,1)S(1)}, bf16[512,1024]{1,0:T(8,128)(2,1)}, u32[]{:S(2)}) copy-start(bf16[512,1024]{1,0:T(8,128)(2,1)} %param.9) | copy-start | bytes 3145732
  36.2 15.4 %collective-permute-start.3 = (bf16[320,1024]{1,0:T(8,128)(2,1)S(1)}, bf16[320,1024]{1,0:T(8,128)(2,1)S(1)}, u32[]{:S(2)}, u32[]{:S(2)}) collective-permute-start(bf16[320,1024]{1,0:T(8,128)(2,1)S(1)} %slice.132), channel_id=1, source_target_pairs={{0,8},{4,12},{8,0},{12,4},{16,24},{20,28},{24,16},{28,20},{1,9},{5... | collective-permute-start | bytes 1966088 | tf_op jit(solution)/shard_map/ppermute | solution.py:21
  37.7 18.6 %collective-permute-start.4 = (bf16[640,1024]{1,0:T(8,128)(2,1)S(1)}, bf16[640,1024]{1,0:T(8,128)(2,1)S(1)}, u32[]{:S(2)}, u32[]{:S(2)}) collective-permute-start(bf16[640,1024]{1,0:T(8,128)(2,1)S(1)} %copy-done.8), channel_id=1, source_target_pairs={{0,4},{4,0},{8,12},{12,8},{16,20},{20,16},{24,28},{28,24},{1,5},{5... | collective-permute-start | bytes 3932168 | tf_op jit(solution)/shard_map/ppermute | solution.py:21
  37.7 19.3 %collective-permute-start.5 = (bf16[640,1024]{1,0:T(8,128)(2,1)}, bf16[640,1024]{1,0:T(8,128)(2,1)S(1)}, u32[]{:S(2)}, u32[]{:S(2)}) collective-permute-start(bf16[640,1024]{1,0:T(8,128)(2,1)} %collective-permute-done), channel_id=1, source_target_pairs={{0,4},{4,0},{8,12},{12,8},{16,20},{20,16},{24,28},{28,24},{1,5},{5... | collective-permute-start | bytes 3932168 | tf_op jit(solution)/shard_map/ppermute | solution.py:21
  38.2 18.9 %collective-permute-start.6 = (bf16[640,1024]{1,0:T(8,128)(2,1)}, bf16[640,1024]{1,0:T(8,128)(2,1)S(1)}, u32[]{:S(2)}, u32[]{:S(2)}) collective-permute-start(bf16[640,1024]{1,0:T(8,128)(2,1)} %collective-permute-done.1), channel_id=1, source_target_pairs={{0,4},{4,0},{8,12},{12,8},{16,20},{20,16},{24,28},{28,24},{1,5},{5... | collective-permute-start | bytes 3932168 | tf_op jit(solution)/shard_map/ppermute | solution.py:21
  51.7 5.6 %collective-permute-start.7 = (bf16[640,1024]{1,0:T(8,128)(2,1)S(1)}, bf16[640,1024]{1,0:T(8,128)(2,1)S(1)}, u32[]{:S(2)}, u32[]{:S(2)}) collective-permute-start(bf16[640,1024]{1,0:T(8,128)(2,1)S(1)} %pad_maximum_fusion), channel_id=1, source_target_pairs={{0,4},{4,0},{8,12},{12,8},{16,20},{20,16},{24,28},{28,24},{1,5},{5... | collective-permute-start | bytes 3932168 | tf_op jit(solution)/shard_map/ppermute | solution.py:21
  54.7 25.6 %collective-permute-start.8 = (bf16[512,1024]{1,0:T(8,128)(2,1)S(1)}, bf16[512,1024]{1,0:T(8,128)(2,1)S(1)}, u32[]{:S(2)}, u32[]{:S(2)}) collective-permute-start(bf16[512,1024]{1,0:T(8,128)(2,1)S(1)} %copy-done.6), channel_id=1, source_target_pairs={{0,8},{4,12},{8,0},{12,4},{16,24},{20,28},{24,16},{28,20},{1,9},{5... | collective-permute-start | bytes 3145736 | tf_op jit(solution)/shard_map/ppermute | solution.py:21
  56.4 31.5 %collective-permute-start.10 = (bf16[512,1024]{1,0:T(8,128)(2,1)S(1)}, bf16[512,1024]{1,0:T(8,128)(2,1)S(1)}, u32[]{:S(2)}, u32[]{:S(2)}) collective-permute-start(bf16[512,1024]{1,0:T(8,128)(2,1)S(1)} %copy-done.6), channel_id=1, source_target_pairs={{0,16},{4,20},{8,24},{12,28},{16,0},{20,4},{24,8},{28,12},{1,17},{... | collective-permute-start | bytes 3145736 | tf_op jit(solution)/shard_map/ppermute | solution.py:21
  68.6 25.3 %copy-start.10 = (bf16[1024,1024]{1,0:T(8,128)(2,1)}, bf16[1024,1024]{1,0:T(8,128)(2,1)S(1)}, u32[]{:S(2)}) copy-start(bf16[1024,1024]{1,0:T(8,128)(2,1)S(1)} %convolution_convert_fusion.1) | copy-start | bytes 6291460
  80.4 13.5 %collective-permute-start.9 = (bf16[256,1024]{1,0:T(8,128)(2,1)S(1)}, bf16[256,1024]{1,0:T(8,128)(2,1)S(1)}, u32[]{:S(2)}, u32[]{:S(2)}) collective-permute-start(bf16[256,1024]{1,0:T(8,128)(2,1)S(1)} %slice.135), channel_id=1, source_target_pairs={{0,16},{4,20},{8,24},{12,28},{16,0},{20,4},{24,8},{28,12},{1,17},{... | collective-permute-start | bytes 1572872 | tf_op jit(solution)/shard_map/ppermute | solution.py:21
  81.0 24.8 %collective-permute-start.12 = (bf16[512,1024]{1,0:T(8,128)(2,1)S(1)}, bf16[512,1024]{1,0:T(8,128)(2,1)}, u32[]{:S(2)}, u32[]{:S(2)}) collective-permute-start(bf16[512,1024]{1,0:T(8,128)(2,1)S(1)} %copy-done.6), channel_id=1, source_target_pairs={{0,4},{4,0},{8,12},{12,8},{16,20},{20,16},{24,28},{28,24},{1,5},{5... | collective-permute-start | bytes 3145736 | tf_op jit(solution)/shard_map/ppermute | solution.py:21
  81.0 27.8 %collective-permute-start.18 = (bf16[512,1024]{1,0:T(8,128)(2,1)}, bf16[512,1024]{1,0:T(8,128)(2,1)}, u32[]{:S(2)}, u32[]{:S(2)}) collective-permute-start(bf16[512,1024]{1,0:T(8,128)(2,1)} %fusion.51), channel_id=1, source_target_pairs={{3,2},{2,1},{1,0},{7,6},{6,5},{5,4},{11,10},{10,9},{9,8},{15,14},{... | collective-permute-start | bytes 3145736 | tf_op jit(solution)/shard_map/ppermute | solution.py:165
  82.3 27.8 %collective-permute-start.16 = (bf16[512,1024]{1,0:T(8,128)(2,1)}, bf16[512,1024]{1,0:T(8,128)(2,1)}, u32[]{:S(2)}, u32[]{:S(2)}) collective-permute-start(bf16[512,1024]{1,0:T(8,128)(2,1)} %fusion.51), channel_id=1, source_target_pairs={{0,1},{1,2},{2,3},{4,5},{5,6},{6,7},{8,9},{9,10},{10,11},{12,13},{... | collective-permute-start | bytes 3145736 | tf_op jit(solution)/shard_map/ppermute | solution.py:163
  87.9 13.8 %collective-permute-start.11 = (bf16[256,1024]{1,0:T(8,128)(2,1)S(1)}, bf16[256,1024]{1,0:T(8,128)(2,1)S(1)}, u32[]{:S(2)}, u32[]{:S(2)}) collective-permute-start(bf16[256,1024]{1,0:T(8,128)(2,1)S(1)} %slice.136), channel_id=1, source_target_pairs={{0,8},{4,12},{8,0},{12,4},{16,24},{20,28},{24,16},{28,20},{1,9},{5... | collective-permute-start | bytes 1572872 | tf_op jit(solution)/shard_map/ppermute | solution.py:21
  93.9 20.2 %collective-permute-start.13 = (bf16[512,1024]{1,0:T(8,128)(2,1)S(1)}, bf16[512,1024]{1,0:T(8,128)(2,1)}, u32[]{:S(2)}, u32[]{:S(2)}) collective-permute-start(bf16[512,1024]{1,0:T(8,128)(2,1)S(1)} %collective-permute-done.8), channel_id=1, source_target_pairs={{0,4},{4,0},{8,12},{12,8},{16,20},{20,16},{24,28},{28,24},{1,5},{5... | collective-permute-start | bytes 3145736 | tf_op jit(solution)/shard_map/ppermute | solution.py:21
  102.5 15.0 %collective-permute-start.14 = (bf16[512,1024]{1,0:T(8,128)(2,1)S(1)}, bf16[512,1024]{1,0:T(8,128)(2,1)}, u32[]{:S(2)}, u32[]{:S(2)}) collective-permute-start(bf16[512,1024]{1,0:T(8,128)(2,1)S(1)} %collective-permute-done.10), channel_id=1, source_target_pairs={{0,4},{4,0},{8,12},{12,8},{16,20},{20,16},{24,28},{28,24},{1,5},{5... | collective-permute-start | bytes 3145736 | tf_op jit(solution)/shard_map/ppermute | solution.py:21
  105.7 14.3 %copy-start.11 = (bf16[1024,1024]{1,0:T(8,128)(2,1)S(1)}, bf16[1024,1024]{1,0:T(8,128)(2,1)}, u32[]{:S(2)}) copy-start(bf16[1024,1024]{1,0:T(8,128)(2,1)} %copy-done.10) | copy-start | bytes 6291460
  105.8 20.9 %collective-permute-start.15 = (bf16[512,1024]{1,0:T(8,128)(2,1)S(1)}, bf16[512,1024]{1,0:T(8,128)(2,1)S(1)}, u32[]{:S(2)}, u32[]{:S(2)}) collective-permute-start(bf16[512,1024]{1,0:T(8,128)(2,1)S(1)} %constant_dynamic-update-slice_fusion.9), channel_id=1, source_target_pairs={{0,4},{4,0},{8,12},{12,8},{16,20},{20,16},{24,28},{28,24},{1,5},{5... | collective-permute-start | bytes 3145736 | tf_op jit(solution)/shard_map/ppermute | solution.py:21
  108.7 46.5 %collective-permute-start.19 = (bf16[512,1024]{1,0:T(8,128)(2,1)}, bf16[512,1024]{1,0:T(8,128)(2,1)}, u32[]{:S(2)}, u32[]{:S(2)}) collective-permute-start(bf16[512,1024]{1,0:T(8,128)(2,1)} %collective-permute-done.18), channel_id=1, source_target_pairs={{2,1},{1,0},{6,5},{5,4},{10,9},{9,8},{14,13},{13,12},{18,17},{17,1... | collective-permute-start | bytes 3145736 | tf_op jit(solution)/shard_map/ppermute | solution.py:165
  110.0 70.5 %collective-permute-start.17 = (bf16[512,1024]{1,0:T(8,128)(2,1)}, bf16[512,1024]{1,0:T(8,128)(2,1)S(1)}, u32[]{:S(2)}, u32[]{:S(2)}) collective-permute-start(bf16[512,1024]{1,0:T(8,128)(2,1)} %collective-permute-done.16), channel_id=1, source_target_pairs={{1,2},{2,3},{5,6},{6,7},{9,10},{10,11},{13,14},{14,15},{17,18},{18... | collective-permute-start | bytes 3145736 | tf_op jit(solution)/shard_map/ppermute | solution.py:163
  117.5 20.1 %slice-start.6 = ((s8[8388608]{0:T(1024)(128)(4,1)}), s8[4194304]{0:T(1024)(128)(4,1)S(1)}, s32[]{:S(2)}) async-start(s8[8388608]{0:T(1024)(128)(4,1)} %bitcast.85), calls=%async_computation.6 | async-start | bytes 8388608
  120.0 17.6 %slice-start.7 = ((s8[8388608]{0:T(1024)(128)(4,1)}), s8[4194304]{0:T(1024)(128)(4,1)S(1)}, s32[]{:S(2)}) async-start(s8[8388608]{0:T(1024)(128)(4,1)} %bitcast.85), calls=%async_computation.7 | async-start | bytes 8388608
  126.6 82.1 %copy-start.4 = (bf16[512,3072]{1,0:T(8,128)(2,1)}, bf16[512,3072]{1,0:T(8,128)(2,1)S(1)}, u32[]{:S(2)}) copy-start(bf16[512,3072]{1,0:T(8,128)(2,1)S(1)} %convolution_convert_fusion) | copy-start | bytes 9437188
  126.6 11.0 %copy-start.7 = (bf16[512,1024]{1,0:T(8,128)(2,1)S(1)}, bf16[512,1024]{1,0:T(8,128)(2,1)}, u32[]{:S(2)}) copy-start(bf16[512,1024]{1,0:T(8,128)(2,1)} %param.9) | copy-start | bytes 3145732
  128.3 13.7 %collective-permute-start.23 = (bf16[512,512]{1,0:T(8,128)(2,1)S(1)}, bf16[512,512]{1,0:T(8,128)(2,1)S(1)}, u32[]{:S(2)}, u32[]{:S(2)}) collective-permute-start(bf16[512,512]{1,0:T(8,128)(2,1)S(1)} %get-tuple-element.63), channel_id=1, source_target_pairs={{3,2},{7,6},{11,10},{15,14},{19,18},{23,22},{27,26},{31,30}} | collective-permute-start | bytes 1572872 | tf_op jit(solution)/shard_map/ppermute | solution.py:196
  129.0 18.8 %collective-permute-start.22 = (bf16[512,512]{1,0:T(8,128)(2,1)S(1)}, bf16[512,512]{1,0:T(8,128)(2,1)S(1)}, u32[]{:S(2)}, u32[]{:S(2)}) collective-permute-start(bf16[512,512]{1,0:T(8,128)(2,1)S(1)} %get-tuple-element.62), channel_id=1, source_target_pairs={{0,1},{4,5},{8,9},{12,13},{16,17},{20,21},{24,25},{28,29}} | collective-permute-start | bytes 1572872 | tf_op jit(solution)/shard_map/ppermute | solution.py:195
  148.3 11.7 %collective-permute-start.25 = (bf16[512,512]{1,0:T(8,128)(2,1)S(1)}, bf16[512,512]{1,0:T(8,128)(2,1)S(1)}, u32[]{:S(2)}, u32[]{:S(2)}) collective-permute-start(bf16[512,512]{1,0:T(8,128)(2,1)S(1)} %get-tuple-element.65), channel_id=1, source_target_pairs={{3,2},{2,1},{7,6},{6,5},{11,10},{10,9},{15,14},{14,13},{19,18},{18... | collective-permute-start | bytes 1572872 | tf_op jit(solution)/shard_map/ppermute | solution.py:196
  149.0 17.3 %collective-permute-start.24 = (bf16[512,512]{1,0:T(8,128)(2,1)S(1)}, bf16[512,512]{1,0:T(8,128)(2,1)S(1)}, u32[]{:S(2)}, u32[]{:S(2)}) collective-permute-start(bf16[512,512]{1,0:T(8,128)(2,1)S(1)} %get-tuple-element.64), channel_id=1, source_target_pairs={{0,1},{1,2},{4,5},{5,6},{8,9},{9,10},{12,13},{13,14},{16,17},{17,1... | collective-permute-start | bytes 1572872 | tf_op jit(solution)/shard_map/ppermute | solution.py:195
  154.5 13.7 %collective-permute-start.28 = (bf16[512,512]{1,0:T(8,128)(2,1)S(1)}, bf16[512,512]{1,0:T(8,128)(2,1)S(1)}, u32[]{:S(2)}, u32[]{:S(2)}) collective-permute-start(bf16[512,512]{1,0:T(8,128)(2,1)S(1)} %get-tuple-element.71), channel_id=1, source_target_pairs={{3,2},{7,6},{11,10},{15,14},{19,18},{23,22},{27,26},{31,30}} | collective-permute-start | bytes 1572872 | tf_op jit(solution)/shard_map/ppermute | solution.py:196
  155.2 19.7 %collective-permute-start.27 = (bf16[512,512]{1,0:T(8,128)(2,1)S(1)}, bf16[512,512]{1,0:T(8,128)(2,1)S(1)}, u32[]{:S(2)}, u32[]{:S(2)}) collective-permute-start(bf16[512,512]{1,0:T(8,128)(2,1)S(1)} %get-tuple-element.70), channel_id=1, source_target_pairs={{0,1},{4,5},{8,9},{12,13},{16,17},{20,21},{24,25},{28,29}} | collective-permute-start | bytes 1572872 | tf_op jit(solution)/shard_map/ppermute | solution.py:195
  160.0 49.1 %collective-permute-start.20 = (bf16[512,1024]{1,0:T(8,128)(2,1)}, bf16[512,1024]{1,0:T(8,128)(2,1)S(1)}, u32[]{:S(2)}, u32[]{:S(2)}) collective-permute-start(bf16[512,1024]{1,0:T(8,128)(2,1)} %collective-permute-done.19), channel_id=1, source_target_pairs={{1,0},{5,4},{9,8},{13,12},{17,16},{21,20},{25,24},{29,28}} | collective-permute-start | bytes 3145736 | tf_op jit(solution)/shard_map/ppermute | solution.py:165
  166.9 31.4 %collective-permute-start.31 = (bf16[512,512]{1,0:T(8,128)(2,1)S(1)}, bf16[512,512]{1,0:T(8,128)(2,1)S(1)}, u32[]{:S(2)}, u32[]{:S(2)}) collective-permute-start(bf16[512,512]{1,0:T(8,128)(2,1)S(1)} %get-tuple-element.75), channel_id=1, source_target_pairs={{3,2},{2,1},{1,0},{7,6},{6,5},{5,4},{11,10},{10,9},{9,8},{15,14},{... | collective-permute-start | bytes 1572872 | tf_op jit(solution)/shard_map/ppermute | solution.py:196
  175.4 26.0 %collective-permute-start.29 = (bf16[512,512]{1,0:T(8,128)(2,1)S(1)}, bf16[512,512]{1,0:T(8,128)(2,1)S(1)}, u32[]{:S(2)}, u32[]{:S(2)}) collective-permute-start(bf16[512,512]{1,0:T(8,128)(2,1)S(1)} %get-tuple-element.72), channel_id=1, source_target_pairs={{0,1},{1,2},{4,5},{5,6},{8,9},{9,10},{12,13},{13,14},{16,17},{17,1... | collective-permute-start | bytes 1572872 | tf_op jit(solution)/shard_map/ppermute | solution.py:195
  179.9 21.6 %collective-permute-start.30 = (bf16[512,512]{1,0:T(8,128)(2,1)S(1)}, bf16[512,512]{1,0:T(8,128)(2,1)S(1)}, u32[]{:S(2)}, u32[]{:S(2)}) collective-permute-start(bf16[512,512]{1,0:T(8,128)(2,1)S(1)} %get-tuple-element.73), channel_id=1, source_target_pairs={{3,2},{2,1},{7,6},{6,5},{11,10},{10,9},{15,14},{14,13},{19,18},{18... | collective-permute-start | bytes 1572872 | tf_op jit(solution)/shard_map/ppermute | solution.py:196
  181.5 20.0 %collective-permute-start.26 = (bf16[512,512]{1,0:T(8,128)(2,1)S(1)}, bf16[512,512]{1,0:T(8,128)(2,1)S(1)}, u32[]{:S(2)}, u32[]{:S(2)}) collective-permute-start(bf16[512,512]{1,0:T(8,128)(2,1)S(1)} %get-tuple-element.66), channel_id=1, source_target_pairs={{0,1},{1,2},{2,3},{4,5},{5,6},{6,7},{8,9},{9,10},{10,11},{12,13},{... | collective-permute-start | bytes 1572872 | tf_op jit(solution)/shard_map/ppermute | solution.py:195
  186.0 12.3 %copy-start.18 = (bf16[512,1024]{1,0:T(8,128)(2,1)S(1)}, bf16[512,1024]{1,0:T(8,128)(2,1)}, u32[]{:S(2)}) copy-start(bf16[512,1024]{1,0:T(8,128)(2,1)} %copy-done.17) | copy-start | bytes 3145732
  198.2 13.6 %collective-permute-start.21 = (bf16[512,1024]{1,0:T(8,128)(2,1)S(1)}, bf16[512,1024]{1,0:T(8,128)(2,1)S(1)}, u32[]{:S(2)}, u32[]{:S(2)}) collective-permute-start(bf16[512,1024]{1,0:T(8,128)(2,1)S(1)} %copy-done.18), channel_id=1, source_target_pairs={{2,3},{6,7},{10,11},{14,15},{18,19},{22,23},{26,27},{30,31}} | collective-permute-start | bytes 3145736 | tf_op jit(solution)/shard_map/ppermute | solution.py:163
  202.1 17.8 %collective-permute-start.38 = (bf16[512,512]{1,0:T(8,128)(2,1)S(1)}, bf16[512,512]{1,0:T(8,128)(2,1)S(1)}, u32[]{:S(2)}, u32[]{:S(2)}) collective-permute-start(bf16[512,512]{1,0:T(8,128)(2,1)S(1)} %get-tuple-element.83), channel_id=1, source_target_pairs={{3,2},{2,1},{1,0},{7,6},{6,5},{5,4},{11,10},{10,9},{9,8},{15,14},{... | collective-permute-start | bytes 1572872 | tf_op jit(solution)/shard_map/ppermute | solution.py:196
  203.4 16.5 %collective-permute-start.37 = (bf16[512,512]{1,0:T(8,128)(2,1)S(1)}, bf16[512,512]{1,0:T(8,128)(2,1)}, u32[]{:S(2)}, u32[]{:S(2)}) collective-permute-start(bf16[512,512]{1,0:T(8,128)(2,1)S(1)} %get-tuple-element.82), channel_id=1, source_target_pairs={{0,1},{1,2},{2,3},{4,5},{5,6},{6,7},{8,9},{9,10},{10,11},{12,13},{... | collective-permute-start | bytes 1572872 | tf_op jit(solution)/shard_map/ppermute | solution.py:195
  219.9 14.4 %collective-permute-start.32 = (bf16[2560,512]{1,0:T(8,128)(2,1)}, bf16[2560,512]{1,0:T(8,128)(2,1)}, u32[]{:S(2)}, u32[]{:S(2)}) collective-permute-start(bf16[2560,512]{1,0:T(8,128)(2,1)} %fusion.14), channel_id=1, source_target_pairs={{0,4},{4,0},{8,12},{12,8},{16,20},{20,16},{24,28},{28,24},{1,5},{5... | collective-permute-start | bytes 7864328 | tf_op jit(solution)/shard_map/ppermute | solution.py:21
  219.9 8.0 %slice-start.3 = ((s8[10485760]{0:T(1024)(128)(4,1)}), s8[4194304]{0:T(1024)(128)(4,1)S(1)}, s32[]{:S(2)}) async-start(s8[10485760]{0:T(1024)(128)(4,1)} %bitcast.83), calls=%async_computation.3 | async-start | bytes 8388608
  227.3 12.9 %collective-permute-start.39 = (bf16[2560,512]{1,0:T(8,128)(2,1)S(1)}, bf16[2560,512]{1,0:T(8,128)(2,1)S(1)}, u32[]{:S(2)}, u32[]{:S(2)}) collective-permute-start(bf16[2560,512]{1,0:T(8,128)(2,1)S(1)} %fusion.17), channel_id=1, source_target_pairs={{0,4},{4,0},{8,12},{12,8},{16,20},{20,16},{24,28},{28,24},{1,5},{5... | collective-permute-start | bytes 7864328 | tf_op jit(solution)/shard_map/ppermute | solution.py:21
  237.0 17.7 %collective-permute-start.33 = (bf16[2,640,256]{2,1,0:T(8,128)(2,1)S(1)}, bf16[2,640,256]{2,1,0:T(8,128)(2,1)S(1)}, u32[]{:S(2)}, u32[]{:S(2)}) collective-permute-start(bf16[2,640,256]{2,1,0:T(8,128)(2,1)S(1)} %pad_maximum_fusion.3), channel_id=1, source_target_pairs={{0,8},{4,12},{8,0},{12,4},{16,24},{20,28},{24,16},{28,20},{1,9},{5... | collective-permute-start | bytes 1966088 | tf_op jit(solution)/shard_map/ppermute | solution.py:21
  238.7 17.7 %collective-permute-start.34 = (bf16[2,640,256]{2,1,0:T(8,128)(2,1)S(1)}, bf16[2,640,256]{2,1,0:T(8,128)(2,1)S(1)}, u32[]{:S(2)}, u32[]{:S(2)}) collective-permute-start(bf16[2,640,256]{2,1,0:T(8,128)(2,1)S(1)} %pad_maximum_fusion.4), channel_id=1, source_target_pairs={{0,16},{4,20},{8,24},{12,28},{16,0},{20,4},{24,8},{28,12},{1,17},{... | collective-permute-start | bytes 1966088 | tf_op jit(solution)/shard_map/ppermute | solution.py:21
  241.1 37.4 %copy-start.5 = (bf16[2560,512]{1,0:T(8,128)(2,1)}, bf16[2560,512]{1,0:T(8,128)(2,1)S(1)}, u32[]{:S(2)}) copy-start(bf16[2560,512]{1,0:T(8,128)(2,1)S(1)} %add_convert_fusion) | copy-start | bytes 7864324
  241.3 27.5 %collective-permute-start.40 = (bf16[2,640,256]{2,1,0:T(8,128)(2,1)S(1)}, bf16[2,640,256]{2,1,0:T(8,128)(2,1)S(1)}, u32[]{:S(2)}, u32[]{:S(2)}) collective-permute-start(bf16[2,640,256]{2,1,0:T(8,128)(2,1)S(1)} %pad_maximum_fusion.5), channel_id=1, source_target_pairs={{0,8},{4,12},{8,0},{12,4},{16,24},{20,28},{24,16},{28,20},{1,9},{5... | collective-permute-start | bytes 1966088 | tf_op jit(solution)/shard_map/ppermute | solution.py:21
  242.0 28.4 %collective-permute-start.41 = (bf16[2,640,256]{2,1,0:T(8,128)(2,1)S(1)}, bf16[2,640,256]{2,1,0:T(8,128)(2,1)S(1)}, u32[]{:S(2)}, u32[]{:S(2)}) collective-permute-start(bf16[2,640,256]{2,1,0:T(8,128)(2,1)S(1)} %pad_maximum_fusion.6), channel_id=1, source_target_pairs={{0,16},{4,20},{8,24},{12,28},{16,0},{20,4},{24,8},{28,12},{1,17},{... | collective-permute-start | bytes 1966088 | tf_op jit(solution)/shard_map/ppermute | solution.py:21
  256.5 20.9 %collective-permute-start.35 = (bf16[1,640,256]{2,1,0:T(8,128)(2,1)S(1)}, bf16[1,640,256]{2,1,0:T(8,128)(2,1)S(1)}, u32[]{:S(2)}, u32[]{:S(2)}) collective-permute-start(bf16[1,640,256]{2,1,0:T(8,128)(2,1)S(1)} %get-tuple-element.120), channel_id=1, source_target_pairs={{0,16},{4,20},{8,24},{12,28},{16,0},{20,4},{24,8},{28,12},{1,17},{... | collective-permute-start | bytes 983048 | tf_op jit(solution)/shard_map/ppermute | solution.py:21
  258.1 19.3 %collective-permute-start.36 = (bf16[1,640,256]{2,1,0:T(8,128)(2,1)S(1)}, bf16[1,640,256]{2,1,0:T(8,128)(2,1)S(1)}, u32[]{:S(2)}, u32[]{:S(2)}) collective-permute-start(bf16[1,640,256]{2,1,0:T(8,128)(2,1)S(1)} %get-tuple-element.119), channel_id=1, source_target_pairs={{0,8},{4,12},{8,0},{12,4},{16,24},{20,28},{24,16},{28,20},{1,9},{5... | collective-permute-start | bytes 983048 | tf_op jit(solution)/shard_map/ppermute | solution.py:21
  270.4 12.9 %copy-start.9 = (bf16[2,640,256]{2,1,0:T(8,128)(2,1)}, bf16[2,640,256]{2,1,0:T(8,128)(2,1)S(1)}, u32[]{:S(2)}) copy-start(bf16[2,640,256]{2,1,0:T(8,128)(2,1)S(1)} %collective-permute-done.41) | copy-start | bytes 1966084
  271.4 11.9 %collective-permute-start.42 = (bf16[1,640,256]{2,1,0:T(8,128)(2,1)}, bf16[1,640,256]{2,1,0:T(8,128)(2,1)}, u32[]{:S(2)}, u32[]{:S(2)}) collective-permute-start(bf16[1,640,256]{2,1,0:T(8,128)(2,1)} %get-tuple-element.112), channel_id=1, source_target_pairs={{0,16},{4,20},{8,24},{12,28},{16,0},{20,4},{24,8},{28,12},{1,17},{... | collective-permute-start | bytes 983048 | tf_op jit(solution)/shard_map/ppermute | solution.py:21
  272.9 10.4 %collective-permute-start.43 = (bf16[1,640,256]{2,1,0:T(8,128)(2,1)}, bf16[1,640,256]{2,1,0:T(8,128)(2,1)}, u32[]{:S(2)}, u32[]{:S(2)}) collective-permute-start(bf16[1,640,256]{2,1,0:T(8,128)(2,1)} %get-tuple-element.111), channel_id=1, source_target_pairs={{0,8},{4,12},{8,0},{12,4},{16,24},{20,28},{24,16},{28,20},{1,9},{5... | collective-permute-start | bytes 983048 | tf_op jit(solution)/shard_map/ppermute | solution.py:21
  286.9 1.2 collective-permute-start.44
  288.1 4.5 %collective-permute-start.47 = (f32[8,128]{1,0:T(8,128)S(1)}, f32[8,128]{1,0:T(8,128)S(1)}, u32[]{:S(2)}, u32[]{:S(2)}) collective-permute-start(f32[8,128]{1,0:T(8,128)S(1)} %broadcast_add_fusion), channel_id=1, source_target_pairs={{0,24},{4,28},{8,16},{12,20},{16,8},{20,12},{24,0},{28,4},{1,25},{... | collective-permute-start | bytes 12296 | tf_op jit(solution)/shard_map/ppermute | solution.py:21
  289.6 3.6 %collective-permute-start.45 = (f32[8,128]{1,0:T(8,128)S(1)}, f32[8,128]{1,0:T(8,128)S(1)}, u32[]{:S(2)}, u32[]{:S(2)}) collective-permute-start(f32[8,128]{1,0:T(8,128)S(1)} %broadcast_add_fusion), channel_id=1, source_target_pairs={{0,8},{4,12},{8,0},{12,4},{16,24},{20,28},{24,16},{28,20},{1,9},{5... | collective-permute-start | bytes 12296 | tf_op jit(solution)/shard_map/ppermute | solution.py:21
  291.1 3.6 %collective-permute-start.46 = (f32[8,128]{1,0:T(8,128)S(1)}, f32[8,128]{1,0:T(8,128)S(1)}, u32[]{:S(2)}, u32[]{:S(2)}) collective-permute-start(f32[8,128]{1,0:T(8,128)S(1)} %broadcast_add_fusion), channel_id=1, source_target_pairs={{0,16},{4,20},{8,24},{12,28},{16,0},{20,4},{24,8},{28,12},{1,17},{... | collective-permute-start | bytes 12296 | tf_op jit(solution)/shard_map/ppermute | solution.py:21
  294.7 14.0 %collective-permute-start.50 = (f32[8,128]{1,0:T(8,128)S(1)}, f32[8,128]{1,0:T(8,128)S(1)}, u32[]{:S(2)}, u32[]{:S(2)}) collective-permute-start(f32[8,128]{1,0:T(8,128)S(1)} %add_add_fusion.1), channel_id=1, source_target_pairs={{0,3},{1,0},{2,1},{3,2},{4,7},{5,4},{6,5},{7,6},{8,11},{9,8},{10,9... | collective-permute-start | bytes 12296 | tf_op jit(solution)/shard_map/ppermute | solution.py:237
  307.4 5.4 %collective-permute-start.48 = (f32[8,128]{1,0:T(8,128)S(1)}, f32[8,128]{1,0:T(8,128)S(1)}, u32[]{:S(2)}, u32[]{:S(2)}) collective-permute-start(f32[8,128]{1,0:T(8,128)S(1)} %add_add_fusion.1), channel_id=1, source_target_pairs={{0,1},{1,2},{2,3},{3,0},{4,5},{5,6},{6,7},{7,4},{8,9},{9,10},{10,1... | collective-permute-start | bytes 12296 | tf_op jit(solution)/shard_map/ppermute | solution.py:237
  307.4 5.4 %collective-permute-start.49 = (f32[8,128]{1,0:T(8,128)S(1)}, f32[8,128]{1,0:T(8,128)S(1)}, u32[]{:S(2)}, u32[]{:S(2)}) collective-permute-start(f32[8,128]{1,0:T(8,128)S(1)} %add_add_fusion.1), channel_id=1, source_target_pairs={{0,2},{1,3},{2,0},{3,1},{4,6},{5,7},{6,4},{7,5},{8,10},{9,11},{10,... | collective-permute-start | bytes 12296 | tf_op jit(solution)/shard_map/ppermute | solution.py:237
  (14 other events, 58.4 us)

commit v4 on v2

--- a/solution.py
+++ b/solution.py
@@ -149,15 +149,29 @@
     def place(c, owner):
         return me ^ (jnp.clip(owner, 0, last) * chunks + c)
 
-    from_low, from_high = [back], [back]
+    def trade(value, pairs, parity):
+        pairs = [pair for pair in pairs if min(pair) % 2 == parity]
+        return lax.ppermute(value, "tp", pairs) if pairs else None
+
+    def add(*terms):
+        terms = [term for term in terms if term is not None]
+        return functools.reduce(lambda one, two: one + two, terms) if terms else None
+
+    evens, odds = [back], [back]
     for hop in range(last):
         pairs = [(i, i + 1) for i in range(hop, last)]
-        from_low.append(lax.ppermute(from_low[-1], "tp", pairs))
-        pairs = [(last - i, last - 1 - i) for i in range(hop, last)]
-        from_high.append(lax.ppermute(from_high[-1], "tp", pairs))
+        pairs += [(last - one, last - two) for one, two in pairs]
+        even = trade(odds[-1], pairs, 0)
+        odd_ = trade(evens[-1], pairs, 1)
+        evens.append(even)
+        odds.append(odd_)
+
     delta = None
     for hop in sorted(range(n_tp), key=lambda hop: max(hop, n_tp - hop) if hop else 0):
-        piece = from_low[hop] + from_high[n_tp - hop] if hop else back
+        piece = back
+        if hop:
+            below, above = add(evens[hop], odds[n_tp - hop]), add(odds[hop], evens[n_tp - hop])
+            piece = jnp.where(at % 2 == 1, below, above)
         owner = lax.rem(at - hop + n_tp, n_tp)
         block = lax.dynamic_slice_in_dim(r_all, (me // 2 ^ owner) * width, width, axis=0)
         part = dot(piece, block, (1, 0))
@@ -175,28 +189,30 @@
     sums, own = [], []
     for c in range(chunks):
         if c:
-            products = lax.optimization_barrier(products + sums[-1][0])[:3]
-        up = down = None
+            products = lax.optimization_barrier(products + (sums[-1][0][0],))[:3]
+        even = odd_ = None
         hops = []
         for hop in range(1, n_tp):
-            send_up, send_down = (partial(products, c, at + k) for k in (n_tp - hop, hop - n_tp))
-            if up is not None:
-                send_up, send_down = send_up + up, send_down + down
-            send_up, send_down = send_up.astype(BF), send_down.astype(BF)
-            send_up, send_down = lax.optimization_barrier((send_up, send_down))
-            up = lax.ppermute(send_up, "tp", [(i, i + 1) for i in range(hop)])
-            down = lax.ppermute(send_down, "tp", [(last - i, last - 1 - i) for i in range(hop)])
-            hops.append((up, down))
+            pairs = [(i, i + 1) for i in range(hop)]
+            pairs += [(last - one, last - two) for one, two in pairs]
+            ends = (at + n_tp - hop, at + hop - n_tp)
+            up_even = at % 2 == 0
+            to_even = add(partial(products, c, jnp.where(up_even, *ends)), odd_).astype(BF)
+            to_odd = add(partial(products, c, jnp.where(up_even, *ends[::-1])), even).astype(BF)
+            to_even, to_odd = lax.optimization_barrier((to_even, to_odd))
+            even = trade(to_even, pairs, 0)
+            odd_ = trade(to_odd, pairs, 1)
+            hops.append([x for x in (even, odd_) if x is not None])
         sums.append(hops)
         own.append(partial(products, c, at).astype(BF))
 
     squares = jnp.zeros((), F32)
     pieces = []
     for c in range(chunks):
-        up, down = sums[c][-1]
+        parts = sums[c][-1]
         if c + 1 < chunks:
-            up, down = after(up, *sums[c + 1][-2]), after(down, *sums[c + 1][-2])
-        proxy_out = (own[c].astype(F32) + up.astype(F32) + down.astype(F32)).astype(BF)
+            parts = [after(part, *sums[c + 1][-2]) for part in parts]
+        proxy_out = add(own[c].astype(F32), *[part.astype(F32) for part in parts]).astype(BF)
         values = jnp.concatenate([delta[:, c * depth : (c + 1) * depth], proxy_out], axis=0)
 
         send = dot(both[:, split:], values, (0, 0)).astype(BF)

time: 301 us -> 306 us (1.017)
  waiting for transfers between devices: 132 us -> 122 us
  starting transfers between devices: 78.9 us -> 87.1 us
  other arithmetic: 13.3 us -> 20.4 us
    ppermute x18 -> x15, starting transfers between devices: 49.2 us -> 59.2 us  [trade(): return lax.ppermute(value, 'tp', pairs) if pairs else None]
    ppermute x18 -> x15, waiting for transfers between devices: 37.7 us -> 31 us  [trade(): return lax.ppermute(value, 'tp', pairs) if pairs else None]
    convert_element_type x6, other arithmetic: 5.53 us -> 9.42 us  [the longest x4 7.17 us: per_device(): add(partial(products, c, jnp.where(up_even, *ends[::-1])), even).astype(BF)]
    ppermute x3, starting transfers between devices: 6.86 us -> 3.1 us  [per_device(): lax.ppermute(total, 'tp', [(i, (i + k) % n_tp) for i in range(n_tp)])]
    ppermute x30, waiting for transfers between devices: 89.8 us -> 86.7 us  [flip(): return lax.ppermute(value, axis, [(i, i ^ bit) for i in range(size)])]
    unnamed x63 -> x61, local copies, waits for them, and re-layouts: 9.57 us -> 8.26 us
  transfers between devices with their start and end apart: 51 -> 48, of which waited for: 22 -> 24; matrix products, arithmetic and copies ran while one was open for 24% -> 26% of each run, Pallas kernels for 1% -> 1%
where the time goes in v4:
time: 306 us; the launch traced here: 305 us
  waiting for transfers between devices  122 us (40%)
  starting transfers between devices  87.1 us (28%)
  matrix products  44.1 us (14%)
  local copies, waits for them, and re-layouts  22.8 us (7%)
  other arithmetic  20.4 us (7%)
  Pallas kernels  5.27 us (2%)
  between operations  3.31 us (1%)
    ppermute x30, waiting for transfers between devices, flip(): return lax.ppermute(value, axis, [(i, i ^ bit) for i in range(size)])  86.7 us
    ppermute x15, starting transfers between devices, trade(): return lax.ppermute(value, 'tp', pairs) if pairs else None  59.2 us
    dot_general x12, matrix products, dot(): lax.dot_general(left, right, ((dims[:1], dims[1:]), ((), ())), preferred_...  44.1 us
    ppermute x15, waiting for transfers between devices, trade(): return lax.ppermute(value, 'tp', pairs) if pairs else None  31 us
    ppermute x30, starting transfers between devices, flip(): return lax.ppermute(value, axis, [(i, i ^ bit) for i in range(size)])  24.9 us
    unnamed x61, local copies, waits for them, and re-layouts  8.26 us
    convert_element_type x4, other arithmetic, per_device(): add(partial(products, c, jnp.where(up_even, *ends[::-1])), even).astype(BF)  7.17 us
  transfers between devices with their start and end apart: 48, of which 24 were waited for; matrix products, arithmetic and copies ran while one was open for 26% of the time, Pallas kernels for 1%

profile of v4, /device:TPU:0, one launch (start us, length us, event | category | flops | bytes accessed | tf_op | source)
XLA Modules:
  0.0 305.5 jit_solution(7993108051747332678)
XLA Ops:
  0.0 3.0 collective-permute-start
  3.0 1.5 collective-permute-start.1
  4.6 2.5 copy-done.1
  7.1 2.5 copy-done.2
  10.2 4.0 %shard_map.55 = bf16[1024,5120]{1,0:T(8,128)(2,1)S(1)} custom-call(s32[8]{0:T(128)S(1)} %stack.83.places, s32[2]{0:T(128)S(1)} %copy-done.3, bf16[512,5120]{1,0:T(8,128)(2,1)S(1)} %copy-done.1, bf16[512,5120]{1,0:T(8,128)(2,1)S(1)} %copy-done.2), custom_call_target="tpu_custom_call" | custom-call | bytes 20971520 | tf_op jit(solution)/shard_map/pallas_call | solution.py:74
  14.2 17.7 %collective-permute-done = bf16[640,1024]{1,0:T(8,128)(2,1)S(1)} collective-permute-done((bf16[640,1024]{1,0:T(8,128)(2,1)}, bf16[640,1024]{1,0:T(8,128)(2,1)S(1)}, u32[]{:S(2)}, u32[]{:S(2)}) %collective-permute-start) | collective-permute-done | bytes 1310752 | tf_op jit(solution)/shard_map/ppermute | solution.py:21
  32.0 1.8 collective-permute-start.2
  33.9 1.6 collective-permute-start.3
  36.0 12.0 %collective-permute-done.2 = bf16[320,1024]{1,0:T(8,128)(2,1)S(1)} collective-permute-done((bf16[320,1024]{1,0:T(8,128)(2,1)S(1)}, bf16[320,1024]{1,0:T(8,128)(2,1)S(1)}, u32[]{:S(2)}, u32[]{:S(2)}) %collective-permute-start.2) | collective-permute-done | bytes 655392 | tf_op jit(solution)/shard_map/ppermute | solution.py:21
  48.0 1.3 collective-permute-done.3
  49.8 1.6 collective-permute-start.9
  52.6 11.2 %convolution_convert_fusion = bf16[1024,1024]{1,0:T(8,128)(2,1)S(1)} fusion(bf16[1024,5120]{1,0:T(8,128)(2,1)S(1)} %shard_map.55, bf16[5120,1024]{1,0:T(8,128)(2,1)S(1)} %constant_dynamic-update-slice_fusion), kind=kOutput, calls=%fused_computation.26 | convolution fusion | flops 10738466816 | bytes 23068672 | tf_op jit(solution)/shard_map/dot_general | solution.py:17
  65.0 10.7 %collective-permute-done.9 = bf16[512,1024]{1,0:T(8,128)(2,1)} collective-permute-done((bf16[512,1024]{1,0:T(8,128)(2,1)}, bf16[512,1024]{1,0:T(8,128)(2,1)}, u32[]{:S(2)}, u32[]{:S(2)}) %collective-permute-start.9) | collective-permute-done | bytes 1048608 | tf_op jit(solution)/shard_map/ppermute | solution.py:21
  78.0 1.9 slice.139
  82.0 1.3 constant_dynamic-update-slice_fusion.18
  83.4 7.0 %collective-permute-done.13 = bf16[256,1024]{1,0:T(8,128)(2,1)S(1)} collective-permute-done((bf16[256,1024]{1,0:T(8,128)(2,1)S(1)}, bf16[256,1024]{1,0:T(8,128)(2,1)S(1)}, u32[]{:S(2)}, u32[]{:S(2)}) %collective-permute-start.13) | collective-permute-done | bytes 524320 | tf_op jit(solution)/shard_map/ppermute | solution.py:21
  91.1 1.6 collective-permute-start.18
  95.8 1.5 constant_dynamic-update-slice_fusion.16
  97.4 1.3 constant_dynamic-update-slice_fusion.14
  98.8 1.3 constant_dynamic-update-slice_fusion.13
  100.1 3.7 %fusion.22 = bf16[512,3072]{1,0:T(8,128)(2,1)S(1)} fusion(bf16[4096,1024]{1,0:T(8,128)(2,1)S(1)} %constant_dynamic-update-slice_fusion.13, bf16[1024,1024]{1,0:T(8,128)(2,1)S(1)} %copy-done.17), kind=kOutput, calls=%fused_computation.16 | convolution fusion | flops 3222798336 | bytes 10485760 | tf_op jit(solution)/shard_map/dot_general | solution.py:17
  104.6 1.9 select_select_fusion.2
  106.5 4.3 %collective-permute-start.21 = (bf16[512,512]{1,0:T(8,128)(2,1)}, bf16[512,512]{1,0:T(8,128)(2,1)}, u32[]{:S(2)}, u32[]{:S(2)}) collective-permute-start(bf16[512,512]{1,0:T(8,128)(2,1)} %get-tuple-element.83), channel_id=1, source_target_pairs={{0,1},{3,2},{4,5},{7,6},{8,9},{11,10},{12,13},{15,14},{16,17},{19,... | collective-permute-start | bytes 1572872 | tf_op jit(solution)/shard_map/ppermute | solution.py:154
  110.8 5.8 %collective-permute-done.18 = bf16[512,1024]{1,0:T(8,128)(2,1)} collective-permute-done((bf16[512,1024]{1,0:T(8,128)(2,1)}, bf16[512,1024]{1,0:T(8,128)(2,1)}, u32[]{:S(2)}, u32[]{:S(2)}) %collective-permute-start.18) | collective-permute-done | bytes 1048608 | tf_op jit(solution)/shard_map/ppermute | solution.py:154
  117.5 8.2 %collective-permute-done.21 = bf16[512,512]{1,0:T(8,128)(2,1)} collective-permute-done((bf16[512,512]{1,0:T(8,128)(2,1)}, bf16[512,512]{1,0:T(8,128)(2,1)}, u32[]{:S(2)}, u32[]{:S(2)}) %collective-permute-start.21) | collective-permute-done | bytes 524320 | tf_op jit(solution)/shard_map/ppermute | solution.py:154
  125.7 2.3 add_convert_fusion.10
  128.0 5.2 %collective-permute-start.23 = (bf16[512,512]{1,0:T(8,128)(2,1)}, bf16[512,512]{1,0:T(8,128)(2,1)}, u32[]{:S(2)}, u32[]{:S(2)}) collective-permute-start(bf16[512,512]{1,0:T(8,128)(2,1)} %get-tuple-element.47), channel_id=1, source_target_pairs={{0,1},{3,2},{4,5},{7,6},{8,9},{11,10},{12,13},{15,14},{16,17},{19,... | collective-permute-start | bytes 1572872 | tf_op jit(solution)/shard_map/ppermute | solution.py:154
  133.2 1.5 collective-permute-start.22
  134.7 1.6 collective-permute-start.16
  136.3 2.5 select_select_fusion
  138.8 4.0 %collective-permute-start.25 = (bf16[512,512]{1,0:T(8,128)(2,1)}, bf16[512,512]{1,0:T(8,128)(2,1)}, u32[]{:S(2)}, u32[]{:S(2)}) collective-permute-start(bf16[512,512]{1,0:T(8,128)(2,1)} %get-tuple-element.79), channel_id=1, source_target_pairs={{0,1},{3,2},{4,5},{7,6},{8,9},{11,10},{12,13},{15,14},{16,17},{19,... | collective-permute-start | bytes 1572872 | tf_op jit(solution)/shard_map/ppermute | solution.py:154
  142.9 1.6 collective-permute-start.20
  144.5 2.0 add_convert_fusion.8
  147.3 6.0 %collective-permute-done.25 = bf16[512,512]{1,0:T(8,128)(2,1)} collective-permute-done((bf16[512,512]{1,0:T(8,128)(2,1)}, bf16[512,512]{1,0:T(8,128)(2,1)}, u32[]{:S(2)}, u32[]{:S(2)}) %collective-permute-start.25) | collective-permute-done | bytes 524320 | tf_op jit(solution)/shard_map/ppermute | solution.py:154
  153.3 1.4 add_convert_fusion.7
  154.7 12.8 %collective-permute-start.26 = (bf16[512,512]{1,0:T(8,128)(2,1)S(1)}, bf16[512,512]{1,0:T(8,128)(2,1)S(1)}, u32[]{:S(2)}, u32[]{:S(2)}) collective-permute-start(bf16[512,512]{1,0:T(8,128)(2,1)S(1)} %copy-done.13), channel_id=1, source_target_pairs={{0,1},{3,2},{4,5},{7,6},{8,9},{11,10},{12,13},{15,14},{16,17},{19,... | collective-permute-start | bytes 1572872 | tf_op jit(solution)/shard_map/ppermute | solution.py:154
  168.2 12.8 %collective-permute-start.24 = (bf16[512,512]{1,0:T(8,128)(2,1)S(1)}, bf16[512,512]{1,0:T(8,128)(2,1)S(1)}, u32[]{:S(2)}, u32[]{:S(2)}) collective-permute-start(bf16[512,512]{1,0:T(8,128)(2,1)S(1)} %get-tuple-element.48), channel_id=1, source_target_pairs={{0,1},{2,3},{3,2},{1,0},{4,5},{6,7},{7,6},{5,4},{8,9},{10,11},{11,... | collective-permute-start | bytes 1572872 | tf_op jit(solution)/shard_map/ppermute | solution.py:154
  183.1 3.0 fusion.31
  186.1 1.3 collective-permute-start.17
  187.4 4.4 %collective-permute-done.24 = bf16[512,512]{1,0:T(8,128)(2,1)S(1)} collective-permute-done((bf16[512,512]{1,0:T(8,128)(2,1)S(1)}, bf16[512,512]{1,0:T(8,128)(2,1)S(1)}, u32[]{:S(2)}, u32[]{:S(2)}) %collective-permute-start.24) | collective-permute-done | bytes 524320 | tf_op jit(solution)/shard_map/ppermute | solution.py:154
  191.8 1.6 add_convert_fusion.4
  193.3 1.5 collective-permute-start.35
  194.8 8.6 %collective-permute-start.34 = (bf16[512,512]{1,0:T(8,128)(2,1)}, bf16[512,512]{1,0:T(8,128)(2,1)}, u32[]{:S(2)}, u32[]{:S(2)}) collective-permute-start(bf16[512,512]{1,0:T(8,128)(2,1)} %get-tuple-element.62), channel_id=1, source_target_pairs={{0,1},{2,3},{3,2},{1,0},{4,5},{6,7},{7,6},{5,4},{8,9},{10,11},{11,... | collective-permute-start | bytes 1572872 | tf_op jit(solution)/shard_map/ppermute | solution.py:154
  203.9 3.0 fusion.25
  206.9 2.6 fusion.27
  209.5 6.7 %collective-permute-done.17 = bf16[512,1024]{1,0:T(8,128)(2,1)S(1)} collective-permute-done((bf16[512,1024]{1,0:T(8,128)(2,1)}, bf16[512,1024]{1,0:T(8,128)(2,1)S(1)}, u32[]{:S(2)}, u32[]{:S(2)}) %collective-permute-start.17) | collective-permute-done | bytes 1048608 | tf_op jit(solution)/shard_map/ppermute | solution.py:154
  216.2 1.3 add_convert_fusion.2
  217.7 4.5 %fusion.16 = bf16[2560,512]{1,0:T(8,128)(2,1)} fusion(bf16[1024,5120]{1,0:T(8,128)(2,1)S(1)} %bitcast.81, bf16[512,512]{1,0:T(8,128)(2,1)S(1)} %add_convert_fusion.6, bf16[512,512]{1,0:T(8,128)(2,1)S(1)} %get-tuple-element.104), kind=kOutput, calls=%fused_computation.14 | convolution fusion | flops 2687762432 | bytes 8912896 | tf_op jit(solution)/shard_map/dot_general | solution.py:17
  222.2 1.9 add_convert_fusion.3
  224.1 5.8 %fusion.19 = bf16[2560,512]{1,0:T(8,128)(2,1)S(1)} fusion(bf16[1024,5120]{1,0:T(8,128)(2,1)} %copy-done, bf16[512,512]{1,0:T(8,128)(2,1)S(1)} %add_convert_fusion.3, bf16[512,512]{1,0:T(8,128)(2,1)S(1)} %get-tuple-element.103), kind=kOutput, calls=%fused_computation.15 | convolution fusion | flops 2687762432 | bytes 8912896 | tf_op jit(solution)/shard_map/dot_general | solution.py:17
  230.5 3.2 %fusion.10 = bf16[2560,512]{1,0:T(8,128)(2,1)S(1)} fusion(bf16[1024,5120]{1,0:T(8,128)(2,1)S(1)} %bitcast.83, bf16[512,512]{1,0:T(8,128)(2,1)S(1)} %copy-done.15, bf16[512,512]{1,0:T(8,128)(2,1)S(1)} %get-tuple-element.104), kind=kOutput, calls=%fused_computation.12 | convolution fusion | flops 2687762432 | bytes 8912896 | tf_op jit(solution)/shard_map/dot_general | solution.py:17
  233.7 3.2 %fusion.13 = bf16[2560,512]{1,0:T(8,128)(2,1)S(1)} fusion(bf16[1024,5120]{1,0:T(8,128)(2,1)S(1)} %bitcast.83, bf16[512,512]{1,0:T(8,128)(2,1)S(1)} %add_convert_fusion.3, bf16[512,512]{1,0:T(8,128)(2,1)S(1)} %get-tuple-element.103), kind=kOutput, calls=%fused_computation.13 | convolution fusion | flops 2687762432 | bytes 8912896 | tf_op jit(solution)/shard_map/dot_general | solution.py:17
  236.9 2.5 add_convert_fusion.1
  239.6 1.6 collective-permute-start.30
  245.1 12.2 %collective-permute-done.30 = bf16[2,640,256]{2,1,0:T(8,128)(2,1)S(1)} collective-permute-done((bf16[2,640,256]{2,1,0:T(8,128)(2,1)S(1)}, bf16[2,640,256]{2,1,0:T(8,128)(2,1)S(1)}, u32[]{:S(2)}, u32[]{:S(2)}) %collective-permute-start.30) | collective-permute-done | bytes 655392 | tf_op jit(solution)/shard_map/ppermute | solution.py:21
  257.3 1.6 collective-permute-done.31
  260.8 10.5 %collective-permute-done.37 = bf16[2,640,256]{2,1,0:T(8,128)(2,1)S(1)} collective-permute-done((bf16[2,640,256]{2,1,0:T(8,128)(2,1)S(1)}, bf16[2,640,256]{2,1,0:T(8,128)(2,1)S(1)}, u32[]{:S(2)}, u32[]{:S(2)}) %collective-permute-start.37) | collective-permute-done | bytes 655392 | tf_op jit(solution)/shard_map/ppermute | solution.py:21
  271.3 1.6 collective-permute-done.38
  275.6 4.3 %collective-permute-done.32 = bf16[1,640,256]{2,1,0:T(8,128)(2,1)S(1)} collective-permute-done((bf16[1,640,256]{2,1,0:T(8,128)(2,1)S(1)}, bf16[1,640,256]{2,1,0:T(8,128)(2,1)S(1)}, u32[]{:S(2)}, u32[]{:S(2)}) %collective-permute-start.32) | collective-permute-done | bytes 327712 | tf_op jit(solution)/shard_map/ppermute | solution.py:21
  282.3 3.6 %collective-permute-done.39 = bf16[1,640,256]{2,1,0:T(8,128)(2,1)} collective-permute-done((bf16[1,640,256]{2,1,0:T(8,128)(2,1)}, bf16[1,640,256]{2,1,0:T(8,128)(2,1)}, u32[]{:S(2)}, u32[]{:S(2)}) %collective-permute-start.39) | collective-permute-done | bytes 327712 | tf_op jit(solution)/shard_map/ppermute | solution.py:21
  285.9 2.3 multiply_reduce_fusion
  292.7 1.5 collective-permute-start.43
  296.3 2.5 collective-permute-start.47
  300.1 4.1 %collective-permute-done.45 = f32[8,128]{1,0:T(8,128)S(1)} collective-permute-done((f32[8,128]{1,0:T(8,128)S(1)}, f32[8,128]{1,0:T(8,128)S(1)}, u32[]{:S(2)}, u32[]{:S(2)}) %collective-permute-start.45) | collective-permute-done | bytes 4128 | tf_op jit(solution)/shard_map/ppermute | solution.py:245
  (151 shorter events, 36.6 us)
Async XLA Ops:
  0.0 32.0 %collective-permute-start = (bf16[640,1024]{1,0:T(8,128)(2,1)}, bf16[640,1024]{1,0:T(8,128)(2,1)S(1)}, u32[]{:S(2)}, u32[]{:S(2)}) collective-permute-start(bf16[640,1024]{1,0:T(8,128)(2,1)} %param.8), channel_id=1, source_target_pairs={{0,8},{4,12},{8,0},{12,4},{16,24},{20,28},{24,16},{28,20},{1,9},{5... | collective-permute-start | bytes 3932168 | tf_op jit(solution)/shard_map/ppermute | solution.py:21
  3.0 30.9 %collective-permute-start.1 = (bf16[640,1024]{1,0:T(8,128)(2,1)}, bf16[640,1024]{1,0:T(8,128)(2,1)S(1)}, u32[]{:S(2)}, u32[]{:S(2)}) collective-permute-start(bf16[640,1024]{1,0:T(8,128)(2,1)} %param.8), channel_id=1, source_target_pairs={{0,16},{4,20},{8,24},{12,28},{16,0},{20,4},{24,8},{28,12},{1,17},{... | collective-permute-start | bytes 3932168 | tf_op jit(solution)/shard_map/ppermute | solution.py:21
  10.2 25.2 %copy-start.9 = (bf16[640,1024]{1,0:T(8,128)(2,1)S(1)}, bf16[640,1024]{1,0:T(8,128)(2,1)}, u32[]{:S(2)}) copy-start(bf16[640,1024]{1,0:T(8,128)(2,1)} %param.8) | copy-start | bytes 3932164
  14.2 38.4 %copy-start = (bf16[1024,5120]{1,0:T(8,128)(2,1)}, bf16[1024,5120]{1,0:T(8,128)(2,1)S(1)}, u32[]{:S(2)}) copy-start(bf16[1024,5120]{1,0:T(8,128)(2,1)S(1)} %shard_map.55) | copy-start | bytes 31457284
  32.0 16.0 %collective-permute-start.2 = (bf16[320,1024]{1,0:T(8,128)(2,1)S(1)}, bf16[320,1024]{1,0:T(8,128)(2,1)S(1)}, u32[]{:S(2)}, u32[]{:S(2)}) collective-permute-start(bf16[320,1024]{1,0:T(8,128)(2,1)S(1)} %slice.134), channel_id=1, source_target_pairs={{0,16},{4,20},{8,24},{12,28},{16,0},{20,4},{24,8},{28,12},{1,17},{... | collective-permute-start | bytes 1966088 | tf_op jit(solution)/shard_map/ppermute | solution.py:21
  33.9 15.4 %collective-permute-start.3 = (bf16[320,1024]{1,0:T(8,128)(2,1)S(1)}, bf16[320,1024]{1,0:T(8,128)(2,1)S(1)}, u32[]{:S(2)}, u32[]{:S(2)}) collective-permute-start(bf16[320,1024]{1,0:T(8,128)(2,1)S(1)} %slice.135), channel_id=1, source_target_pairs={{0,8},{4,12},{8,0},{12,4},{16,24},{20,28},{24,16},{28,20},{1,9},{5... | collective-permute-start | bytes 1966088 | tf_op jit(solution)/shard_map/ppermute | solution.py:21
  35.4 16.0 %collective-permute-start.4 = (bf16[640,1024]{1,0:T(8,128)(2,1)S(1)}, bf16[640,1024]{1,0:T(8,128)(2,1)S(1)}, u32[]{:S(2)}, u32[]{:S(2)}) collective-permute-start(bf16[640,1024]{1,0:T(8,128)(2,1)S(1)} %copy-done.9), channel_id=1, source_target_pairs={{0,4},{4,0},{8,12},{12,8},{16,20},{20,16},{24,28},{28,24},{1,5},{5... | collective-permute-start | bytes 3932168 | tf_op jit(solution)/shard_map/ppermute | solution.py:21
  35.4 16.7 %collective-permute-start.5 = (bf16[640,1024]{1,0:T(8,128)(2,1)S(1)}, bf16[640,1024]{1,0:T(8,128)(2,1)S(1)}, u32[]{:S(2)}, u32[]{:S(2)}) collective-permute-start(bf16[640,1024]{1,0:T(8,128)(2,1)S(1)} %collective-permute-done), channel_id=1, source_target_pairs={{0,4},{4,0},{8,12},{12,8},{16,20},{20,16},{24,28},{28,24},{1,5},{5... | collective-permute-start | bytes 3932168 | tf_op jit(solution)/shard_map/ppermute | solution.py:21
  36.0 16.3 %collective-permute-start.6 = (bf16[640,1024]{1,0:T(8,128)(2,1)S(1)}, bf16[640,1024]{1,0:T(8,128)(2,1)S(1)}, u32[]{:S(2)}, u32[]{:S(2)}) collective-permute-start(bf16[640,1024]{1,0:T(8,128)(2,1)S(1)} %collective-permute-done.1), channel_id=1, source_target_pairs={{0,4},{4,0},{8,12},{12,8},{16,20},{20,16},{24,28},{28,24},{1,5},{5... | collective-permute-start | bytes 3932168 | tf_op jit(solution)/shard_map/ppermute | solution.py:21
  49.4 3.1 %collective-permute-start.7 = (bf16[640,1024]{1,0:T(8,128)(2,1)S(1)}, bf16[640,1024]{1,0:T(8,128)(2,1)S(1)}, u32[]{:S(2)}, u32[]{:S(2)}) collective-permute-start(bf16[640,1024]{1,0:T(8,128)(2,1)S(1)} %pad_maximum_fusion), channel_id=1, source_target_pairs={{0,4},{4,0},{8,12},{12,8},{16,20},{20,16},{24,28},{28,24},{1,5},{5... | collective-permute-start | bytes 3932168 | tf_op jit(solution)/shard_map/ppermute | solution.py:21
  49.8 25.9 %collective-permute-start.9 = (bf16[512,1024]{1,0:T(8,128)(2,1)}, bf16[512,1024]{1,0:T(8,128)(2,1)}, u32[]{:S(2)}, u32[]{:S(2)}) collective-permute-start(bf16[512,1024]{1,0:T(8,128)(2,1)} %param.9), channel_id=1, source_target_pairs={{0,8},{4,12},{8,0},{12,4},{16,24},{20,28},{24,16},{28,20},{1,9},{5... | collective-permute-start | bytes 3145736 | tf_op jit(solution)/shard_map/ppermute | solution.py:21
  51.4 26.5 %collective-permute-start.11 = (bf16[512,1024]{1,0:T(8,128)(2,1)}, bf16[512,1024]{1,0:T(8,128)(2,1)}, u32[]{:S(2)}, u32[]{:S(2)}) collective-permute-start(bf16[512,1024]{1,0:T(8,128)(2,1)} %param.9), channel_id=1, source_target_pairs={{0,16},{4,20},{8,24},{12,28},{16,0},{20,4},{24,8},{28,12},{1,17},{... | collective-permute-start | bytes 3145736 | tf_op jit(solution)/shard_map/ppermute | solution.py:21
  63.8 13.0 %copy-start.16 = (bf16[1024,1024]{1,0:T(8,128)(2,1)}, bf16[1024,1024]{1,0:T(8,128)(2,1)S(1)}, u32[]{:S(2)}) copy-start(bf16[1024,1024]{1,0:T(8,128)(2,1)S(1)} %convolution_convert_fusion) | copy-start | bytes 6291460
  64.9 30.8 %collective-permute-start.8 = (bf16[512,1024]{1,0:T(8,128)(2,1)}, bf16[512,1024]{1,0:T(8,128)(2,1)S(1)}, u32[]{:S(2)}, u32[]{:S(2)}) collective-permute-start(bf16[512,1024]{1,0:T(8,128)(2,1)} %param.9), channel_id=1, source_target_pairs={{0,4},{4,0},{8,12},{12,8},{16,20},{20,16},{24,28},{28,24},{1,5},{5... | collective-permute-start | bytes 3145736 | tf_op jit(solution)/shard_map/ppermute | solution.py:21
  76.8 13.5 %collective-permute-start.13 = (bf16[256,1024]{1,0:T(8,128)(2,1)S(1)}, bf16[256,1024]{1,0:T(8,128)(2,1)S(1)}, u32[]{:S(2)}, u32[]{:S(2)}) collective-permute-start(bf16[256,1024]{1,0:T(8,128)(2,1)S(1)} %slice.138), channel_id=1, source_target_pairs={{0,16},{4,20},{8,24},{12,28},{16,0},{20,4},{24,8},{28,12},{1,17},{... | collective-permute-start | bytes 1572872 | tf_op jit(solution)/shard_map/ppermute | solution.py:21
  78.0 19.3 %collective-permute-start.10 = (bf16[512,1024]{1,0:T(8,128)(2,1)}, bf16[512,1024]{1,0:T(8,128)(2,1)S(1)}, u32[]{:S(2)}, u32[]{:S(2)}) collective-permute-start(bf16[512,1024]{1,0:T(8,128)(2,1)} %collective-permute-done.9), channel_id=1, source_target_pairs={{0,4},{4,0},{8,12},{12,8},{16,20},{20,16},{24,28},{28,24},{1,5},{5... | collective-permute-start | bytes 3145736 | tf_op jit(solution)/shard_map/ppermute | solution.py:21
  79.8 14.7 %collective-permute-start.14 = (bf16[256,1024]{1,0:T(8,128)(2,1)}, bf16[256,1024]{1,0:T(8,128)(2,1)}, u32[]{:S(2)}, u32[]{:S(2)}) collective-permute-start(bf16[256,1024]{1,0:T(8,128)(2,1)} %slice.139), channel_id=1, source_target_pairs={{0,8},{4,12},{8,0},{12,4},{16,24},{20,28},{24,16},{28,20},{1,9},{5... | collective-permute-start | bytes 1572872 | tf_op jit(solution)/shard_map/ppermute | solution.py:21
  80.7 18.0 %collective-permute-start.12 = (bf16[512,1024]{1,0:T(8,128)(2,1)}, bf16[512,1024]{1,0:T(8,128)(2,1)}, u32[]{:S(2)}, u32[]{:S(2)}) collective-permute-start(bf16[512,1024]{1,0:T(8,128)(2,1)} %collective-permute-done.11), channel_id=1, source_target_pairs={{0,4},{4,0},{8,12},{12,8},{16,20},{20,16},{24,28},{28,24},{1,5},{5... | collective-permute-start | bytes 3145736 | tf_op jit(solution)/shard_map/ppermute | solution.py:21
  91.1 25.4 %collective-permute-start.18 = (bf16[512,1024]{1,0:T(8,128)(2,1)}, bf16[512,1024]{1,0:T(8,128)(2,1)}, u32[]{:S(2)}, u32[]{:S(2)}) collective-permute-start(bf16[512,1024]{1,0:T(8,128)(2,1)} %fusion.58), channel_id=1, source_target_pairs={{0,1},{2,3},{3,2},{1,0},{4,5},{6,7},{7,6},{5,4},{8,9},{10,11},{11,... | collective-permute-start | bytes 3145736 | tf_op jit(solution)/shard_map/ppermute | solution.py:154
  95.6 8.3 %collective-permute-start.15 = (bf16[512,1024]{1,0:T(8,128)(2,1)S(1)}, bf16[512,1024]{1,0:T(8,128)(2,1)S(1)}, u32[]{:S(2)}, u32[]{:S(2)}) collective-permute-start(bf16[512,1024]{1,0:T(8,128)(2,1)S(1)} %constant_dynamic-update-slice_fusion.9), channel_id=1, source_target_pairs={{0,4},{4,0},{8,12},{12,8},{16,20},{20,16},{24,28},{28,24},{1,5},{5... | collective-permute-start | bytes 3145736 | tf_op jit(solution)/shard_map/ppermute | solution.py:21
  106.5 19.2 %collective-permute-start.21 = (bf16[512,512]{1,0:T(8,128)(2,1)}, bf16[512,512]{1,0:T(8,128)(2,1)}, u32[]{:S(2)}, u32[]{:S(2)}) collective-permute-start(bf16[512,512]{1,0:T(8,128)(2,1)} %get-tuple-element.83), channel_id=1, source_target_pairs={{0,1},{3,2},{4,5},{7,6},{8,9},{11,10},{12,13},{15,14},{16,17},{19,... | collective-permute-start | bytes 1572872 | tf_op jit(solution)/shard_map/ppermute | solution.py:154
  116.6 26.3 %collective-permute-start.19 = (bf16[512,1024]{1,0:T(8,128)(2,1)}, bf16[512,1024]{1,0:T(8,128)(2,1)S(1)}, u32[]{:S(2)}, u32[]{:S(2)}) collective-permute-start(bf16[512,1024]{1,0:T(8,128)(2,1)} %collective-permute-done.18), channel_id=1, source_target_pairs={{1,2},{2,1},{5,6},{6,5},{9,10},{10,9},{13,14},{14,13},{17,18},{18,... | collective-permute-start | bytes 3145736 | tf_op jit(solution)/shard_map/ppermute | solution.py:154
  128.0 16.5 %collective-permute-start.23 = (bf16[512,512]{1,0:T(8,128)(2,1)}, bf16[512,512]{1,0:T(8,128)(2,1)}, u32[]{:S(2)}, u32[]{:S(2)}) collective-permute-start(bf16[512,512]{1,0:T(8,128)(2,1)} %get-tuple-element.47), channel_id=1, source_target_pairs={{0,1},{3,2},{4,5},{7,6},{8,9},{11,10},{12,13},{15,14},{16,17},{19,... | collective-permute-start | bytes 1572872 | tf_op jit(solution)/shard_map/ppermute | solution.py:154
  133.2 11.3 %collective-permute-start.22 = (bf16[512,512]{1,0:T(8,128)(2,1)}, bf16[512,512]{1,0:T(8,128)(2,1)}, u32[]{:S(2)}, u32[]{:S(2)}) collective-permute-start(bf16[512,512]{1,0:T(8,128)(2,1)} %add_convert_fusion.10), channel_id=1, source_target_pairs={{1,2},{2,1},{5,6},{6,5},{9,10},{10,9},{13,14},{14,13},{17,18},{18,... | collective-permute-start | bytes 1572872 | tf_op jit(solution)/shard_map/ppermute | solution.py:154
  134.7 33.5 %collective-permute-start.16 = (bf16[512,1024]{1,0:T(8,128)(2,1)}, bf16[512,1024]{1,0:T(8,128)(2,1)}, u32[]{:S(2)}, u32[]{:S(2)}) collective-permute-start(bf16[512,1024]{1,0:T(8,128)(2,1)} %fusion.58), channel_id=1, source_target_pairs={{1,2},{2,1},{5,6},{6,5},{9,10},{10,9},{13,14},{14,13},{17,18},{18,... | collective-permute-start | bytes 3145736 | tf_op jit(solution)/shard_map/ppermute | solution.py:154
  138.8 14.4 %collective-permute-start.25 = (bf16[512,512]{1,0:T(8,128)(2,1)}, bf16[512,512]{1,0:T(8,128)(2,1)}, u32[]{:S(2)}, u32[]{:S(2)}) collective-permute-start(bf16[512,512]{1,0:T(8,128)(2,1)} %get-tuple-element.79), channel_id=1, source_target_pairs={{0,1},{3,2},{4,5},{7,6},{8,9},{11,10},{12,13},{15,14},{16,17},{19,... | collective-permute-start | bytes 1572872 | tf_op jit(solution)/shard_map/ppermute | solution.py:154
  142.9 10.4 %copy-start.8 = (bf16[512,3072]{1,0:T(8,128)(2,1)S(1)}, bf16[512,3072]{1,0:T(8,128)(2,1)}, u32[]{:S(2)}) copy-start(bf16[512,3072]{1,0:T(8,128)(2,1)} %copy-done.7) | copy-start | bytes 9437188
  142.9 11.8 %copy-start.13 = (bf16[512,512]{1,0:T(8,128)(2,1)S(1)}, bf16[512,512]{1,0:T(8,128)(2,1)}, u32[]{:S(2)}) copy-start(bf16[512,512]{1,0:T(8,128)(2,1)} %get-tuple-element.52) | copy-start | bytes 1572868
  142.9 39.2 %copy-start.11 = (bf16[512,1024]{1,0:T(8,128)(2,1)S(1)}, bf16[512,1024]{1,0:T(8,128)(2,1)}, u32[]{:S(2)}) copy-start(bf16[512,1024]{1,0:T(8,128)(2,1)} %copy-done.10) | copy-start | bytes 3145732
  142.9 60.9 %collective-permute-start.20 = (bf16[512,1024]{1,0:T(8,128)(2,1)S(1)}, bf16[512,1024]{1,0:T(8,128)(2,1)S(1)}, u32[]{:S(2)}, u32[]{:S(2)}) collective-permute-start(bf16[512,1024]{1,0:T(8,128)(2,1)S(1)} %collective-permute-done.19), channel_id=1, source_target_pairs={{2,3},{1,0},{6,7},{5,4},{10,11},{9,8},{14,15},{13,12},{18,19},{17,... | collective-permute-start | bytes 3145736 | tf_op jit(solution)/shard_map/ppermute | solution.py:154
  146.5 36.6 %copy-start.18 = (bf16[1024,1024]{1,0:T(8,128)(2,1)S(1)}, bf16[1024,1024]{1,0:T(8,128)(2,1)}, u32[]{:S(2)}) copy-start(bf16[1024,1024]{1,0:T(8,128)(2,1)} %copy-done.16) | copy-start | bytes 6291460
  146.5 39.6 %collective-permute-start.28 = (bf16[512,512]{1,0:T(8,128)(2,1)S(1)}, bf16[512,512]{1,0:T(8,128)(2,1)S(1)}, u32[]{:S(2)}, u32[]{:S(2)}) collective-permute-start(bf16[512,512]{1,0:T(8,128)(2,1)S(1)} %get-tuple-element.55), channel_id=1, source_target_pairs={{1,2},{2,1},{5,6},{6,5},{9,10},{10,9},{13,14},{14,13},{17,18},{18,... | collective-permute-start | bytes 1572872 | tf_op jit(solution)/shard_map/ppermute | solution.py:154
  154.7 32.8 %collective-permute-start.26 = (bf16[512,512]{1,0:T(8,128)(2,1)S(1)}, bf16[512,512]{1,0:T(8,128)(2,1)S(1)}, u32[]{:S(2)}, u32[]{:S(2)}) collective-permute-start(bf16[512,512]{1,0:T(8,128)(2,1)S(1)} %copy-done.13), channel_id=1, source_target_pairs={{0,1},{3,2},{4,5},{7,6},{8,9},{11,10},{12,13},{15,14},{16,17},{19,... | collective-permute-start | bytes 1572872 | tf_op jit(solution)/shard_map/ppermute | solution.py:154
  167.5 19.9 %collective-permute-start.27 = (bf16[512,512]{1,0:T(8,128)(2,1)S(1)}, bf16[512,512]{1,0:T(8,128)(2,1)S(1)}, u32[]{:S(2)}, u32[]{:S(2)}) collective-permute-start(bf16[512,512]{1,0:T(8,128)(2,1)S(1)} %add_convert_fusion.7), channel_id=1, source_target_pairs={{1,2},{2,1},{5,6},{6,5},{9,10},{10,9},{13,14},{14,13},{17,18},{18,... | collective-permute-start | bytes 1572872 | tf_op jit(solution)/shard_map/ppermute | solution.py:154
  168.2 23.6 %collective-permute-start.24 = (bf16[512,512]{1,0:T(8,128)(2,1)S(1)}, bf16[512,512]{1,0:T(8,128)(2,1)S(1)}, u32[]{:S(2)}, u32[]{:S(2)}) collective-permute-start(bf16[512,512]{1,0:T(8,128)(2,1)S(1)} %get-tuple-element.48), channel_id=1, source_target_pairs={{0,1},{2,3},{3,2},{1,0},{4,5},{6,7},{7,6},{5,4},{8,9},{10,11},{11,... | collective-permute-start | bytes 1572872 | tf_op jit(solution)/shard_map/ppermute | solution.py:154
  183.1 20.8 %copy-start.5 = (bf16[4096,1024]{1,0:T(8,128)(2,1)S(1)}, bf16[4096,1024]{1,0:T(8,128)(2,1)}, u32[]{:S(2)}) copy-start(bf16[4096,1024]{1,0:T(8,128)(2,1)} %constant_dynamic-update-slice_fusion.11) | copy-start | bytes 25165828
  186.1 30.1 %collective-permute-start.17 = (bf16[512,1024]{1,0:T(8,128)(2,1)}, bf16[512,1024]{1,0:T(8,128)(2,1)S(1)}, u32[]{:S(2)}, u32[]{:S(2)}) collective-permute-start(bf16[512,1024]{1,0:T(8,128)(2,1)} %collective-permute-done.16), channel_id=1, source_target_pairs={{2,3},{1,0},{6,7},{5,4},{10,11},{9,8},{14,15},{13,12},{18,19},{17,... | collective-permute-start | bytes 3145736 | tf_op jit(solution)/shard_map/ppermute | solution.py:154
  193.3 28.8 %collective-permute-start.35 = (bf16[512,512]{1,0:T(8,128)(2,1)}, bf16[512,512]{1,0:T(8,128)(2,1)}, u32[]{:S(2)}, u32[]{:S(2)}) collective-permute-start(bf16[512,512]{1,0:T(8,128)(2,1)} %get-tuple-element.63), channel_id=1, source_target_pairs={{1,2},{2,1},{5,6},{6,5},{9,10},{10,9},{13,14},{14,13},{17,18},{18,... | collective-permute-start | bytes 1572872 | tf_op jit(solution)/shard_map/ppermute | solution.py:154
  194.8 27.4 %collective-permute-start.34 = (bf16[512,512]{1,0:T(8,128)(2,1)}, bf16[512,512]{1,0:T(8,128)(2,1)}, u32[]{:S(2)}, u32[]{:S(2)}) collective-permute-start(bf16[512,512]{1,0:T(8,128)(2,1)} %get-tuple-element.62), channel_id=1, source_target_pairs={{0,1},{2,3},{3,2},{1,0},{4,5},{6,7},{7,6},{5,4},{8,9},{10,11},{11,... | collective-permute-start | bytes 1572872 | tf_op jit(solution)/shard_map/ppermute | solution.py:154
  203.8 13.8 %copy-start.14 = (bf16[512,512]{1,0:T(8,128)(2,1)}, bf16[512,512]{1,0:T(8,128)(2,1)S(1)}, u32[]{:S(2)}) copy-start(bf16[512,512]{1,0:T(8,128)(2,1)S(1)} %add_convert_fusion.6) | copy-start | bytes 1572868
  206.8 10.8 %slice-start = ((s8[10485760]{0:T(1024)(128)(4,1)}), s8[4194304]{0:T(1024)(128)(4,1)S(1)}, s32[]{:S(2)}) async-start(s8[10485760]{0:T(1024)(128)(4,1)} %bitcast.80), calls=%async_computation | async-start | bytes 8388608
  206.9 10.8 %slice-start.1 = ((s8[10485760]{0:T(1024)(128)(4,1)}), s8[4194304]{0:T(1024)(128)(4,1)S(1)}, s32[]{:S(2)}) async-start(s8[10485760]{0:T(1024)(128)(4,1)} %bitcast.80), calls=%async_computation.1 | async-start | bytes 8388608
  209.5 8.1 %slice-start.2 = ((s8[10485760]{0:T(1024)(128)(4,1)}), s8[2097152]{0:T(1024)(128)(4,1)S(1)}, s32[]{:S(2)}) async-start(s8[10485760]{0:T(1024)(128)(4,1)} %bitcast.80), calls=%async_computation.2 | async-start | bytes 4194304
  222.2 14.7 %collective-permute-start.29 = (bf16[2560,512]{1,0:T(8,128)(2,1)}, bf16[2560,512]{1,0:T(8,128)(2,1)}, u32[]{:S(2)}, u32[]{:S(2)}) collective-permute-start(bf16[2560,512]{1,0:T(8,128)(2,1)} %fusion.16), channel_id=1, source_target_pairs={{0,4},{4,0},{8,12},{12,8},{16,20},{20,16},{24,28},{28,24},{1,5},{5... | collective-permute-start | bytes 7864328 | tf_op jit(solution)/shard_map/ppermute | solution.py:21
  222.2 8.3 %slice-start.3 = ((s8[10485760]{0:T(1024)(128)(4,1)}), s8[4194304]{0:T(1024)(128)(4,1)S(1)}, s32[]{:S(2)}) async-start(s8[10485760]{0:T(1024)(128)(4,1)} %bitcast.82), calls=%async_computation.3 | async-start | bytes 8388608
  224.0 6.4 %slice-start.4 = ((s8[10485760]{0:T(1024)(128)(4,1)}), s8[4194304]{0:T(1024)(128)(4,1)S(1)}, s32[]{:S(2)}) async-start(s8[10485760]{0:T(1024)(128)(4,1)} %bitcast.82), calls=%async_computation.4 | async-start | bytes 8388608
  229.9 11.9 %collective-permute-start.36 = (bf16[2560,512]{1,0:T(8,128)(2,1)S(1)}, bf16[2560,512]{1,0:T(8,128)(2,1)S(1)}, u32[]{:S(2)}, u32[]{:S(2)}) collective-permute-start(bf16[2560,512]{1,0:T(8,128)(2,1)S(1)} %fusion.19), channel_id=1, source_target_pairs={{0,4},{4,0},{8,12},{12,8},{16,20},{20,16},{24,28},{28,24},{1,5},{5... | collective-permute-start | bytes 7864328 | tf_op jit(solution)/shard_map/ppermute | solution.py:21
  239.6 17.7 %collective-permute-start.30 = (bf16[2,640,256]{2,1,0:T(8,128)(2,1)S(1)}, bf16[2,640,256]{2,1,0:T(8,128)(2,1)S(1)}, u32[]{:S(2)}, u32[]{:S(2)}) collective-permute-start(bf16[2,640,256]{2,1,0:T(8,128)(2,1)S(1)} %pad_maximum_fusion.3), channel_id=1, source_target_pairs={{0,8},{4,12},{8,0},{12,4},{16,24},{20,28},{24,16},{28,20},{1,9},{5... | collective-permute-start | bytes 1966088 | tf_op jit(solution)/shard_map/ppermute | solution.py:21
  241.2 17.7 %collective-permute-start.31 = (bf16[2,640,256]{2,1,0:T(8,128)(2,1)S(1)}, bf16[2,640,256]{2,1,0:T(8,128)(2,1)S(1)}, u32[]{:S(2)}, u32[]{:S(2)}) collective-permute-start(bf16[2,640,256]{2,1,0:T(8,128)(2,1)S(1)} %pad_maximum_fusion.4), channel_id=1, source_target_pairs={{0,16},{4,20},{8,24},{12,28},{16,0},{20,4},{24,8},{28,12},{1,17},{... | collective-permute-start | bytes 1966088 | tf_op jit(solution)/shard_map/ppermute | solution.py:21
  242.7 31.3 %copy-start.6 = (bf16[2560,512]{1,0:T(8,128)(2,1)}, bf16[2560,512]{1,0:T(8,128)(2,1)S(1)}, u32[]{:S(2)}) copy-start(bf16[2560,512]{1,0:T(8,128)(2,1)S(1)} %add_convert_fusion) | copy-start | bytes 7864324
  242.8 28.5 %collective-permute-start.37 = (bf16[2,640,256]{2,1,0:T(8,128)(2,1)S(1)}, bf16[2,640,256]{2,1,0:T(8,128)(2,1)S(1)}, u32[]{:S(2)}, u32[]{:S(2)}) collective-permute-start(bf16[2,640,256]{2,1,0:T(8,128)(2,1)S(1)} %pad_maximum_fusion.5), channel_id=1, source_target_pairs={{0,8},{4,12},{8,0},{12,4},{16,24},{20,28},{24,16},{28,20},{1,9},{5... | collective-permute-start | bytes 1966088 | tf_op jit(solution)/shard_map/ppermute | solution.py:21
  244.1 28.8 %collective-permute-start.38 = (bf16[2,640,256]{2,1,0:T(8,128)(2,1)S(1)}, bf16[2,640,256]{2,1,0:T(8,128)(2,1)S(1)}, u32[]{:S(2)}, u32[]{:S(2)}) collective-permute-start(bf16[2,640,256]{2,1,0:T(8,128)(2,1)S(1)} %pad_maximum_fusion.6), channel_id=1, source_target_pairs={{0,16},{4,20},{8,24},{12,28},{16,0},{20,4},{24,8},{28,12},{1,17},{... | collective-permute-start | bytes 1966088 | tf_op jit(solution)/shard_map/ppermute | solution.py:21
  259.1 20.9 %collective-permute-start.32 = (bf16[1,640,256]{2,1,0:T(8,128)(2,1)S(1)}, bf16[1,640,256]{2,1,0:T(8,128)(2,1)S(1)}, u32[]{:S(2)}, u32[]{:S(2)}) collective-permute-start(bf16[1,640,256]{2,1,0:T(8,128)(2,1)S(1)} %get-tuple-element.96), channel_id=1, source_target_pairs={{0,16},{4,20},{8,24},{12,28},{16,0},{20,4},{24,8},{28,12},{1,17},{... | collective-permute-start | bytes 983048 | tf_op jit(solution)/shard_map/ppermute | solution.py:21
  259.6 20.3 %collective-permute-start.33 = (bf16[1,640,256]{2,1,0:T(8,128)(2,1)S(1)}, bf16[1,640,256]{2,1,0:T(8,128)(2,1)S(1)}, u32[]{:S(2)}, u32[]{:S(2)}) collective-permute-start(bf16[1,640,256]{2,1,0:T(8,128)(2,1)S(1)} %get-tuple-element.95), channel_id=1, source_target_pairs={{0,8},{4,12},{8,0},{12,4},{16,24},{20,28},{24,16},{28,20},{1,9},{5... | collective-permute-start | bytes 983048 | tf_op jit(solution)/shard_map/ppermute | solution.py:21
  272.9 12.9 %copy-start.12 = (bf16[2,640,256]{2,1,0:T(8,128)(2,1)}, bf16[2,640,256]{2,1,0:T(8,128)(2,1)S(1)}, u32[]{:S(2)}) copy-start(bf16[2,640,256]{2,1,0:T(8,128)(2,1)S(1)} %collective-permute-done.38) | copy-start | bytes 1966084
  274.0 11.9 %collective-permute-start.39 = (bf16[1,640,256]{2,1,0:T(8,128)(2,1)}, bf16[1,640,256]{2,1,0:T(8,128)(2,1)}, u32[]{:S(2)}, u32[]{:S(2)}) collective-permute-start(bf16[1,640,256]{2,1,0:T(8,128)(2,1)} %get-tuple-element.88), channel_id=1, source_target_pairs={{0,16},{4,20},{8,24},{12,28},{16,0},{20,4},{24,8},{28,12},{1,17},{... | collective-permute-start | bytes 983048 | tf_op jit(solution)/shard_map/ppermute | solution.py:21
  274.5 11.4 %collective-permute-start.40 = (bf16[1,640,256]{2,1,0:T(8,128)(2,1)}, bf16[1,640,256]{2,1,0:T(8,128)(2,1)}, u32[]{:S(2)}, u32[]{:S(2)}) collective-permute-start(bf16[1,640,256]{2,1,0:T(8,128)(2,1)} %get-tuple-element.87), channel_id=1, source_target_pairs={{0,8},{4,12},{8,0},{12,4},{16,24},{20,28},{24,16},{28,20},{1,9},{5... | collective-permute-start | bytes 983048 | tf_op jit(solution)/shard_map/ppermute | solution.py:21
  289.5 1.2 collective-permute-start.41
  290.7 4.5 %collective-permute-start.44 = (f32[8,128]{1,0:T(8,128)S(1)}, f32[8,128]{1,0:T(8,128)S(1)}, u32[]{:S(2)}, u32[]{:S(2)}) collective-permute-start(f32[8,128]{1,0:T(8,128)S(1)} %broadcast_add_fusion), channel_id=1, source_target_pairs={{0,24},{4,28},{8,16},{12,20},{16,8},{20,12},{24,0},{28,4},{1,25},{... | collective-permute-start | bytes 12296 | tf_op jit(solution)/shard_map/ppermute | solution.py:21
  291.8 3.6 %collective-permute-start.42 = (f32[8,128]{1,0:T(8,128)S(1)}, f32[8,128]{1,0:T(8,128)S(1)}, u32[]{:S(2)}, u32[]{:S(2)}) collective-permute-start(f32[8,128]{1,0:T(8,128)S(1)} %broadcast_add_fusion), channel_id=1, source_target_pairs={{0,8},{4,12},{8,0},{12,4},{16,24},{20,28},{24,16},{28,20},{1,9},{5... | collective-permute-start | bytes 12296 | tf_op jit(solution)/shard_map/ppermute | solution.py:21
  292.7 3.6 %collective-permute-start.43 = (f32[8,128]{1,0:T(8,128)S(1)}, f32[8,128]{1,0:T(8,128)S(1)}, u32[]{:S(2)}, u32[]{:S(2)}) collective-permute-start(f32[8,128]{1,0:T(8,128)S(1)} %broadcast_add_fusion), channel_id=1, source_target_pairs={{0,16},{4,20},{8,24},{12,28},{16,0},{20,4},{24,8},{28,12},{1,17},{... | collective-permute-start | bytes 12296 | tf_op jit(solution)/shard_map/ppermute | solution.py:21
  296.3 3.8 %collective-permute-start.47 = (f32[8,128]{1,0:T(8,128)S(1)}, f32[8,128]{1,0:T(8,128)S(1)}, u32[]{:S(2)}, u32[]{:S(2)}) collective-permute-start(f32[8,128]{1,0:T(8,128)S(1)} %add_add_fusion.1), channel_id=1, source_target_pairs={{0,3},{1,0},{2,1},{3,2},{4,7},{5,4},{6,5},{7,6},{8,11},{9,8},{10,9... | collective-permute-start | bytes 12296 | tf_op jit(solution)/shard_map/ppermute | solution.py:245
  298.8 5.4 %collective-permute-start.45 = (f32[8,128]{1,0:T(8,128)S(1)}, f32[8,128]{1,0:T(8,128)S(1)}, u32[]{:S(2)}, u32[]{:S(2)}) collective-permute-start(f32[8,128]{1,0:T(8,128)S(1)} %add_add_fusion.1), channel_id=1, source_target_pairs={{0,1},{1,2},{2,3},{3,0},{4,5},{5,6},{6,7},{7,4},{8,9},{9,10},{10,1... | collective-permute-start | bytes 12296 | tf_op jit(solution)/shard_map/ppermute | solution.py:245
  298.8 5.4 %collective-permute-start.46 = (f32[8,128]{1,0:T(8,128)S(1)}, f32[8,128]{1,0:T(8,128)S(1)}, u32[]{:S(2)}, u32[]{:S(2)}) collective-permute-start(f32[8,128]{1,0:T(8,128)S(1)} %add_add_fusion.1), channel_id=1, source_target_pairs={{0,2},{1,3},{2,0},{3,1},{4,6},{5,7},{6,4},{7,5},{8,10},{9,11},{10,... | collective-permute-start | bytes 12296 | tf_op jit(solution)/shard_map/ppermute | solution.py:245
  (10 other events, 32.7 us)

commit v5 on v4

--- a/solution.py
+++ b/solution.py
@@ -106,6 +106,15 @@
     )(total, *pieces)
 
 
+def unset(rows, cols):
+    return pl.pallas_call(
+        lambda out_ref: None,
+        out_shape=jax.ShapeDtypeStruct((rows, cols), BF),
+        out_specs=pl.BlockSpec(memory_space=pl.ANY),
+        name="unset",
+    )()
+
+
 def per_device(n_fsdp, n_tp, activations, cotangent, lengths, grow_operator, proxy_weight):
     me = lax.axis_index("fsdp")
     at = lax.axis_index("tp")
@@ -137,14 +146,13 @@
 
     assert chunks == 2
     odd = me % 2
-    r_all = jnp.zeros((total_p, width), BF)
-    for m in range(close):
-        r_all = lax.dynamic_update_slice_in_dim(r_all, r[m], (m ^ odd) * depth, axis=0)
-    product_near = dot(forward, r_all[: close * depth], (1, 1)).astype(BF)
-    for m in range(close, n_fsdp):
-        block = after(r[m], product_near)
+    r_near = jnp.concatenate([r[m] for m in range(close)], axis=0)
+    product_near = dot(forward, r_near, (1, 1)).astype(BF)
+    product_far = [dot(forward, r[close + i], (1, 1)).astype(BF) for i in range(2)]
+    r_all = unset(total_p, width)
+    for m in range(n_fsdp):
+        block = after(r[m], product_far[0])
         r_all = lax.dynamic_update_slice_in_dim(r_all, block, (m ^ odd) * depth, axis=0)
-    product_far = [dot(forward, r[close + i], (1, 1)).astype(BF) for i in range(2)]
 
     def place(c, owner):
         return me ^ (jnp.clip(owner, 0, last) * chunks + c)
@@ -180,7 +188,7 @@
 
     def partial(products, c, owner):
         block = place(c, owner)
-        start = (jnp.minimum(block, close - 1) ^ odd) * depth
+        start = jnp.minimum(block, close - 1) * depth
         near = lax.dynamic_slice_in_dim(products[0], start, depth, axis=1)
         far = jnp.where(block == close, *products[1:])
         return jnp.where(block < close, near, far).astype(F32)
@@ -241,9 +249,7 @@
     total = jnp.broadcast_to(squares, (8, 128))
     total = total + flip(total, "fsdp", n_fsdp, 1)
     total = total + sum(flip(total, "fsdp", n_fsdp, m) for m in keeps[1:])
-    total = total + sum(
-        lax.ppermute(total, "tp", [(i, (i + k) % n_tp) for i in range(n_tp)]) for k in range(1, n_tp)
-    )
+    total = total + sum(flip(total, "tp", n_tp, k) for k in range(1, n_tp))
     return scaled(total, pieces, total_d * total_p)
 
 

time: 306 us -> 301 us (0.984)
  starting transfers between devices: 87.1 us -> 64.5 us
  waiting for transfers between devices: 122 us -> 140 us
  local copies, waits for them, and re-layouts: 22.8 us -> 32.3 us
  other arithmetic: 20.4 us -> 12.6 us
    ppermute x15, starting transfers between devices: 59.2 us -> 36.7 us  [trade(): return lax.ppermute(value, 'tp', pairs) if pairs else None]
    ppermute x15, waiting for transfers between devices: 31 us -> 48.1 us  [trade(): return lax.ppermute(value, 'tp', pairs) if pairs else None]
    unnamed x61 -> x70, local copies, waits for them, and re-layouts: 8.26 us -> 18.7 us
    dynamic_update_slice x6 -> x0, local copies, waits for them, and re-layouts: 5.7 us -> none  [per_device(): lax.dynamic_update_slice_in_dim(r_all, r[m], (m ^ odd) * depth, axis=0)]
    convert_element_type x4, other arithmetic: 7.17 us -> 1.73 us  [per_device(): add(partial(products, c, jnp.where(up_even, *ends[::-1])), even).astype(BF)]
    ppermute x30 -> x33, waiting for transfers between devices: 86.7 us -> 91.7 us  [flip(): return lax.ppermute(value, axis, [(i, i ^ bit) for i in range(size)])]
    ppermute x3 -> x0, waiting for transfers between devices: 4.79 us -> none  [per_device(): lax.ppermute(total, 'tp', [(i, (i + k) % n_tp) for i in range(n_tp)])]
    ppermute x3 -> x0, starting transfers between devices: 3.1 us -> none  [per_device(): lax.ppermute(total, 'tp', [(i, (i + k) % n_tp) for i in range(n_tp)])]
where the time goes in v5:
time: 301 us; the launch traced here: 300 us
  waiting for transfers between devices  140 us (47%)
  starting transfers between devices  64.5 us (21%)
  matrix products  42.4 us (14%)
  local copies, waits for them, and re-layouts  32.3 us (11%)
  other arithmetic  12.6 us (4%)
  Pallas kernels  5.27 us (2%)
  between operations  3.35 us (1%)
    ppermute x33, waiting for transfers between devices, flip(): return lax.ppermute(value, axis, [(i, i ^ bit) for i in range(size)])  91.7 us
    ppermute x15, waiting for transfers between devices, trade(): return lax.ppermute(value, 'tp', pairs) if pairs else None  48.1 us
    dot_general x12, matrix products, dot(): lax.dot_general(left, right, ((dims[:1], dims[1:]), ((), ())), preferred_...  42.4 us
    ppermute x15, starting transfers between devices, trade(): return lax.ppermute(value, 'tp', pairs) if pairs else None  36.7 us
    ppermute x33, starting transfers between devices, flip(): return lax.ppermute(value, axis, [(i, i ^ bit) for i in range(size)])  27.8 us
    unnamed x70, local copies, waits for them, and re-layouts  18.7 us
  transfers between devices with their start and end apart: 48, of which 24 were waited for; matrix products, arithmetic and copies ran while one was open for 26% of the time, Pallas kernels for 1%

profile of v5, /device:TPU:0, one launch (start us, length us, event | category | flops | bytes accessed | tf_op | source)
XLA Modules:
  0.0 300.3 jit_solution(3588276062291202780)
XLA Ops:
  0.0 3.0 collective-permute-start
  3.0 1.5 collective-permute-start.1
  4.6 2.5 copy-done.1
  7.1 2.5 copy-done.2
  10.2 4.0 %shard_map.55 = bf16[1024,5120]{1,0:T(8,128)(2,1)S(1)} custom-call(s32[8]{0:T(128)S(1)} %stack.83.places, s32[2]{0:T(128)S(1)} %copy-done.3, bf16[512,5120]{1,0:T(8,128)(2,1)S(1)} %copy-done.1, bf16[512,5120]{1,0:T(8,128)(2,1)S(1)} %copy-done.2), custom_call_target="tpu_custom_call" | custom-call | bytes 20971520 | tf_op jit(solution)/shard_map/pallas_call | solution.py:74
  14.2 17.8 %collective-permute-done = bf16[640,1024]{1,0:T(8,128)(2,1)} collective-permute-done((bf16[640,1024]{1,0:T(8,128)(2,1)}, bf16[640,1024]{1,0:T(8,128)(2,1)}, u32[]{:S(2)}, u32[]{:S(2)}) %collective-permute-start) | collective-permute-done | bytes 1310752 | tf_op jit(solution)/shard_map/ppermute | solution.py:21
  33.2 1.8 collective-permute-start.2
  36.2 1.6 collective-permute-start.3
  38.3 10.9 %collective-permute-done.2 = bf16[320,1024]{1,0:T(8,128)(2,1)S(1)} collective-permute-done((bf16[320,1024]{1,0:T(8,128)(2,1)S(1)}, bf16[320,1024]{1,0:T(8,128)(2,1)S(1)}, u32[]{:S(2)}, u32[]{:S(2)}) %collective-permute-start.2) | collective-permute-done | bytes 655392 | tf_op jit(solution)/shard_map/ppermute | solution.py:21
  49.2 2.4 collective-permute-done.3
  51.9 1.4 constant_dynamic-update-slice_fusion.7
  53.3 1.4 constant_dynamic-update-slice_fusion.6
  54.7 1.6 collective-permute-start.8
  57.4 11.2 %convolution_convert_fusion.1 = bf16[1024,1024]{1,0:T(8,128)(2,1)S(1)} fusion(bf16[1024,5120]{1,0:T(8,128)(2,1)S(1)} %shard_map.55, bf16[5120,1024]{1,0:T(8,128)(2,1)S(1)} %constant_dynamic-update-slice_fusion), kind=kOutput, calls=%fused_computation.24 | convolution fusion | flops 10738466816 | bytes 23068672 | tf_op jit(solution)/shard_map/dot_general | solution.py:17
  68.6 1.1 fusion.53
  69.7 1.6 collective-permute-start.18
  71.3 9.0 %collective-permute-done.8 = bf16[512,1024]{1,0:T(8,128)(2,1)S(1)} collective-permute-done((bf16[512,1024]{1,0:T(8,128)(2,1)S(1)}, bf16[512,1024]{1,0:T(8,128)(2,1)S(1)}, u32[]{:S(2)}, u32[]{:S(2)}) %collective-permute-start.8) | collective-permute-done | bytes 1048608 | tf_op jit(solution)/shard_map/ppermute | solution.py:21
  83.3 10.7 %collective-permute-done.9 = bf16[256,1024]{1,0:T(8,128)(2,1)S(1)} collective-permute-done((bf16[256,1024]{1,0:T(8,128)(2,1)S(1)}, bf16[256,1024]{1,0:T(8,128)(2,1)S(1)}, u32[]{:S(2)}, u32[]{:S(2)}) %collective-permute-start.9) | collective-permute-done | bytes 524320 | tf_op jit(solution)/shard_map/ppermute | solution.py:21
  100.2 2.3 constant_dynamic-update-slice_fusion.15
  103.5 2.3 constant_dynamic-update-slice_fusion.13
  106.9 2.5 constant_dynamic-update-slice_fusion.11
  109.4 6.6 %convolution_convert_fusion = bf16[512,3072]{1,0:T(8,128)(2,1)S(1)} fusion(bf16[3072,1024]{1,0:T(8,128)(2,1)} %constant_dynamic-update-slice_fusion.11, bf16[1024,1024]{1,0:T(8,128)(2,1)S(1)} %copy-done.13), kind=kOutput, calls=%fused_computation.14 | convolution fusion | flops 3222798336 | bytes 10485760 | tf_op jit(solution)/shard_map/dot_general | solution.py:17
  117.8 7.8 %collective-permute-start.21 = (bf16[512,512]{1,0:T(8,128)(2,1)S(1)}, bf16[512,512]{1,0:T(8,128)(2,1)S(1)}, u32[]{:S(2)}, u32[]{:S(2)}) collective-permute-start(bf16[512,512]{1,0:T(8,128)(2,1)S(1)} %get-tuple-element.95), channel_id=1, source_target_pairs={{0,1},{3,2},{4,5},{7,6},{8,9},{11,10},{12,13},{15,14},{16,17},{19,... | collective-permute-start | bytes 1572872 | tf_op jit(solution)/shard_map/ppermute | solution.py:162
  125.7 1.3 constant_dynamic-update-slice_fusion.23
  127.2 1.3 constant_dynamic-update-slice_fusion.21
  128.5 8.2 %collective-permute-done.21 = bf16[512,512]{1,0:T(8,128)(2,1)S(1)} collective-permute-done((bf16[512,512]{1,0:T(8,128)(2,1)S(1)}, bf16[512,512]{1,0:T(8,128)(2,1)S(1)}, u32[]{:S(2)}, u32[]{:S(2)}) %collective-permute-start.21) | collective-permute-done | bytes 524320 | tf_op jit(solution)/shard_map/ppermute | solution.py:162
  137.0 4.4 %collective-permute-start.23 = (bf16[512,512]{1,0:T(8,128)(2,1)S(1)}, bf16[512,512]{1,0:T(8,128)(2,1)S(1)}, u32[]{:S(2)}, u32[]{:S(2)}) collective-permute-start(bf16[512,512]{1,0:T(8,128)(2,1)S(1)} %get-tuple-element.59), channel_id=1, source_target_pairs={{0,1},{3,2},{4,5},{7,6},{8,9},{11,10},{12,13},{15,14},{16,17},{19,... | collective-permute-start | bytes 1572872 | tf_op jit(solution)/shard_map/ppermute | solution.py:162
  142.6 4.1 %collective-permute-start.25 = (bf16[512,512]{1,0:T(8,128)(2,1)S(1)}, bf16[512,512]{1,0:T(8,128)(2,1)S(1)}, u32[]{:S(2)}, u32[]{:S(2)}) collective-permute-start(bf16[512,512]{1,0:T(8,128)(2,1)S(1)} %get-tuple-element.91), channel_id=1, source_target_pairs={{0,1},{3,2},{4,5},{7,6},{8,9},{11,10},{12,13},{15,14},{16,17},{19,... | collective-permute-start | bytes 1572872 | tf_op jit(solution)/shard_map/ppermute | solution.py:162
  146.8 1.3 constant_dynamic-update-slice_fusion.19
  148.1 1.3 collective-permute-start.20
  149.4 4.3 %collective-permute-done.23 = bf16[512,512]{1,0:T(8,128)(2,1)S(1)} collective-permute-done((bf16[512,512]{1,0:T(8,128)(2,1)S(1)}, bf16[512,512]{1,0:T(8,128)(2,1)S(1)}, u32[]{:S(2)}, u32[]{:S(2)}) %collective-permute-start.23) | collective-permute-done | bytes 524320 | tf_op jit(solution)/shard_map/ppermute | solution.py:162
  155.0 8.2 %collective-permute-done.25 = bf16[512,512]{1,0:T(8,128)(2,1)S(1)} collective-permute-done((bf16[512,512]{1,0:T(8,128)(2,1)S(1)}, bf16[512,512]{1,0:T(8,128)(2,1)S(1)}, u32[]{:S(2)}, u32[]{:S(2)}) %collective-permute-start.25) | collective-permute-done | bytes 524320 | tf_op jit(solution)/shard_map/ppermute | solution.py:162
  163.5 4.4 %collective-permute-start.26 = (bf16[512,512]{1,0:T(8,128)(2,1)S(1)}, bf16[512,512]{1,0:T(8,128)(2,1)S(1)}, u32[]{:S(2)}, u32[]{:S(2)}) collective-permute-start(bf16[512,512]{1,0:T(8,128)(2,1)S(1)} %get-tuple-element.64), channel_id=1, source_target_pairs={{0,1},{3,2},{4,5},{7,6},{8,9},{11,10},{12,13},{15,14},{16,17},{19,... | collective-permute-start | bytes 1572872 | tf_op jit(solution)/shard_map/ppermute | solution.py:162
  168.6 2.2 collective-permute-start.24
  171.1 1.3 fusion.26
  172.4 1.3 collective-permute-start.17
  173.7 6.5 %collective-permute-done.26 = bf16[512,512]{1,0:T(8,128)(2,1)S(1)} collective-permute-done((bf16[512,512]{1,0:T(8,128)(2,1)S(1)}, bf16[512,512]{1,0:T(8,128)(2,1)S(1)}, u32[]{:S(2)}, u32[]{:S(2)}) %collective-permute-start.26) | collective-permute-done | bytes 524320 | tf_op jit(solution)/shard_map/ppermute | solution.py:162
  180.2 8.6 %collective-permute-done.24 = bf16[512,512]{1,0:T(8,128)(2,1)S(1)} collective-permute-done((bf16[512,512]{1,0:T(8,128)(2,1)S(1)}, bf16[512,512]{1,0:T(8,128)(2,1)S(1)}, u32[]{:S(2)}, u32[]{:S(2)}) %collective-permute-start.24) | collective-permute-done | bytes 524320 | tf_op jit(solution)/shard_map/ppermute | solution.py:162
  190.0 5.3 %collective-permute-start.34 = (bf16[512,512]{1,0:T(8,128)(2,1)S(1)}, bf16[512,512]{1,0:T(8,128)(2,1)}, u32[]{:S(2)}, u32[]{:S(2)}) collective-permute-start(bf16[512,512]{1,0:T(8,128)(2,1)S(1)} %get-tuple-element.74), channel_id=1, source_target_pairs={{0,1},{2,3},{3,2},{1,0},{4,5},{6,7},{7,6},{5,4},{8,9},{10,11},{11,... | collective-permute-start | bytes 1572872 | tf_op jit(solution)/shard_map/ppermute | solution.py:162
  195.7 2.6 fusion.20
  198.3 1.3 fusion.22
  199.6 10.1 %collective-permute-done.17 = bf16[512,1024]{1,0:T(8,128)(2,1)S(1)} collective-permute-done((bf16[512,1024]{1,0:T(8,128)(2,1)S(1)}, bf16[512,1024]{1,0:T(8,128)(2,1)S(1)}, u32[]{:S(2)}, u32[]{:S(2)}) %collective-permute-start.17) | collective-permute-done | bytes 1048608 | tf_op jit(solution)/shard_map/ppermute | solution.py:162
  209.8 1.3 add_convert_fusion.2
  212.0 4.5 %fusion.14 = bf16[2560,512]{1,0:T(8,128)(2,1)} fusion(bf16[1024,5120]{1,0:T(8,128)(2,1)S(1)} %bitcast.82, bf16[512,512]{1,0:T(8,128)(2,1)S(1)} %add_convert_fusion.6, bf16[512,512]{1,0:T(8,128)(2,1)S(1)} %get-tuple-element.116), kind=kOutput, calls=%fused_computation.12 | convolution fusion | flops 2687762432 | bytes 8912896 | tf_op jit(solution)/shard_map/dot_general | solution.py:17
  216.5 2.3 collective-permute-done.34
  218.7 1.7 add_convert_fusion.3
  220.5 5.7 %fusion.17 = bf16[2560,512]{1,0:T(8,128)(2,1)S(1)} fusion(bf16[1024,5120]{1,0:T(8,128)(2,1)} %copy-done, bf16[512,512]{1,0:T(8,128)(2,1)S(1)} %add_convert_fusion.3, bf16[512,512]{1,0:T(8,128)(2,1)} %get-tuple-element.115), kind=kOutput, calls=%fused_computation.13 | convolution fusion | flops 2687762432 | bytes 8912896 | tf_op jit(solution)/shard_map/dot_general | solution.py:17
  226.3 3.2 %fusion.8 = bf16[2560,512]{1,0:T(8,128)(2,1)S(1)} fusion(bf16[1024,5120]{1,0:T(8,128)(2,1)S(1)} %bitcast.84, bf16[512,512]{1,0:T(8,128)(2,1)S(1)} %add_convert_fusion.6, bf16[512,512]{1,0:T(8,128)(2,1)S(1)} %copy-done.17), kind=kOutput, calls=%fused_computation.10 | convolution fusion | flops 2687762432 | bytes 8912896 | tf_op jit(solution)/shard_map/dot_general | solution.py:17
  229.5 3.2 %fusion.11 = bf16[2560,512]{1,0:T(8,128)(2,1)S(1)} fusion(bf16[1024,5120]{1,0:T(8,128)(2,1)S(1)} %bitcast.84, bf16[512,512]{1,0:T(8,128)(2,1)S(1)} %add_convert_fusion.3, bf16[512,512]{1,0:T(8,128)(2,1)S(1)} %copy-done.15), kind=kOutput, calls=%fused_computation.11 | convolution fusion | flops 2687762432 | bytes 8912896 | tf_op jit(solution)/shard_map/dot_general | solution.py:17
  232.7 2.5 add_convert_fusion.1
  235.4 1.6 collective-permute-start.30
  240.9 12.2 %collective-permute-done.30 = bf16[2,640,256]{2,1,0:T(8,128)(2,1)S(1)} collective-permute-done((bf16[2,640,256]{2,1,0:T(8,128)(2,1)S(1)}, bf16[2,640,256]{2,1,0:T(8,128)(2,1)S(1)}, u32[]{:S(2)}, u32[]{:S(2)}) %collective-permute-start.30) | collective-permute-done | bytes 655392 | tf_op jit(solution)/shard_map/ppermute | solution.py:21
  253.1 1.6 collective-permute-done.31
  256.4 10.7 %collective-permute-done.37 = bf16[2,640,256]{2,1,0:T(8,128)(2,1)S(1)} collective-permute-done((bf16[2,640,256]{2,1,0:T(8,128)(2,1)S(1)}, bf16[2,640,256]{2,1,0:T(8,128)(2,1)S(1)}, u32[]{:S(2)}, u32[]{:S(2)}) %collective-permute-start.37) | collective-permute-done | bytes 655392 | tf_op jit(solution)/shard_map/ppermute | solution.py:21
  267.1 1.6 collective-permute-done.38
  271.3 4.5 %collective-permute-done.32 = bf16[1,640,256]{2,1,0:T(8,128)(2,1)S(1)} collective-permute-done((bf16[1,640,256]{2,1,0:T(8,128)(2,1)S(1)}, bf16[1,640,256]{2,1,0:T(8,128)(2,1)S(1)}, u32[]{:S(2)}, u32[]{:S(2)}) %collective-permute-start.32) | collective-permute-done | bytes 327712 | tf_op jit(solution)/shard_map/ppermute | solution.py:21
  278.0 4.1 %collective-permute-done.39 = bf16[1,640,256]{2,1,0:T(8,128)(2,1)} collective-permute-done((bf16[1,640,256]{2,1,0:T(8,128)(2,1)}, bf16[1,640,256]{2,1,0:T(8,128)(2,1)}, u32[]{:S(2)}, u32[]{:S(2)}) %collective-permute-start.39) | collective-permute-done | bytes 327712 | tf_op jit(solution)/shard_map/ppermute | solution.py:21
  282.1 2.3 multiply_reduce_fusion
  285.8 1.2 collective-permute-done.41
  287.9 1.5 collective-permute-start.42
  291.5 1.5 collective-permute-done.43
  293.0 1.3 collective-permute-start.47
  294.3 3.1 %collective-permute-start.46 = (f32[8,128]{1,0:T(8,128)S(1)}, f32[8,128]{1,0:T(8,128)S(1)}, u32[]{:S(2)}, u32[]{:S(2)}) collective-permute-start(f32[8,128]{1,0:T(8,128)S(1)} %add_add_fusion.1), channel_id=1, source_target_pairs={{0,2},{1,3},{2,0},{3,1},{4,6},{5,7},{6,4},{7,5},{8,10},{9,11},{10,... | collective-permute-start | bytes 12296 | tf_op jit(solution)/shard_map/ppermute | solution.py:21
  299.0 1.3 shard_map.56
  (162 shorter events, 38.7 us)
Async XLA Ops:
  0.0 32.1 %collective-permute-start = (bf16[640,1024]{1,0:T(8,128)(2,1)}, bf16[640,1024]{1,0:T(8,128)(2,1)}, u32[]{:S(2)}, u32[]{:S(2)}) collective-permute-start(bf16[640,1024]{1,0:T(8,128)(2,1)} %param.8), channel_id=1, source_target_pairs={{0,8},{4,12},{8,0},{12,4},{16,24},{20,28},{24,16},{28,20},{1,9},{5... | collective-permute-start | bytes 3932168 | tf_op jit(solution)/shard_map/ppermute | solution.py:21
  3.0 32.1 %collective-permute-start.1 = (bf16[640,1024]{1,0:T(8,128)(2,1)}, bf16[640,1024]{1,0:T(8,128)(2,1)}, u32[]{:S(2)}, u32[]{:S(2)}) collective-permute-start(bf16[640,1024]{1,0:T(8,128)(2,1)} %param.8), channel_id=1, source_target_pairs={{0,16},{4,20},{8,24},{12,28},{16,0},{20,4},{24,8},{28,12},{1,17},{... | collective-permute-start | bytes 3932168 | tf_op jit(solution)/shard_map/ppermute | solution.py:21
  10.2 27.5 %copy-start.8 = (bf16[640,1024]{1,0:T(8,128)(2,1)S(1)}, bf16[640,1024]{1,0:T(8,128)(2,1)}, u32[]{:S(2)}) copy-start(bf16[640,1024]{1,0:T(8,128)(2,1)} %param.8) | copy-start | bytes 3932164
  14.2 43.2 %copy-start = (bf16[1024,5120]{1,0:T(8,128)(2,1)}, bf16[1024,5120]{1,0:T(8,128)(2,1)S(1)}, u32[]{:S(2)}) copy-start(bf16[1024,5120]{1,0:T(8,128)(2,1)S(1)} %shard_map.55) | copy-start | bytes 31457284
  33.2 16.0 %collective-permute-start.2 = (bf16[320,1024]{1,0:T(8,128)(2,1)S(1)}, bf16[320,1024]{1,0:T(8,128)(2,1)S(1)}, u32[]{:S(2)}, u32[]{:S(2)}) collective-permute-start(bf16[320,1024]{1,0:T(8,128)(2,1)S(1)} %slice.131), channel_id=1, source_target_pairs={{0,16},{4,20},{8,24},{12,28},{16,0},{20,4},{24,8},{28,12},{1,17},{... | collective-permute-start | bytes 1966088 | tf_op jit(solution)/shard_map/ppermute | solution.py:21
  36.2 18.5 %copy-start.6 = (bf16[512,1024]{1,0:T(8,128)(2,1)S(1)}, bf16[512,1024]{1,0:T(8,128)(2,1)}, u32[]{:S(2)}) copy-start(bf16[512,1024]{1,0:T(8,128)(2,1)} %param.9) | copy-start | bytes 3145732
  36.2 15.4 %collective-permute-start.3 = (bf16[320,1024]{1,0:T(8,128)(2,1)S(1)}, bf16[320,1024]{1,0:T(8,128)(2,1)S(1)}, u32[]{:S(2)}, u32[]{:S(2)}) collective-permute-start(bf16[320,1024]{1,0:T(8,128)(2,1)S(1)} %slice.132), channel_id=1, source_target_pairs={{0,8},{4,12},{8,0},{12,4},{16,24},{20,28},{24,16},{28,20},{1,9},{5... | collective-permute-start | bytes 1966088 | tf_op jit(solution)/shard_map/ppermute | solution.py:21
  37.7 18.6 %collective-permute-start.4 = (bf16[640,1024]{1,0:T(8,128)(2,1)S(1)}, bf16[640,1024]{1,0:T(8,128)(2,1)S(1)}, u32[]{:S(2)}, u32[]{:S(2)}) collective-permute-start(bf16[640,1024]{1,0:T(8,128)(2,1)S(1)} %copy-done.8), channel_id=1, source_target_pairs={{0,4},{4,0},{8,12},{12,8},{16,20},{20,16},{24,28},{28,24},{1,5},{5... | collective-permute-start | bytes 3932168 | tf_op jit(solution)/shard_map/ppermute | solution.py:21
  37.7 19.3 %collective-permute-start.5 = (bf16[640,1024]{1,0:T(8,128)(2,1)}, bf16[640,1024]{1,0:T(8,128)(2,1)S(1)}, u32[]{:S(2)}, u32[]{:S(2)}) collective-permute-start(bf16[640,1024]{1,0:T(8,128)(2,1)} %collective-permute-done), channel_id=1, source_target_pairs={{0,4},{4,0},{8,12},{12,8},{16,20},{20,16},{24,28},{28,24},{1,5},{5... | collective-permute-start | bytes 3932168 | tf_op jit(solution)/shard_map/ppermute | solution.py:21
  38.2 18.9 %collective-permute-start.6 = (bf16[640,1024]{1,0:T(8,128)(2,1)}, bf16[640,1024]{1,0:T(8,128)(2,1)S(1)}, u32[]{:S(2)}, u32[]{:S(2)}) collective-permute-start(bf16[640,1024]{1,0:T(8,128)(2,1)} %collective-permute-done.1), channel_id=1, source_target_pairs={{0,4},{4,0},{8,12},{12,8},{16,20},{20,16},{24,28},{28,24},{1,5},{5... | collective-permute-start | bytes 3932168 | tf_op jit(solution)/shard_map/ppermute | solution.py:21
  51.7 5.6 %collective-permute-start.7 = (bf16[640,1024]{1,0:T(8,128)(2,1)S(1)}, bf16[640,1024]{1,0:T(8,128)(2,1)S(1)}, u32[]{:S(2)}, u32[]{:S(2)}) collective-permute-start(bf16[640,1024]{1,0:T(8,128)(2,1)S(1)} %pad_maximum_fusion), channel_id=1, source_target_pairs={{0,4},{4,0},{8,12},{12,8},{16,20},{20,16},{24,28},{28,24},{1,5},{5... | collective-permute-start | bytes 3932168 | tf_op jit(solution)/shard_map/ppermute | solution.py:21
  54.7 25.6 %collective-permute-start.8 = (bf16[512,1024]{1,0:T(8,128)(2,1)S(1)}, bf16[512,1024]{1,0:T(8,128)(2,1)S(1)}, u32[]{:S(2)}, u32[]{:S(2)}) collective-permute-start(bf16[512,1024]{1,0:T(8,128)(2,1)S(1)} %copy-done.6), channel_id=1, source_target_pairs={{0,8},{4,12},{8,0},{12,4},{16,24},{20,28},{24,16},{28,20},{1,9},{5... | collective-permute-start | bytes 3145736 | tf_op jit(solution)/shard_map/ppermute | solution.py:21
  56.4 25.3 %collective-permute-start.10 = (bf16[512,1024]{1,0:T(8,128)(2,1)S(1)}, bf16[512,1024]{1,0:T(8,128)(2,1)S(1)}, u32[]{:S(2)}, u32[]{:S(2)}) collective-permute-start(bf16[512,1024]{1,0:T(8,128)(2,1)S(1)} %copy-done.6), channel_id=1, source_target_pairs={{0,16},{4,20},{8,24},{12,28},{16,0},{20,4},{24,8},{28,12},{1,17},{... | collective-permute-start | bytes 3145736 | tf_op jit(solution)/shard_map/ppermute | solution.py:21
  68.6 14.7 %copy-start.12 = (bf16[1024,1024]{1,0:T(8,128)(2,1)}, bf16[1024,1024]{1,0:T(8,128)(2,1)S(1)}, u32[]{:S(2)}) copy-start(bf16[1024,1024]{1,0:T(8,128)(2,1)S(1)} %convolution_convert_fusion.1) | copy-start | bytes 6291460
  69.7 29.0 %collective-permute-start.12 = (bf16[512,1024]{1,0:T(8,128)(2,1)S(1)}, bf16[512,1024]{1,0:T(8,128)(2,1)}, u32[]{:S(2)}, u32[]{:S(2)}) collective-permute-start(bf16[512,1024]{1,0:T(8,128)(2,1)S(1)} %copy-done.6), channel_id=1, source_target_pairs={{0,4},{4,0},{8,12},{12,8},{16,20},{20,16},{24,28},{28,24},{1,5},{5... | collective-permute-start | bytes 3145736 | tf_op jit(solution)/shard_map/ppermute | solution.py:21
  69.7 29.6 %collective-permute-start.18 = (bf16[512,1024]{1,0:T(8,128)(2,1)}, bf16[512,1024]{1,0:T(8,128)(2,1)}, u32[]{:S(2)}, u32[]{:S(2)}) collective-permute-start(bf16[512,1024]{1,0:T(8,128)(2,1)} %fusion.53), channel_id=1, source_target_pairs={{0,1},{2,3},{3,2},{1,0},{4,5},{6,7},{7,6},{5,4},{8,9},{10,11},{11,... | collective-permute-start | bytes 3145736 | tf_op jit(solution)/shard_map/ppermute | solution.py:162
  80.4 13.6 %collective-permute-start.9 = (bf16[256,1024]{1,0:T(8,128)(2,1)S(1)}, bf16[256,1024]{1,0:T(8,128)(2,1)S(1)}, u32[]{:S(2)}, u32[]{:S(2)}) collective-permute-start(bf16[256,1024]{1,0:T(8,128)(2,1)S(1)} %slice.135), channel_id=1, source_target_pairs={{0,16},{4,20},{8,24},{12,28},{16,0},{20,4},{24,8},{28,12},{1,17},{... | collective-permute-start | bytes 1572872 | tf_op jit(solution)/shard_map/ppermute | solution.py:21
  81.0 22.6 %collective-permute-start.13 = (bf16[512,1024]{1,0:T(8,128)(2,1)S(1)}, bf16[512,1024]{1,0:T(8,128)(2,1)}, u32[]{:S(2)}, u32[]{:S(2)}) collective-permute-start(bf16[512,1024]{1,0:T(8,128)(2,1)S(1)} %collective-permute-done.8), channel_id=1, source_target_pairs={{0,4},{4,0},{8,12},{12,8},{16,20},{20,16},{24,28},{28,24},{1,5},{5... | collective-permute-start | bytes 3145736 | tf_op jit(solution)/shard_map/ppermute | solution.py:21
  82.6 14.4 %collective-permute-start.11 = (bf16[256,1024]{1,0:T(8,128)(2,1)}, bf16[256,1024]{1,0:T(8,128)(2,1)}, u32[]{:S(2)}, u32[]{:S(2)}) collective-permute-start(bf16[256,1024]{1,0:T(8,128)(2,1)} %slice.136), channel_id=1, source_target_pairs={{0,8},{4,12},{8,0},{12,4},{16,24},{20,28},{24,16},{28,20},{1,9},{5... | collective-permute-start | bytes 1572872 | tf_op jit(solution)/shard_map/ppermute | solution.py:21
  94.8 12.2 %collective-permute-start.14 = (bf16[512,1024]{1,0:T(8,128)(2,1)S(1)}, bf16[512,1024]{1,0:T(8,128)(2,1)}, u32[]{:S(2)}, u32[]{:S(2)}) collective-permute-start(bf16[512,1024]{1,0:T(8,128)(2,1)S(1)} %collective-permute-done.10), channel_id=1, source_target_pairs={{0,4},{4,0},{8,12},{12,8},{16,20},{20,16},{24,28},{28,24},{1,5},{5... | collective-permute-start | bytes 3145736 | tf_op jit(solution)/shard_map/ppermute | solution.py:21
  96.9 71.7 %collective-permute-start.16 = (bf16[512,1024]{1,0:T(8,128)(2,1)}, bf16[512,1024]{1,0:T(8,128)(2,1)S(1)}, u32[]{:S(2)}, u32[]{:S(2)}) collective-permute-start(bf16[512,1024]{1,0:T(8,128)(2,1)} %fusion.53), channel_id=1, source_target_pairs={{1,2},{2,1},{5,6},{6,5},{9,10},{10,9},{13,14},{14,13},{17,18},{18,... | collective-permute-start | bytes 3145736 | tf_op jit(solution)/shard_map/ppermute | solution.py:162
  98.7 10.7 %copy-start.13 = (bf16[1024,1024]{1,0:T(8,128)(2,1)S(1)}, bf16[1024,1024]{1,0:T(8,128)(2,1)}, u32[]{:S(2)}) copy-start(bf16[1024,1024]{1,0:T(8,128)(2,1)} %copy-done.12) | copy-start | bytes 6291460
  98.8 17.3 %collective-permute-start.15 = (bf16[512,1024]{1,0:T(8,128)(2,1)S(1)}, bf16[512,1024]{1,0:T(8,128)(2,1)S(1)}, u32[]{:S(2)}, u32[]{:S(2)}) collective-permute-start(bf16[512,1024]{1,0:T(8,128)(2,1)S(1)} %constant_dynamic-update-slice_fusion.9), channel_id=1, source_target_pairs={{0,4},{4,0},{8,12},{12,8},{16,20},{20,16},{24,28},{28,24},{1,5},{5... | collective-permute-start | bytes 3145736 | tf_op jit(solution)/shard_map/ppermute | solution.py:21
  99.3 48.8 %collective-permute-start.19 = (bf16[512,1024]{1,0:T(8,128)(2,1)}, bf16[512,1024]{1,0:T(8,128)(2,1)S(1)}, u32[]{:S(2)}, u32[]{:S(2)}) collective-permute-start(bf16[512,1024]{1,0:T(8,128)(2,1)} %collective-permute-done.18), channel_id=1, source_target_pairs={{1,2},{2,1},{5,6},{6,5},{9,10},{10,9},{13,14},{14,13},{17,18},{18,... | collective-permute-start | bytes 3145736 | tf_op jit(solution)/shard_map/ppermute | solution.py:162
  106.9 18.6 %slice-start.6 = ((s8[8388608]{0:T(1024)(128)(4,1)}), s8[4194304]{0:T(1024)(128)(4,1)S(1)}, s32[]{:S(2)}) async-start(s8[8388608]{0:T(1024)(128)(4,1)} %bitcast.85), calls=%async_computation.6 | async-start | bytes 8388608
  109.4 16.1 %slice-start.7 = ((s8[8388608]{0:T(1024)(128)(4,1)}), s8[4194304]{0:T(1024)(128)(4,1)S(1)}, s32[]{:S(2)}) async-start(s8[8388608]{0:T(1024)(128)(4,1)} %bitcast.85), calls=%async_computation.7 | async-start | bytes 8388608
  116.1 79.3 %copy-start.5 = (bf16[512,3072]{1,0:T(8,128)(2,1)}, bf16[512,3072]{1,0:T(8,128)(2,1)S(1)}, u32[]{:S(2)}) copy-start(bf16[512,3072]{1,0:T(8,128)(2,1)S(1)} %convolution_convert_fusion) | copy-start | bytes 9437188
  116.1 9.5 %copy-start.7 = (bf16[512,1024]{1,0:T(8,128)(2,1)S(1)}, bf16[512,1024]{1,0:T(8,128)(2,1)}, u32[]{:S(2)}) copy-start(bf16[512,1024]{1,0:T(8,128)(2,1)} %param.9) | copy-start | bytes 3145732
  117.8 18.9 %collective-permute-start.21 = (bf16[512,512]{1,0:T(8,128)(2,1)S(1)}, bf16[512,512]{1,0:T(8,128)(2,1)S(1)}, u32[]{:S(2)}, u32[]{:S(2)}) collective-permute-start(bf16[512,512]{1,0:T(8,128)(2,1)S(1)} %get-tuple-element.95), channel_id=1, source_target_pairs={{0,1},{3,2},{4,5},{7,6},{8,9},{11,10},{12,13},{15,14},{16,17},{19,... | collective-permute-start | bytes 1572872 | tf_op jit(solution)/shard_map/ppermute | solution.py:162
  137.0 16.7 %collective-permute-start.23 = (bf16[512,512]{1,0:T(8,128)(2,1)S(1)}, bf16[512,512]{1,0:T(8,128)(2,1)S(1)}, u32[]{:S(2)}, u32[]{:S(2)}) collective-permute-start(bf16[512,512]{1,0:T(8,128)(2,1)S(1)} %get-tuple-element.59), channel_id=1, source_target_pairs={{0,1},{3,2},{4,5},{7,6},{8,9},{11,10},{12,13},{15,14},{16,17},{19,... | collective-permute-start | bytes 1572872 | tf_op jit(solution)/shard_map/ppermute | solution.py:162
  141.5 12.3 %collective-permute-start.22 = (bf16[512,512]{1,0:T(8,128)(2,1)S(1)}, bf16[512,512]{1,0:T(8,128)(2,1)S(1)}, u32[]{:S(2)}, u32[]{:S(2)}) collective-permute-start(bf16[512,512]{1,0:T(8,128)(2,1)S(1)} %add_convert_fusion.10), channel_id=1, source_target_pairs={{1,2},{2,1},{5,6},{6,5},{9,10},{10,9},{13,14},{14,13},{17,18},{18,... | collective-permute-start | bytes 1572872 | tf_op jit(solution)/shard_map/ppermute | solution.py:162
  142.6 20.6 %collective-permute-start.25 = (bf16[512,512]{1,0:T(8,128)(2,1)S(1)}, bf16[512,512]{1,0:T(8,128)(2,1)S(1)}, u32[]{:S(2)}, u32[]{:S(2)}) collective-permute-start(bf16[512,512]{1,0:T(8,128)(2,1)S(1)} %get-tuple-element.91), channel_id=1, source_target_pairs={{0,1},{3,2},{4,5},{7,6},{8,9},{11,10},{12,13},{15,14},{16,17},{19,... | collective-permute-start | bytes 1572872 | tf_op jit(solution)/shard_map/ppermute | solution.py:162
  148.1 22.9 %copy-start.9 = (bf16[512,1024]{1,0:T(8,128)(2,1)}, bf16[512,1024]{1,0:T(8,128)(2,1)S(1)}, u32[]{:S(2)}) copy-start(bf16[512,1024]{1,0:T(8,128)(2,1)S(1)} %collective-permute-done.19) | copy-start | bytes 3145732
  148.1 47.6 %collective-permute-start.20 = (bf16[512,1024]{1,0:T(8,128)(2,1)S(1)}, bf16[512,1024]{1,0:T(8,128)(2,1)S(1)}, u32[]{:S(2)}, u32[]{:S(2)}) collective-permute-start(bf16[512,1024]{1,0:T(8,128)(2,1)S(1)} %collective-permute-done.19), channel_id=1, source_target_pairs={{2,3},{1,0},{6,7},{5,4},{10,11},{9,8},{14,15},{13,12},{18,19},{17,... | collective-permute-start | bytes 3145736 | tf_op jit(solution)/shard_map/ppermute | solution.py:162
  154.3 18.1 %collective-permute-start.28 = (bf16[512,512]{1,0:T(8,128)(2,1)S(1)}, bf16[512,512]{1,0:T(8,128)(2,1)S(1)}, u32[]{:S(2)}, u32[]{:S(2)}) collective-permute-start(bf16[512,512]{1,0:T(8,128)(2,1)S(1)} %get-tuple-element.67), channel_id=1, source_target_pairs={{1,2},{2,1},{5,6},{6,5},{9,10},{10,9},{13,14},{14,13},{17,18},{18,... | collective-permute-start | bytes 1572872 | tf_op jit(solution)/shard_map/ppermute | solution.py:162
  163.5 16.7 %collective-permute-start.26 = (bf16[512,512]{1,0:T(8,128)(2,1)S(1)}, bf16[512,512]{1,0:T(8,128)(2,1)S(1)}, u32[]{:S(2)}, u32[]{:S(2)}) collective-permute-start(bf16[512,512]{1,0:T(8,128)(2,1)S(1)} %get-tuple-element.64), channel_id=1, source_target_pairs={{0,1},{3,2},{4,5},{7,6},{8,9},{11,10},{12,13},{15,14},{16,17},{19,... | collective-permute-start | bytes 1572872 | tf_op jit(solution)/shard_map/ppermute | solution.py:162
  167.9 12.3 %collective-permute-start.27 = (bf16[512,512]{1,0:T(8,128)(2,1)S(1)}, bf16[512,512]{1,0:T(8,128)(2,1)S(1)}, u32[]{:S(2)}, u32[]{:S(2)}) collective-permute-start(bf16[512,512]{1,0:T(8,128)(2,1)S(1)} %add_convert_fusion.7), channel_id=1, source_target_pairs={{1,2},{2,1},{5,6},{6,5},{9,10},{10,9},{13,14},{14,13},{17,18},{18,... | collective-permute-start | bytes 1572872 | tf_op jit(solution)/shard_map/ppermute | solution.py:162
  168.6 20.1 %collective-permute-start.24 = (bf16[512,512]{1,0:T(8,128)(2,1)S(1)}, bf16[512,512]{1,0:T(8,128)(2,1)S(1)}, u32[]{:S(2)}, u32[]{:S(2)}) collective-permute-start(bf16[512,512]{1,0:T(8,128)(2,1)S(1)} %get-tuple-element.60), channel_id=1, source_target_pairs={{0,1},{2,3},{3,2},{1,0},{4,5},{6,7},{7,6},{5,4},{8,9},{10,11},{11,... | collective-permute-start | bytes 1572872 | tf_op jit(solution)/shard_map/ppermute | solution.py:162
  172.4 37.4 %collective-permute-start.17 = (bf16[512,1024]{1,0:T(8,128)(2,1)S(1)}, bf16[512,1024]{1,0:T(8,128)(2,1)S(1)}, u32[]{:S(2)}, u32[]{:S(2)}) collective-permute-start(bf16[512,1024]{1,0:T(8,128)(2,1)S(1)} %copy-done.19), channel_id=1, source_target_pairs={{2,3},{1,0},{6,7},{5,4},{10,11},{9,8},{14,15},{13,12},{18,19},{17,... | collective-permute-start | bytes 3145736 | tf_op jit(solution)/shard_map/ppermute | solution.py:162
  189.3 27.2 %collective-permute-start.35 = (bf16[512,512]{1,0:T(8,128)(2,1)S(1)}, bf16[512,512]{1,0:T(8,128)(2,1)S(1)}, u32[]{:S(2)}, u32[]{:S(2)}) collective-permute-start(bf16[512,512]{1,0:T(8,128)(2,1)S(1)} %get-tuple-element.75), channel_id=1, source_target_pairs={{1,2},{2,1},{5,6},{6,5},{9,10},{10,9},{13,14},{14,13},{17,18},{18,... | collective-permute-start | bytes 1572872 | tf_op jit(solution)/shard_map/ppermute | solution.py:162
  190.0 28.7 %collective-permute-start.34 = (bf16[512,512]{1,0:T(8,128)(2,1)S(1)}, bf16[512,512]{1,0:T(8,128)(2,1)}, u32[]{:S(2)}, u32[]{:S(2)}) collective-permute-start(bf16[512,512]{1,0:T(8,128)(2,1)S(1)} %get-tuple-element.74), channel_id=1, source_target_pairs={{0,1},{2,3},{3,2},{1,0},{4,5},{6,7},{7,6},{5,4},{8,9},{10,11},{11,... | collective-permute-start | bytes 1572872 | tf_op jit(solution)/shard_map/ppermute | solution.py:162
  195.7 14.1 %copy-start.10 = (bf16[512,1024]{1,0:T(8,128)(2,1)S(1)}, bf16[512,1024]{1,0:T(8,128)(2,1)}, u32[]{:S(2)}) copy-start(bf16[512,1024]{1,0:T(8,128)(2,1)} %copy-done.9) | copy-start | bytes 3145732
  198.3 13.6 %slice-start = ((s8[10485760]{0:T(1024)(128)(4,1)}), s8[4194304]{0:T(1024)(128)(4,1)S(1)}, s32[]{:S(2)}) async-start(s8[10485760]{0:T(1024)(128)(4,1)} %bitcast.81), calls=%async_computation | async-start | bytes 8388608
  198.3 13.6 %slice-start.1 = ((s8[10485760]{0:T(1024)(128)(4,1)}), s8[4194304]{0:T(1024)(128)(4,1)S(1)}, s32[]{:S(2)}) async-start(s8[10485760]{0:T(1024)(128)(4,1)} %bitcast.81), calls=%async_computation.1 | async-start | bytes 8388608
  199.6 12.3 %slice-start.2 = ((s8[10485760]{0:T(1024)(128)(4,1)}), s8[2097152]{0:T(1024)(128)(4,1)S(1)}, s32[]{:S(2)}) async-start(s8[10485760]{0:T(1024)(128)(4,1)} %bitcast.81), calls=%async_computation.2 | async-start | bytes 4194304
  216.5 16.2 %collective-permute-start.29 = (bf16[2560,512]{1,0:T(8,128)(2,1)}, bf16[2560,512]{1,0:T(8,128)(2,1)}, u32[]{:S(2)}, u32[]{:S(2)}) collective-permute-start(bf16[2560,512]{1,0:T(8,128)(2,1)} %fusion.14), channel_id=1, source_target_pairs={{0,4},{4,0},{8,12},{12,8},{16,20},{20,16},{24,28},{28,24},{1,5},{5... | collective-permute-start | bytes 7864328 | tf_op jit(solution)/shard_map/ppermute | solution.py:21
  226.1 11.9 %collective-permute-start.36 = (bf16[2560,512]{1,0:T(8,128)(2,1)S(1)}, bf16[2560,512]{1,0:T(8,128)(2,1)S(1)}, u32[]{:S(2)}, u32[]{:S(2)}) collective-permute-start(bf16[2560,512]{1,0:T(8,128)(2,1)S(1)} %fusion.17), channel_id=1, source_target_pairs={{0,4},{4,0},{8,12},{12,8},{16,20},{20,16},{24,28},{28,24},{1,5},{5... | collective-permute-start | bytes 7864328 | tf_op jit(solution)/shard_map/ppermute | solution.py:21
  235.4 17.7 %collective-permute-start.30 = (bf16[2,640,256]{2,1,0:T(8,128)(2,1)S(1)}, bf16[2,640,256]{2,1,0:T(8,128)(2,1)S(1)}, u32[]{:S(2)}, u32[]{:S(2)}) collective-permute-start(bf16[2,640,256]{2,1,0:T(8,128)(2,1)S(1)} %pad_maximum_fusion.3), channel_id=1, source_target_pairs={{0,8},{4,12},{8,0},{12,4},{16,24},{20,28},{24,16},{28,20},{1,9},{5... | collective-permute-start | bytes 1966088 | tf_op jit(solution)/shard_map/ppermute | solution.py:21
  237.0 17.7 %collective-permute-start.31 = (bf16[2,640,256]{2,1,0:T(8,128)(2,1)S(1)}, bf16[2,640,256]{2,1,0:T(8,128)(2,1)S(1)}, u32[]{:S(2)}, u32[]{:S(2)}) collective-permute-start(bf16[2,640,256]{2,1,0:T(8,128)(2,1)S(1)} %pad_maximum_fusion.4), channel_id=1, source_target_pairs={{0,16},{4,20},{8,24},{12,28},{16,0},{20,4},{24,8},{28,12},{1,17},{... | collective-permute-start | bytes 1966088 | tf_op jit(solution)/shard_map/ppermute | solution.py:21
  238.9 37.8 %copy-start.4 = (bf16[2560,512]{1,0:T(8,128)(2,1)}, bf16[2560,512]{1,0:T(8,128)(2,1)S(1)}, u32[]{:S(2)}) copy-start(bf16[2560,512]{1,0:T(8,128)(2,1)S(1)} %add_convert_fusion) | copy-start | bytes 7864324
  239.1 28.0 %collective-permute-start.37 = (bf16[2,640,256]{2,1,0:T(8,128)(2,1)S(1)}, bf16[2,640,256]{2,1,0:T(8,128)(2,1)S(1)}, u32[]{:S(2)}, u32[]{:S(2)}) collective-permute-start(bf16[2,640,256]{2,1,0:T(8,128)(2,1)S(1)} %pad_maximum_fusion.5), channel_id=1, source_target_pairs={{0,8},{4,12},{8,0},{12,4},{16,24},{20,28},{24,16},{28,20},{1,9},{5... | collective-permute-start | bytes 1966088 | tf_op jit(solution)/shard_map/ppermute | solution.py:21
  239.7 29.0 %collective-permute-start.38 = (bf16[2,640,256]{2,1,0:T(8,128)(2,1)S(1)}, bf16[2,640,256]{2,1,0:T(8,128)(2,1)S(1)}, u32[]{:S(2)}, u32[]{:S(2)}) collective-permute-start(bf16[2,640,256]{2,1,0:T(8,128)(2,1)S(1)} %pad_maximum_fusion.6), channel_id=1, source_target_pairs={{0,16},{4,20},{8,24},{12,28},{16,0},{20,4},{24,8},{28,12},{1,17},{... | collective-permute-start | bytes 1966088 | tf_op jit(solution)/shard_map/ppermute | solution.py:21
  254.9 20.9 %collective-permute-start.32 = (bf16[1,640,256]{2,1,0:T(8,128)(2,1)S(1)}, bf16[1,640,256]{2,1,0:T(8,128)(2,1)S(1)}, u32[]{:S(2)}, u32[]{:S(2)}) collective-permute-start(bf16[1,640,256]{2,1,0:T(8,128)(2,1)S(1)} %get-tuple-element.108), channel_id=1, source_target_pairs={{0,16},{4,20},{8,24},{12,28},{16,0},{20,4},{24,8},{28,12},{1,17},{... | collective-permute-start | bytes 983048 | tf_op jit(solution)/shard_map/ppermute | solution.py:21
  255.9 19.9 %collective-permute-start.33 = (bf16[1,640,256]{2,1,0:T(8,128)(2,1)S(1)}, bf16[1,640,256]{2,1,0:T(8,128)(2,1)S(1)}, u32[]{:S(2)}, u32[]{:S(2)}) collective-permute-start(bf16[1,640,256]{2,1,0:T(8,128)(2,1)S(1)} %get-tuple-element.107), channel_id=1, source_target_pairs={{0,8},{4,12},{8,0},{12,4},{16,24},{20,28},{24,16},{28,20},{1,9},{5... | collective-permute-start | bytes 983048 | tf_op jit(solution)/shard_map/ppermute | solution.py:21
  268.7 13.4 %copy-start.11 = (bf16[2,640,256]{2,1,0:T(8,128)(2,1)}, bf16[2,640,256]{2,1,0:T(8,128)(2,1)S(1)}, u32[]{:S(2)}) copy-start(bf16[2,640,256]{2,1,0:T(8,128)(2,1)S(1)} %collective-permute-done.38) | copy-start | bytes 1966084
  269.8 12.3 %collective-permute-start.39 = (bf16[1,640,256]{2,1,0:T(8,128)(2,1)}, bf16[1,640,256]{2,1,0:T(8,128)(2,1)}, u32[]{:S(2)}, u32[]{:S(2)}) collective-permute-start(bf16[1,640,256]{2,1,0:T(8,128)(2,1)} %get-tuple-element.100), channel_id=1, source_target_pairs={{0,16},{4,20},{8,24},{12,28},{16,0},{20,4},{24,8},{28,12},{1,17},{... | collective-permute-start | bytes 983048 | tf_op jit(solution)/shard_map/ppermute | solution.py:21
  270.8 11.4 %collective-permute-start.40 = (bf16[1,640,256]{2,1,0:T(8,128)(2,1)}, bf16[1,640,256]{2,1,0:T(8,128)(2,1)}, u32[]{:S(2)}, u32[]{:S(2)}) collective-permute-start(bf16[1,640,256]{2,1,0:T(8,128)(2,1)} %get-tuple-element.99), channel_id=1, source_target_pairs={{0,8},{4,12},{8,0},{12,4},{16,24},{20,28},{24,16},{28,20},{1,9},{5... | collective-permute-start | bytes 983048 | tf_op jit(solution)/shard_map/ppermute | solution.py:21
  285.7 1.2 collective-permute-start.41
  287.0 4.5 %collective-permute-start.44 = (f32[8,128]{1,0:T(8,128)S(1)}, f32[8,128]{1,0:T(8,128)S(1)}, u32[]{:S(2)}, u32[]{:S(2)}) collective-permute-start(f32[8,128]{1,0:T(8,128)S(1)} %broadcast_add_fusion), channel_id=1, source_target_pairs={{0,24},{4,28},{8,16},{12,20},{16,8},{20,12},{24,0},{28,4},{1,25},{... | collective-permute-start | bytes 12296 | tf_op jit(solution)/shard_map/ppermute | solution.py:21
  287.9 3.6 %collective-permute-start.42 = (f32[8,128]{1,0:T(8,128)S(1)}, f32[8,128]{1,0:T(8,128)S(1)}, u32[]{:S(2)}, u32[]{:S(2)}) collective-permute-start(f32[8,128]{1,0:T(8,128)S(1)} %broadcast_add_fusion), channel_id=1, source_target_pairs={{0,8},{4,12},{8,0},{12,4},{16,24},{20,28},{24,16},{28,20},{1,9},{5... | collective-permute-start | bytes 12296 | tf_op jit(solution)/shard_map/ppermute | solution.py:21
  289.4 3.6 %collective-permute-start.43 = (f32[8,128]{1,0:T(8,128)S(1)}, f32[8,128]{1,0:T(8,128)S(1)}, u32[]{:S(2)}, u32[]{:S(2)}) collective-permute-start(f32[8,128]{1,0:T(8,128)S(1)} %broadcast_add_fusion), channel_id=1, source_target_pairs={{0,16},{4,20},{8,24},{12,28},{16,0},{20,4},{24,8},{28,12},{1,17},{... | collective-permute-start | bytes 12296 | tf_op jit(solution)/shard_map/ppermute | solution.py:21
  293.0 5.4 %collective-permute-start.47 = (f32[8,128]{1,0:T(8,128)S(1)}, f32[8,128]{1,0:T(8,128)S(1)}, u32[]{:S(2)}, u32[]{:S(2)}) collective-permute-start(f32[8,128]{1,0:T(8,128)S(1)} %add_add_fusion.1), channel_id=1, source_target_pairs={{0,3},{1,2},{2,1},{3,0},{4,7},{5,6},{6,5},{7,4},{8,11},{9,10},{10,... | collective-permute-start | bytes 12296 | tf_op jit(solution)/shard_map/ppermute | solution.py:21
  294.3 4.1 %collective-permute-start.45 = (f32[8,128]{1,0:T(8,128)S(1)}, f32[8,128]{1,0:T(8,128)S(1)}, u32[]{:S(2)}, u32[]{:S(2)}) collective-permute-start(f32[8,128]{1,0:T(8,128)S(1)} %add_add_fusion.1), channel_id=1, source_target_pairs={{0,1},{1,0},{2,3},{3,2},{4,5},{5,4},{6,7},{7,6},{8,9},{9,8},{10,11... | collective-permute-start | bytes 12296 | tf_op jit(solution)/shard_map/ppermute | solution.py:21
  294.3 4.6 %collective-permute-start.46 = (f32[8,128]{1,0:T(8,128)S(1)}, f32[8,128]{1,0:T(8,128)S(1)}, u32[]{:S(2)}, u32[]{:S(2)}) collective-permute-start(f32[8,128]{1,0:T(8,128)S(1)} %add_add_fusion.1), channel_id=1, source_target_pairs={{0,2},{1,3},{2,0},{3,1},{4,6},{5,7},{6,4},{7,5},{8,10},{9,11},{10,... | collective-permute-start | bytes 12296 | tf_op jit(solution)/shard_map/ppermute | solution.py:21
  (12 other events, 42.8 us)
